TPU v7x, 512 devices: a whole 4x8x8 slice. The times are simulated.
512 devices in a mesh: mem: 64 (over y, z_lo, core), band: 8 (over x, z_hi).
Axes of the slice: x: 4, y: 8, z: 8 (z_hi: 2, z_lo: 4; z = z_hi * 4 + z_lo), core: 2. Of those that a mesh axis runs over, the one named last changes fastest.
Arguments:
- ensemble: bfloat16 [64, 12, 128, 512], P('mem', None, 'band'), may hold values from -6 to 6
- alpha: float32 [64, 12, 128, 512], P('mem', None, 'band'), may hold values from -6 to 6
- lat_lower: int32 [384], P('band'), may hold values from -1 to 15, as said below
- lat_weight: float32 [384], P('band'), may hold values from 0 to 1
- background: float32 [12, 512, 1152], P(None, ('band', 'mem')), may hold values from -6 to 6
- obs_cell: int32 [512, 256], P(('band', 'mem')), may hold values from 0 to 1151
- obs_value: float32 [12, 512, 256], P(None, ('band', 'mem')), may hold values from -6 to 6
- obs_precision: float32 [512, 256], P(('band', 'mem')), may hold values from 1 to 10
Outputs:
- advected: float32 [12, 512, 1152], P(None, ('band', 'mem'))
- gradient: float32 [64, 12, 128, 512], P('mem', None, 'band')
Inputs may be any that keep to these rules, and one draw needn't show every extreme that they name: `lat_lower`: fine rows of the first band use lower rows from 0, those of the last band up to 14 of their band, so that their upper row reaches 15; other bands reach -1 and 15. `obs_cell`: the cell is r * 24 + c for fine row r and column c within the tile.
All inputs are finite; a program needn't handle non-finite values.
Results may differ from a plain program's by a relative error of at most 0.0004.
Values sent between devices are 32-bit elements; how exact they have to be, the bound alone decides.
No kernel may reach another device: no remote copies, remote signals or barrier semaphores. Data moves between devices by JAX's collectives and lax.ppermute only.
A program may use at most 64 MiB of HBM per device.

v0:
```python
import math

import jax
import jax.numpy as jnp
from jax import lax
from jax.sharding import PartitionSpec as P

advect_rate = 0.25
highest = lax.Precision.HIGHEST


def padded_2(array, sides, width, wrap):
    for axis, dim in sides:
        size, length = (lax.axis_size(axis), array.shape[dim])
        up = [(i, (i + 1) % size) for i in range(size if wrap else size - 1)]
        down = [(j, i) for i, j in up]
        last = lax.slice_in_dim(array, length - width, length, axis=dim)
        initial = lax.slice_in_dim(array, 0, width, axis=dim)
        before = lax.ppermute(last, axis, up)
        after = lax.ppermute(initial, axis, down)
        array = jnp.concatenate([before, array, after], axis=dim)
    return array


def cut_along(array, dim, size):
    lengths = array.shape
    parts = array.reshape(*lengths[:dim], size, lengths[dim] // size, *lengths[dim + 1 :])
    return jnp.moveaxis(parts, dim, 0)


def sum_at_owner(array, axis, dim):
    size = lax.axis_size(axis)
    parts = lax.all_to_all(cut_along(array, dim, size), axis, 0, 0, tiled=True)
    return jnp.sum(parts, axis=0)


def from_everyone(array, axis):
    copies = jnp.broadcast_to(array, (lax.axis_size(axis), *array.shape))
    return lax.all_to_all(copies, axis, split_axis=0, concat_axis=0, tiled=True)


def in_order(parts, dim):
    lengths = list(parts.shape[1:])
    lengths[dim] *= parts.shape[0]
    return jnp.moveaxis(parts, 0, dim).reshape(lengths)


def gather_directly(array, axis, dim):
    parts = from_everyone(array, axis)
    return in_order(parts, dim)


def band_rows(grid_field):
    return padded_2(grid_field, (("band", 2),), 1, False)


def smooth_local(grid_field):
    padded = band_rows(grid_field)
    grid_field = 0.25 * padded[:, :, :-2] + 0.5 * padded[:, :, 1:-1] + 0.25 * padded[:, :, 2:]
    return 0.25 * jnp.roll(grid_field, 1, 3) + 0.5 * grid_field + 0.25 * jnp.roll(grid_field, -1, 3)


def coarse_frame(grid_field):
    return padded_2(grid_field, (("band", 1), ("mem", 2)), 1, True)


def flux_slope(grid_field):
    padded = padded_2(grid_field, (("mem", 2),), 1, True)
    return 0.5 * (padded[:, :, 2:] - padded[:, :, :-2])


def latitude_local(lat_lower, lat_weight, coarse_rows):
    padded = jnp.arange(coarse_rows + 2, dtype=jnp.int32)[None, :]
    lower_row = lat_lower[:, None] + 1
    weight = lat_weight[:, None]
    return (1.0 - weight) * (padded == lower_row) + weight * (padded == lower_row + 1)


def longitude_local(coarse_cols, fine_cols, first, count):
    fine_ratio = fine_cols // coarse_cols
    fine_index = jnp.arange(count, dtype=jnp.int32) + first
    numerator = 2 * fine_index + 1 + fine_ratio
    upper_col = numerator // (2 * fine_ratio)
    fraction = (numerator % (2 * fine_ratio)).astype(jnp.float32) / (2 * fine_ratio)
    padded = jnp.arange(coarse_cols + 2, dtype=jnp.int32)[:, None]
    return (1.0 - fraction)[None, :] * (padded == upper_col[None, :]) + fraction[None, :] * (
        padded == upper_col[None, :] + 1
    )


def shards(ensemble, alpha, lat_lower, lat_weight, background, obs_cell, obs_value, obs_precision):
    groups = lax.axis_size("mem")
    member_scale = 1.0 / math.sqrt(ensemble.shape[0] * groups - 1)
    levels = ensemble.shape[1]
    coarse_rows = ensemble.shape[2]
    coarse_lon = ensemble.shape[3]
    block_cols = coarse_lon // groups
    fine_rows = lat_lower.shape[0]
    cell_count = background.shape[2]
    fine_cols = cell_count // fine_rows
    back_grid = background.reshape(levels, fine_rows, fine_cols)
    back_wide = padded_2(back_grid, (("mem", 2),), 1, True)
    members_f = ensemble.astype(jnp.float32)
    partial_value = jnp.sum(smooth_local(alpha) * members_f, axis=0) * member_scale
    increment = sum_at_owner(partial_value, "mem", 2)
    lat_table = latitude_local(lat_lower, lat_weight, coarse_rows)
    lon_table = longitude_local(block_cols, fine_cols, 0, fine_cols)
    bordered = coarse_frame(increment)
    lat_rows = jnp.einsum("ik,lkc->lic", lat_table, bordered, precision=highest)
    wide_table = longitude_local(block_cols, fine_cols, -1, fine_cols + 2)
    wide_state = back_wide + jnp.einsum("lic,cj->lij", lat_rows, wide_table, precision=highest)
    fine_state = wide_state[:, :, 1:-1]
    lon_slope = 0.5 * (wide_state[:, :, 2:] - wide_state[:, :, :-2])
    advected = fine_state - advect_rate * fine_state * lon_slope
    flat_model = advected.reshape(levels, cell_count)
    obs_onehot = (obs_cell[0][:, None] == jnp.arange(cell_count, dtype=jnp.int32)[None, :]).astype(
        jnp.float32
    )
    observed = jnp.einsum("lc,nc->ln", flat_model, obs_onehot, precision=highest)
    weighted = obs_precision[0][None, :] * (observed - obs_value[:, 0, :])
    cotangent = jnp.dot(weighted, obs_onehot, precision=highest).reshape(
        levels, fine_rows, fine_cols
    )
    adj_flux = flux_slope(fine_state * cotangent)
    adjoint = cotangent - advect_rate * (cotangent * lon_slope - adj_flux)
    back_rows = jnp.einsum("lij,cj->lic", adjoint, lon_table, precision=highest)
    spread_back = jnp.einsum("ik,lic->lkc", lat_table, back_rows, precision=highest)
    last_row = coarse_rows - 1
    last_col = block_cols - 1
    framed = coarse_frame(spread_back)
    inner_rows = slice(2, coarse_rows + 2)
    inner_cols = slice(2, block_cols + 2)
    far_row = coarse_rows + 3
    far_col = block_cols + 3
    own_block = framed[:, inner_rows, inner_cols]
    own_block = (
        own_block.at[:, 0, :]
        .add(framed[:, 0, inner_cols])
        .at[:, last_row, :]
        .add(framed[:, far_row, inner_cols])
    )
    own_block = (
        own_block.at[:, :, 0]
        .add(framed[:, inner_rows, 0])
        .at[:, :, last_col]
        .add(framed[:, inner_rows, far_col])
    )
    own_block = (
        own_block.at[:, 0, 0].add(framed[:, 0, 0]).at[:, 0, last_col].add(framed[:, 0, far_col])
    )
    own_block = (
        own_block.at[:, last_row, 0]
        .add(framed[:, far_row, 0])
        .at[:, last_row, last_col]
        .add(framed[:, far_row, far_col])
    )
    coarse_gradient = gather_directly(own_block, "mem", 2)
    gradient = smooth_local(members_f * coarse_gradient[None] * member_scale)
    return (advected.reshape(levels, 1, cell_count), gradient)


def solution(mesh):
    return jax.shard_map(
        shards,
        mesh=mesh,
        in_specs=(
            P("mem", None, "band", None),
            P("mem", None, "band", None),
            P("band"),
            P("band"),
            P(None, ("band", "mem"), None),
            P(("band", "mem"), None),
            P(None, ("band", "mem"), None),
            P(("band", "mem"), None),
        ),
        out_specs=(P(None, ("band", "mem"), None), P("mem", None, "band", None)),
        check_vma=False,
    )
```

profile of v0, /device:TPU:6, one launch (start us, length us, event | category | flops | bytes accessed | tf_op | source)
XLA Modules:
  0.0 191.6 jit_solution(12472340646126494486)
XLA Ops:
  1.8 11.2 %collective-permute-start.3 = (f32[1,12,1,512]{3,2,1,0:T(1,128)S(1)}, f32[1,12,1,512]{3,2,1,0:T(1,128)S(1)}, u32[]{:S(2)}, u32[]{:S(2)}) collective-permute-start(f32[1,12,1,512]{3,2,1,0:T(1,128)S(1)} %get-tuple-element.117), channel_id=1, source_target_pairs={{1,0},{2,1},{3,2},{4,3},{5,4},{6,5},{7,6},{9,8},{10,9},{11,10},{12... | collective-permute-start | bytes 73736 | tf_op jit(solution)/shard_map/ppermute | solution.py:20
  13.0 1.9 %collective-permute-start.2 = (f32[1,12,1,512]{3,2,1,0:T(1,128)S(1)}, f32[1,12,1,512]{3,2,1,0:T(1,128)S(1)}, u32[]{:S(2)}, u32[]{:S(2)}) collective-permute-start(f32[1,12,1,512]{3,2,1,0:T(1,128)S(1)} %get-tuple-element.116), channel_id=1, source_target_pairs={{0,1},{1,2},{2,3},{3,4},{4,5},{5,6},{6,7},{8,9},{9,10},{10,11},{11... | collective-permute-start | bytes 73736 | tf_op jit(solution)/shard_map/ppermute | solution.py:19
  16.8 7.3 %collective-permute-start.1 = (f32[12,48,1]{1,2,0:T(1,128)}, f32[12,48,1]{1,2,0:T(1,128)S(1)}, u32[]{:S(2)}, u32[]{:S(2)}) collective-permute-start(f32[12,48,1]{1,2,0:T(1,128)} %get-tuple-element.125), channel_id=1, source_target_pairs={{8,0},{16,8},{24,16},{32,24},{40,32},{48,40},{56,48},{64,56},{72,6... | collective-permute-start | bytes 6920 | tf_op jit(solution)/shard_map/ppermute | solution.py:20
  29.2 2.1 %copy_bitcast_fusion.1 = f32[64,12,8,16]{3,2,1,0:T(8,128)} fusion(f32[1,12,16,512]{2,3,1,0:T(8,128)S(1)} %copy.122), kind=kLoop, calls=%fused_computation.157 | loop fusion | bytes 786432
  31.3 3.4 %reshape.445 = f32[64,1,1536]{2,1,0:T(1,128)} reshape(f32[64,12,8,16]{3,2,1,0:T(8,128)} %copy_bitcast_fusion.1) | data formatting | bytes 786432
  34.8 9.1 %all-to-all-start = ((f32[64,1,1536]{2,1,0:T(1,128)}), f32[64,1,1536]{2,1,0:T(1,128)S(1)}, u32[]{:S(2)}, u32[]{:S(2)}) async-start(f32[64,1,1536]{2,1,0:T(1,128)} %reshape.445), calls=%async_computation | async-start | bytes 786432 | tf_op jit(solution)/shard_map/all_to_all | solution.py:33
  46.3 12.4 %all-to-all-done = f32[64,1,1536]{2,1,0:T(1,128)S(1)} async-done(((f32[64,1,1536]{2,1,0:T(1,128)}), f32[64,1,1536]{2,1,0:T(1,128)S(1)}, u32[]{:S(2)}, u32[]{:S(2)}) %all-to-all-start) | async-done | bytes 393248 | tf_op jit(solution)/shard_map/all_to_all | solution.py:33
  62.3 8.4 %collective-permute-start.5 = (f32[12,1,8]{1,2,0:T(8,128)S(1)}, f32[12,1,8]{1,2,0:T(8,128)S(1)}, u32[]{:S(2)}, u32[]{:S(2)}) collective-permute-start(f32[12,1,8]{1,2,0:T(8,128)S(1)} %get-tuple-element.129), channel_id=1, source_target_pairs={{1,0},{2,1},{3,2},{4,3},{5,4},{6,5},{7,6},{0,7},{9,8},{10,9},{11,1... | collective-permute-start | bytes 1160 | tf_op jit(solution)/shard_map/ppermute | solution.py:20
  70.7 1.9 %collective-permute-start.4 = (f32[12,1,8]{1,2,0:T(8,128)S(1)}, f32[12,1,8]{1,2,0:T(8,128)S(1)}, u32[]{:S(2)}, u32[]{:S(2)}) collective-permute-start(f32[12,1,8]{1,2,0:T(8,128)S(1)} %get-tuple-element.128), channel_id=1, source_target_pairs={{0,1},{1,2},{2,3},{3,4},{4,5},{5,6},{6,7},{7,0},{8,9},{9,10},{10,1... | collective-permute-start | bytes 1160 | tf_op jit(solution)/shard_map/ppermute | solution.py:19
  73.2 8.6 %collective-permute-done.4 = f32[12,1,8]{1,2,0:T(8,128)S(1)} collective-permute-done((f32[12,1,8]{1,2,0:T(8,128)S(1)}, f32[12,1,8]{1,2,0:T(8,128)S(1)}, u32[]{:S(2)}, u32[]{:S(2)}) %collective-permute-start.4) | collective-permute-done | bytes 416 | tf_op jit(solution)/shard_map/ppermute | solution.py:19
  81.9 2.9 %collective-permute-start.7 = (f32[12,18,1]{1,2,0:T(1,128)S(1)}, f32[12,18,1]{1,2,0:T(1,128)S(1)}, u32[]{:S(2)}, u32[]{:S(2)}) collective-permute-start(f32[12,18,1]{1,2,0:T(1,128)S(1)} %get-tuple-element.123), channel_id=1, source_target_pairs={{8,0},{16,8},{24,16},{32,24},{40,32},{48,40},{56,48},{64,56},{72,6... | collective-permute-start | bytes 2600 | tf_op jit(solution)/shard_map/ppermute | solution.py:20
  84.8 1.9 %collective-permute-start.6 = (f32[12,18,1]{1,2,0:T(1,128)S(1)}, f32[12,18,1]{1,2,0:T(1,128)S(1)}, u32[]{:S(2)}, u32[]{:S(2)}) collective-permute-start(f32[12,18,1]{1,2,0:T(1,128)S(1)} %get-tuple-element.122), channel_id=1, source_target_pairs={{0,8},{8,16},{16,24},{24,32},{32,40},{40,48},{48,56},{56,64},{64,7... | collective-permute-start | bytes 2600 | tf_op jit(solution)/shard_map/ppermute | solution.py:19
  86.7 6.9 %collective-permute-done.6 = f32[12,18,1]{1,2,0:T(1,128)S(1)} collective-permute-done((f32[12,18,1]{1,2,0:T(1,128)S(1)}, f32[12,18,1]{1,2,0:T(1,128)S(1)}, u32[]{:S(2)}, u32[]{:S(2)}) %collective-permute-start.6) | collective-permute-done | bytes 896 | tf_op jit(solution)/shard_map/ppermute | solution.py:19
  98.4 7.5 %collective-permute-start.8 = (f32[12,48,1]{1,2,0:T(1,128)S(1)}, f32[12,48,1]{1,2,0:T(1,128)S(1)}, u32[]{:S(2)}, u32[]{:S(2)}) collective-permute-start(f32[12,48,1]{1,2,0:T(1,128)S(1)} %get-tuple-element.120), channel_id=1, source_target_pairs={{8,0},{16,8},{24,16},{32,24},{40,32},{48,40},{56,48},{64,56},{72,6... | collective-permute-start | bytes 6920 | tf_op jit(solution)/shard_map/ppermute | solution.py:20
  107.9 2.0 %collective-permute-start.10 = (f32[12,1,10]{1,0,2:T(8,128)S(1)}, f32[12,1,10]{1,0,2:T(8,128)S(1)}, u32[]{:S(2)}, u32[]{:S(2)}) collective-permute-start(f32[12,1,10]{1,0,2:T(8,128)S(1)} %get-tuple-element.127), channel_id=1, source_target_pairs={{0,1},{1,2},{2,3},{3,4},{4,5},{5,6},{6,7},{7,0},{8,9},{9,10},{10,1... | collective-permute-start | bytes 1448 | tf_op jit(solution)/shard_map/ppermute | solution.py:19
  109.9 8.6 %collective-permute-start.11 = (f32[12,1,10]{1,0,2:T(8,128)S(1)}, f32[12,1,10]{1,0,2:T(8,128)S(1)}, u32[]{:S(2)}, u32[]{:S(2)}) collective-permute-start(f32[12,1,10]{1,0,2:T(8,128)S(1)} %get-tuple-element.126), channel_id=1, source_target_pairs={{1,0},{2,1},{3,2},{4,3},{5,4},{6,5},{7,6},{0,7},{9,8},{10,9},{11,1... | collective-permute-start | bytes 1448 | tf_op jit(solution)/shard_map/ppermute | solution.py:20
  123.0 7.5 %collective-permute-start.13 = (f32[12,20,1]{1,0,2:T(8,128)S(1)}, f32[12,20,1]{1,0,2:T(8,128)S(1)}, u32[]{:S(2)}, u32[]{:S(2)}) collective-permute-start(f32[12,20,1]{1,0,2:T(8,128)S(1)} %get-tuple-element.118), channel_id=1, source_target_pairs={{8,0},{16,8},{24,16},{32,24},{40,32},{48,40},{56,48},{64,56},{72,6... | collective-permute-start | bytes 2888 | tf_op jit(solution)/shard_map/ppermute | solution.py:20
  132.1 2.0 %add_select_fusion = f32[12,1,1]{1,0,2:T(8,128)S(1)} fusion(f32[12,20,1]{1,0,2:T(8,128)S(1)} %collective-permute-done.13, f32[12,16,8]{1,0,2:T(8,128)S(1)} %scatter-add.34, s32[]{:T(128)} %bitcast.9, s32[]{:T(128)} %bitcast.10, pred[]{:T(512)} %and_reduce_fusion), kind=kLoop, calls=%fused_computation.66 | loop fusion | flops 24 | bytes 153 | tf_op jit(solution)/shard_map/select.13
  138.2 23.5 %all_to_all.10 = f32[64,1,1536]{2,1,0:T(1,128)S(1)} all-to-all(f32[64,1,1536]{2,1,0:T(1,128)} %reshape.447), channel_id=1, replica_groups=mesh['mem'=64,'band'=8] {'mem'}, dimensions={0} | all-to-all | bytes 786432 | tf_op jit(solution)/shard_map/all_to_all | solution.py:39
  161.7 2.3 %reduce.24 = f32[64,1536]{1,0:T(8,128)} reduce(f32[64,1,1536]{2,1,0:T(1,128)S(1)} %all_to_all.10, f32[]{:T(128)} %broadcast.573), dimensions={1}, to_apply=%all_to_all.7.reduce_sub_computation | reduce | bytes 786436 | tf_op jit(solution)/shard_map/all_to_all | solution.py:39
  164.1 2.1 %reshape.448 = f32[64,12,8,16]{3,2,1,0:T(8,128)S(1)} reshape(f32[64,1536]{1,0:T(8,128)} %reduce.24) | data formatting | bytes 786432
  168.0 2.4 %copy.133 = f32[1,12,16,512]{3,2,1,0:T(8,128)S(1)} copy(f32[1,12,16,512]{2,3,1,0:T(8,128)} %copy_bitcast_fusion) | data formatting | bytes 786432 | tf_op jit(solution)/shard_map/broadcast_in_dim;reshape | solution.py:158
  170.5 9.1 %collective-permute-start.15 = (f32[1,12,1,512]{3,2,1,0:T(1,128)S(1)}, f32[1,12,1,512]{3,2,1,0:T(1,128)S(1)}, u32[]{:S(2)}, u32[]{:S(2)}) collective-permute-start(f32[1,12,1,512]{3,2,1,0:T(1,128)S(1)} %get-tuple-element.111), channel_id=1, source_target_pairs={{1,0},{2,1},{3,2},{4,3},{5,4},{6,5},{7,6},{9,8},{10,9},{11,10},{12... | collective-permute-start | bytes 73736 | tf_op jit(solution)/shard_map/ppermute | solution.py:20
  182.4 7.8 %collective-permute-done.14 = f32[1,12,1,512]{3,2,1,0:T(1,128)S(1)} collective-permute-done((f32[1,12,1,512]{3,2,1,0:T(1,128)S(1)}, f32[1,12,1,512]{3,2,1,0:T(1,128)S(1)}, u32[]{:S(2)}, u32[]{:S(2)}) %collective-permute-start.14) | collective-permute-done | bytes 24608 | tf_op jit(solution)/shard_map/ppermute | solution.py:19
  (120 shorter events, 37.4 us)
Async XLA Ops:
  1.8 24.3 %collective-permute-start.3 = (f32[1,12,1,512]{3,2,1,0:T(1,128)S(1)}, f32[1,12,1,512]{3,2,1,0:T(1,128)S(1)}, u32[]{:S(2)}, u32[]{:S(2)}) collective-permute-start(f32[1,12,1,512]{3,2,1,0:T(1,128)S(1)} %get-tuple-element.117), channel_id=1, source_target_pairs={{1,0},{2,1},{3,2},{4,3},{5,4},{6,5},{7,6},{9,8},{10,9},{11,10},{12... | collective-permute-start | bytes 73736 | tf_op jit(solution)/shard_map/ppermute | solution.py:20
  13.0 13.1 %collective-permute-start.2 = (f32[1,12,1,512]{3,2,1,0:T(1,128)S(1)}, f32[1,12,1,512]{3,2,1,0:T(1,128)S(1)}, u32[]{:S(2)}, u32[]{:S(2)}) collective-permute-start(f32[1,12,1,512]{3,2,1,0:T(1,128)S(1)} %get-tuple-element.116), channel_id=1, source_target_pairs={{0,1},{1,2},{2,3},{3,4},{4,5},{5,6},{6,7},{8,9},{9,10},{10,11},{11... | collective-permute-start | bytes 73736 | tf_op jit(solution)/shard_map/ppermute | solution.py:19
  16.8 77.1 %collective-permute-start.1 = (f32[12,48,1]{1,2,0:T(1,128)}, f32[12,48,1]{1,2,0:T(1,128)S(1)}, u32[]{:S(2)}, u32[]{:S(2)}) collective-permute-start(f32[12,48,1]{1,2,0:T(1,128)} %get-tuple-element.125), channel_id=1, source_target_pairs={{8,0},{16,8},{24,16},{32,24},{40,32},{48,40},{56,48},{64,56},{72,6... | collective-permute-start | bytes 6920 | tf_op jit(solution)/shard_map/ppermute | solution.py:20
  24.1 69.9 %collective-permute-start = (f32[12,48,1]{1,2,0:T(1,128)}, f32[12,48,1]{1,2,0:T(1,128)S(1)}, u32[]{:S(2)}, u32[]{:S(2)}) collective-permute-start(f32[12,48,1]{1,2,0:T(1,128)} %get-tuple-element.124), channel_id=1, source_target_pairs={{0,8},{8,16},{16,24},{24,32},{32,40},{40,48},{48,56},{56,64},{64,7... | collective-permute-start | bytes 6920 | tf_op jit(solution)/shard_map/ppermute | solution.py:19
  34.8 24.0 %all-to-all-start = ((f32[64,1,1536]{2,1,0:T(1,128)}), f32[64,1,1536]{2,1,0:T(1,128)S(1)}, u32[]{:S(2)}, u32[]{:S(2)}) async-start(f32[64,1,1536]{2,1,0:T(1,128)} %reshape.445), calls=%async_computation | async-start | bytes 786432 | tf_op jit(solution)/shard_map/all_to_all | solution.py:33
  61.9 32.1 %copy-start.4 = (f32[12,48,24]{1,2,0:T(8,128)S(1)}, f32[12,48,24]{1,2,0:T(8,128)}, u32[]{:S(2)}) copy-start(f32[12,48,24]{1,2,0:T(8,128)} %copy-done.3) | copy-start | bytes 165892
  61.9 32.1 %copy-start.12 = (f32[26]{0:T(128)S(1)}, f32[26]{0:T(128)}, u32[]{:S(2)}) copy-start(f32[26]{0:T(128)} %get-tuple-element.138) | copy-start | bytes 316
  61.9 32.1 %copy-start.13 = (f32[26]{0:T(128)S(1)}, f32[26]{0:T(128)}, u32[]{:S(2)}) copy-start(f32[26]{0:T(128)} %get-tuple-element.139) | copy-start | bytes 316
  61.9 32.9 %copy-start.15 = (f32[12,1,256]{2,1,0:T(1,128)S(1)}, f32[12,1,256]{2,1,0:T(1,128)}, u32[]{:S(2)}) copy-start(f32[12,1,256]{2,1,0:T(1,128)} %param.30) | copy-start | bytes 36868
  61.9 32.9 %copy-start.16 = (f32[1,256]{1,0:T(1,128)S(1)}, f32[1,256]{1,0:T(1,128)}, u32[]{:S(2)}) copy-start(f32[1,256]{1,0:T(1,128)} %param.31) | copy-start | bytes 3076
  61.9 32.9 %copy-start.17 = (s32[1,256]{1,0:T(1,128)S(1)}, s32[1,256]{1,0:T(1,128)}, u32[]{:S(2)}) copy-start(s32[1,256]{1,0:T(1,128)} %param.29) | copy-start | bytes 3076
  62.2 56.4 %copy-start.6 = (s32[2]{0:T(128)S(1)}, s32[2]{0:T(128)}, u32[]{:S(2)}) copy-start(s32[2]{0:T(128)} %copy-done.5) | copy-start | bytes 28
  62.3 10.9 %collective-permute-start.5 = (f32[12,1,8]{1,2,0:T(8,128)S(1)}, f32[12,1,8]{1,2,0:T(8,128)S(1)}, u32[]{:S(2)}, u32[]{:S(2)}) collective-permute-start(f32[12,1,8]{1,2,0:T(8,128)S(1)} %get-tuple-element.129), channel_id=1, source_target_pairs={{1,0},{2,1},{3,2},{4,3},{5,4},{6,5},{7,6},{0,7},{9,8},{10,9},{11,1... | collective-permute-start | bytes 1160 | tf_op jit(solution)/shard_map/ppermute | solution.py:20
  70.7 11.1 %collective-permute-start.4 = (f32[12,1,8]{1,2,0:T(8,128)S(1)}, f32[12,1,8]{1,2,0:T(8,128)S(1)}, u32[]{:S(2)}, u32[]{:S(2)}) collective-permute-start(f32[12,1,8]{1,2,0:T(8,128)S(1)} %get-tuple-element.128), channel_id=1, source_target_pairs={{0,1},{1,2},{2,3},{3,4},{4,5},{5,6},{6,7},{7,0},{8,9},{9,10},{10,1... | collective-permute-start | bytes 1160 | tf_op jit(solution)/shard_map/ppermute | solution.py:19
  81.9 4.8 %collective-permute-start.7 = (f32[12,18,1]{1,2,0:T(1,128)S(1)}, f32[12,18,1]{1,2,0:T(1,128)S(1)}, u32[]{:S(2)}, u32[]{:S(2)}) collective-permute-start(f32[12,18,1]{1,2,0:T(1,128)S(1)} %get-tuple-element.123), channel_id=1, source_target_pairs={{8,0},{16,8},{24,16},{32,24},{40,32},{48,40},{56,48},{64,56},{72,6... | collective-permute-start | bytes 2600 | tf_op jit(solution)/shard_map/ppermute | solution.py:20
  84.8 8.9 %collective-permute-start.6 = (f32[12,18,1]{1,2,0:T(1,128)S(1)}, f32[12,18,1]{1,2,0:T(1,128)S(1)}, u32[]{:S(2)}, u32[]{:S(2)}) collective-permute-start(f32[12,18,1]{1,2,0:T(1,128)S(1)} %get-tuple-element.122), channel_id=1, source_target_pairs={{0,8},{8,16},{16,24},{24,32},{32,40},{40,48},{48,56},{56,64},{64,7... | collective-permute-start | bytes 2600 | tf_op jit(solution)/shard_map/ppermute | solution.py:19
  96.5 9.5 %collective-permute-start.9 = (f32[12,48,1]{1,2,0:T(1,128)S(1)}, f32[12,48,1]{1,2,0:T(1,128)S(1)}, u32[]{:S(2)}, u32[]{:S(2)}) collective-permute-start(f32[12,48,1]{1,2,0:T(1,128)S(1)} %get-tuple-element.121), channel_id=1, source_target_pairs={{0,8},{8,16},{16,24},{24,32},{32,40},{40,48},{48,56},{56,64},{64,7... | collective-permute-start | bytes 6920 | tf_op jit(solution)/shard_map/ppermute | solution.py:19
  98.4 8.9 %collective-permute-start.8 = (f32[12,48,1]{1,2,0:T(1,128)S(1)}, f32[12,48,1]{1,2,0:T(1,128)S(1)}, u32[]{:S(2)}, u32[]{:S(2)}) collective-permute-start(f32[12,48,1]{1,2,0:T(1,128)S(1)} %get-tuple-element.120), channel_id=1, source_target_pairs={{8,0},{16,8},{24,16},{32,24},{40,32},{48,40},{56,48},{64,56},{72,6... | collective-permute-start | bytes 6920 | tf_op jit(solution)/shard_map/ppermute | solution.py:20
  107.9 11.6 %collective-permute-start.10 = (f32[12,1,10]{1,0,2:T(8,128)S(1)}, f32[12,1,10]{1,0,2:T(8,128)S(1)}, u32[]{:S(2)}, u32[]{:S(2)}) collective-permute-start(f32[12,1,10]{1,0,2:T(8,128)S(1)} %get-tuple-element.127), channel_id=1, source_target_pairs={{0,1},{1,2},{2,3},{3,4},{4,5},{5,6},{6,7},{7,0},{8,9},{9,10},{10,1... | collective-permute-start | bytes 1448 | tf_op jit(solution)/shard_map/ppermute | solution.py:19
  109.9 11.1 %collective-permute-start.11 = (f32[12,1,10]{1,0,2:T(8,128)S(1)}, f32[12,1,10]{1,0,2:T(8,128)S(1)}, u32[]{:S(2)}, u32[]{:S(2)}) collective-permute-start(f32[12,1,10]{1,0,2:T(8,128)S(1)} %get-tuple-element.126), channel_id=1, source_target_pairs={{1,0},{2,1},{3,2},{4,3},{5,4},{6,5},{7,6},{0,7},{9,8},{10,9},{11,1... | collective-permute-start | bytes 1448 | tf_op jit(solution)/shard_map/ppermute | solution.py:20
  121.1 10.4 %collective-permute-start.12 = (f32[12,20,1]{1,0,2:T(8,128)S(1)}, f32[12,20,1]{1,0,2:T(8,128)S(1)}, u32[]{:S(2)}, u32[]{:S(2)}) collective-permute-start(f32[12,20,1]{1,0,2:T(8,128)S(1)} %get-tuple-element.119), channel_id=1, source_target_pairs={{0,8},{8,16},{16,24},{24,32},{32,40},{40,48},{48,56},{56,64},{64,7... | collective-permute-start | bytes 2888 | tf_op jit(solution)/shard_map/ppermute | solution.py:19
  123.0 8.9 %collective-permute-start.13 = (f32[12,20,1]{1,0,2:T(8,128)S(1)}, f32[12,20,1]{1,0,2:T(8,128)S(1)}, u32[]{:S(2)}, u32[]{:S(2)}) collective-permute-start(f32[12,20,1]{1,0,2:T(8,128)S(1)} %get-tuple-element.118), channel_id=1, source_target_pairs={{8,0},{16,8},{24,16},{32,24},{40,32},{48,40},{56,48},{64,56},{72,6... | collective-permute-start | bytes 2888 | tf_op jit(solution)/shard_map/ppermute | solution.py:20
  170.5 11.9 %collective-permute-start.15 = (f32[1,12,1,512]{3,2,1,0:T(1,128)S(1)}, f32[1,12,1,512]{3,2,1,0:T(1,128)S(1)}, u32[]{:S(2)}, u32[]{:S(2)}) collective-permute-start(f32[1,12,1,512]{3,2,1,0:T(1,128)S(1)} %get-tuple-element.111), channel_id=1, source_target_pairs={{1,0},{2,1},{3,2},{4,3},{5,4},{6,5},{7,6},{9,8},{10,9},{11,10},{12... | collective-permute-start | bytes 73736 | tf_op jit(solution)/shard_map/ppermute | solution.py:20
  179.6 10.6 %collective-permute-start.14 = (f32[1,12,1,512]{3,2,1,0:T(1,128)S(1)}, f32[1,12,1,512]{3,2,1,0:T(1,128)S(1)}, u32[]{:S(2)}, u32[]{:S(2)}) collective-permute-start(f32[1,12,1,512]{3,2,1,0:T(1,128)S(1)} %get-tuple-element.110), channel_id=1, source_target_pairs={{0,1},{1,2},{2,3},{3,4},{4,5},{5,6},{6,7},{8,9},{9,10},{10,11},{11... | collective-permute-start | bytes 73736 | tf_op jit(solution)/shard_map/ppermute | solution.py:19
  (12 other events, 250.7 us)
where the time goes:
time: 192 us
  starting transfers between devices  87.1 us (45%)
  waiting for transfers between devices  39.6 us (21%)
  local copies, waits for them, and re-layouts  24.2 us (13%)
  blocking collectives  23.5 us (12%)
  other arithmetic  13.4 us (7%)
  matrix products  2.46 us (1%)
    ppermute x8, starting transfers between devices, padded_2(): after = lax.ppermute(initial, axis, down)  62.6 us
    ppermute x8, waiting for transfers between devices, padded_2(): before = lax.ppermute(last, axis, up)  23.6 us
    all_to_all x1, blocking collectives, from_everyone(): return lax.all_to_all(copies, axis, split_axis=0, concat_axis=0, tiled=True)  23.5 us
    ppermute x8, starting transfers between devices, padded_2(): before = lax.ppermute(last, axis, up)  15.4 us
    all_to_all x1, waiting for transfers between devices, sum_at_owner(): parts = lax.all_to_all(cut_along(array, dim, size), axis, 0, 0, tiled=True)  12.4 us
    unnamed x44, local copies, waits for them, and re-layouts  10.9 us
    all_to_all x1, starting transfers between devices, sum_at_owner(): parts = lax.all_to_all(cut_along(array, dim, size), axis, 0, 0, tiled=True)  9.07 us
    another operation x2, local copies, waits for them, and re-layouts, shards(): gradient = smooth_local(members_f * coarse_gradient[None] * member_scale)  4.25 us
  transfers between devices with their start and end apart: 17, of which 9 were waited for; matrix products, arithmetic and copies ran while one was open for 10% of the time, Pallas kernels for 0%

commit v1 on v0

v1 whole, which is shorter than its diff:
```python
import functools
import math

import jax
import jax.numpy as jnp
from jax import lax
from jax.experimental import pallas as pl
from jax.experimental.pallas import tpu as pltpu
from jax.sharding import PartitionSpec as P

LEV = 12
LPAD = 16
ROWS = 16
COLS = 512
GROUPS = 64
BLOCK = COLS // GROUPS
FRAME = BLOCK + 2
FINE_R = 48
FINE_C = 24
NOBS = 256
Q = LEV * (ROWS + 2)
TILES_PER = 17
CHUNK = TILES_PER * 128
MAIN = LEV * ROWS

advect_rate = 0.25
highest = lax.Precision.HIGHEST


def lon_smooth(x):
    axis = x.ndim - 1
    return 0.25 * pltpu.roll(x, 1, axis) + 0.5 * x + 0.25 * pltpu.roll(x, COLS - 1, axis)


def interp(j):
    n = 2 * j + 4
    return n // 6, (n % 6) / 6.0


def product_kernel(scale, alpha_ref, ens_ref, prev_ref, next_ref, out_ref, pad, x_ref, xt_lo, xt_hi, flat):
    pad[:, 8:24, :] = alpha_ref[...]
    pad[:, 7, :] = prev_ref[1]
    pad[:, 24, :] = next_ref[0]
    body = 0.25 * pad[:, 7:23, :] + 0.5 * alpha_ref[...] + 0.25 * pad[:, 9:25, :]
    body = lon_smooth(body) * (ens_ref[...].astype(jnp.float32) * scale)
    top = 0.25 * prev_ref[0] + 0.5 * prev_ref[1] + 0.25 * alpha_ref[:, 0, :]
    low = 0.25 * alpha_ref[:, ROWS - 1, :] + 0.5 * next_ref[0] + 0.25 * next_ref[1]
    x_ref[:MAIN, :] = body.reshape(MAIN, COLS)
    x_ref[MAIN : MAIN + LEV, :] = lon_smooth(top) * (prev_ref[2] * scale)
    x_ref[MAIN + LEV : Q, :] = lon_smooth(low) * (next_ref[2] * scale)
    x_ref[Q:, :] = jnp.zeros((256 - Q, COLS), jnp.float32)
    for half, xt in enumerate((xt_lo, xt_hi)):
        xt[8 : 8 + COLS, :] = x_ref[128 * half : 128 * (half + 1), :].T
        xt[7:8, :] = xt[7 + COLS : 8 + COLS, :]
        xt[8 + COLS : 9 + COLS, :] = xt[8:9, :]
    flat[:, FRAME * Q :] = jnp.zeros((GROUPS, CHUNK - FRAME * Q), jnp.float32)
    for c in range(FRAME):
        rows = pl.ds(7 + c, GROUPS, stride=BLOCK)
        flat[:, c * Q : c * Q + 128] = xt_lo[rows, :]
        flat[:, c * Q + 128 : (c + 1) * Q] = xt_hi[rows, :][:, : Q - 128]
    for t in range(TILES_PER):
        out_ref[pl.ds(t, GROUPS, stride=TILES_PER), :] = flat[:, 128 * t : 128 * (t + 1)]


def tile_kernel(g_ref, bg_ref, lower_ref, weight_ref, row_ref, col_ref, val_ref, prec_ref,
                adv_ref, own_ref, up_ref, down_ref, flat):
    for t in range(TILES_PER):
        part = g_ref[pl.ds(t, GROUPS, stride=TILES_PER), :]
        flat[0:1, 128 * t : 128 * (t + 1)] = jnp.sum(part, axis=0, keepdims=True)
    q = lax.broadcasted_iota(jnp.int32, (1, Q), 1)
    spot = jnp.where(q < MAIN, (q & 15) + 1, jnp.where(q < MAIN + LEV, 0, ROWS + 1))
    level = jnp.where(q < MAIN, q >> 4, jnp.where(q < MAIN + LEV, q - MAIN, q - MAIN - LEV))
    mask = lax.broadcasted_iota(jnp.int32, (LPAD, Q), 0) == level
    low = lower_ref[...] + 1
    weight = weight_ref[...]

    def table(place):
        return jnp.where(place == low, 1.0 - weight, 0.0) + jnp.where(place == low + 1, weight, 0.0)

    lat = table(spot)
    spread = [jnp.where(mask, flat[0:1, c * Q : (c + 1) * Q], 0.0) for c in range(FRAME)]
    lat_rows = lax.dot_general(jnp.concatenate(spread, axis=0), lat, (((1,), (1,)), ((), ())), precision=highest,
                               preferred_element_type=jnp.float32).reshape(FRAME, LPAD, FINE_R)
    state = []
    for j in range(-1, FINE_C + 1):
        lo, f = interp(j)
        state.append((1.0 - f) * lat_rows[lo] + f * lat_rows[lo + 1] + bg_ref[j + 1])
    slope = [0.5 * (state[j + 2] - state[j]) for j in range(FINE_C)]
    model = [state[j + 1] - advect_rate * state[j + 1] * slope[j] for j in range(FINE_C)]
    for j in range(FINE_C):
        adv_ref[j] = model[j]
    pick_row = (lax.broadcasted_iota(jnp.int32, (FINE_R, NOBS), 0) == row_ref[...]).astype(jnp.float32)
    pick_col = [(col_ref[...] == j).astype(jnp.float32) for j in range(FINE_C)]
    seen = jnp.dot(jnp.concatenate(model, axis=0), pick_row, precision=highest,
                   preferred_element_type=jnp.float32).reshape(FINE_C, LPAD, NOBS)
    observed = sum(pick_col[j] * seen[j] for j in range(FINE_C))
    weighted = prec_ref[...] * (observed - val_ref[...])
    back = jnp.concatenate([pick_col[j] * weighted for j in range(FINE_C)], axis=0)
    cot = lax.dot_general(back, pick_row, (((1,), (1,)), ((), ())), precision=highest,
                          preferred_element_type=jnp.float32).reshape(FINE_C, LPAD, FINE_R)
    half_rate = 0.5 * advect_rate
    flux = [half_rate * state[j + 1] * cot[j] for j in range(FINE_C)]
    total = [None] * FRAME
    for j in range(-1, FINE_C + 1):
        adj = None
        if 0 <= j < FINE_C:
            adj = cot[j] - advect_rate * cot[j] * slope[j]
        if j + 1 < FINE_C:
            adj = flux[j + 1] if adj is None else adj + flux[j + 1]
        if j - 1 >= 0:
            adj = -flux[j - 1] if adj is None else adj - flux[j - 1]
        lo, f = interp(j)
        for c, w in ((lo, 1.0 - f), (lo + 1, f)):
            if w:
                total[c] = w * adj if total[c] is None else total[c] + w * adj
    coarse = jnp.concatenate(total, axis=0)
    for place, ref in ((spot, own_ref), (spot + ROWS, up_ref), (spot - ROWS, down_ref)):
        lat = table(place)
        wide = jnp.dot(coarse, lat, precision=highest, preferred_element_type=jnp.float32).reshape(FRAME, LPAD, Q)
        for c in range(FRAME):
            flat[0:1, c * Q : (c + 1) * Q] = jnp.sum(jnp.where(mask, wide[c], 0.0), axis=0, keepdims=True)
        for t in range(TILES_PER):
            ref[t : t + 1, :] = flat[0:1, 128 * t : 128 * (t + 1)]


def share_kernel(own_ref, prev_ref, next_ref, out_ref):
    total = own_ref[...] + prev_ref[...] + next_ref[...]
    for m in range(GROUPS):
        out_ref[TILES_PER * m : TILES_PER * (m + 1), :] = total


def gradient_kernel(scale, g_ref, ens_ref, prev_ref, next_ref, out_ref, pad, xt_lo, xt_hi, flat):
    for t in range(TILES_PER):
        flat[:, 128 * t : 128 * (t + 1)] = g_ref[pl.ds(t, GROUPS, stride=TILES_PER), :]
    slots = [flat[:, c * Q : (c + 1) * Q] for c in range(FRAME)]
    slots[1] = slots[1] + pltpu.roll(slots[FRAME - 1], 1, 0)
    slots[BLOCK] = slots[BLOCK] + pltpu.roll(slots[0], GROUPS - 1, 0)
    for c in range(1, BLOCK + 1):
        rows = pl.ds(c - 1, GROUPS, stride=BLOCK)
        xt_lo[rows, :] = slots[c][:, :128]
        xt_hi[rows, : Q - 128] = slots[c][:, 128:]
    lo = xt_lo[...].T * scale
    hi = xt_hi[...].T * scale
    field = jnp.concatenate([lo, hi[: MAIN - 128, :]], axis=0).reshape(LEV, ROWS, COLS) * ens_ref[...].astype(jnp.float32)
    pad[:, 8:24, :] = field
    pad[:, 7, :] = hi[MAIN - 128 : MAIN - 128 + LEV, :] * prev_ref[2]
    pad[:, 24, :] = hi[MAIN - 128 + LEV : Q - 128, :] * next_ref[2]
    out_ref[...] = lon_smooth(0.25 * pad[:, 7:23, :] + 0.5 * field + 0.25 * pad[:, 9:25, :])


def call(kernel, out, scratch, *args):
    return pl.pallas_call(
        kernel,
        out_shape=out,
        in_specs=[pl.BlockSpec(memory_space=pltpu.VMEM)] * len(args),
        out_specs=jax.tree.map(lambda _: pl.BlockSpec(memory_space=pltpu.VMEM), out),
        scratch_shapes=scratch,
        compiler_params=pltpu.CompilerParams(vmem_limit_bytes=40 * 1024 * 1024),
    )(*args)


def f32(*shape):
    return jax.ShapeDtypeStruct(shape, jnp.float32)


def both_ways(up_value, down_value, axis, wrap):
    size = lax.axis_size(axis)
    up = [(i, (i + 1) % size) for i in range(size if wrap else size - 1)]
    down = [(j, i) for i, j in up]
    return lax.ppermute(up_value, axis, up), lax.ppermute(down_value, axis, down)


def exchange(flat):
    parts = lax.all_to_all(flat.reshape(GROUPS, 1, CHUNK), "mem", 0, 0, tiled=True)
    return parts.reshape(GROUPS * TILES_PER, 128)


def shards(ensemble, alpha, lat_lower, lat_weight, background, obs_cell, obs_value, obs_precision):
    scale = 1.0 / math.sqrt(GROUPS - 1)
    ens = ensemble[0]
    alf = alpha[0]
    last = jnp.stack([alf[:, ROWS - 2], alf[:, ROWS - 1], ens[:, ROWS - 1].astype(jnp.float32)])
    first = jnp.stack([alf[:, 0], alf[:, 1], ens[:, 0].astype(jnp.float32)])
    before, after = both_ways(last, first, "band", False)

    grid = background.reshape(LEV, FINE_R, FINE_C).transpose(2, 0, 1)
    left, right = both_ways(grid[FINE_C - 1], grid[0], "mem", True)
    wide = jnp.concatenate([left[None], grid, right[None]], axis=0)
    wide = jnp.pad(wide, ((0, 0), (0, LPAD - LEV), (0, 0)))
    value = jnp.pad(obs_value[:, 0, :], ((0, LPAD - LEV), (0, 0)))

    vmem = pltpu.VMEM
    packed = call(
        functools.partial(product_kernel, scale),
        f32(GROUPS * TILES_PER, 128),
        [vmem((LEV, 32, COLS), jnp.float32), vmem((256, COLS), jnp.float32), vmem((COLS + 16, 128), jnp.float32),
         vmem((COLS + 16, 128), jnp.float32), vmem((GROUPS, CHUNK), jnp.float32)],
        alf, ens, before, after,
    )
    gathered = exchange(packed)
    moved, own, up, down = call(
        tile_kernel,
        (f32(FINE_C, LPAD, FINE_R), f32(TILES_PER, 128), f32(TILES_PER, 128), f32(TILES_PER, 128)),
        [vmem((8, CHUNK), jnp.float32)],
        gathered, wide, lat_lower[:, None], lat_weight[:, None], obs_cell // FINE_C, obs_cell % FINE_C, value, obs_precision,
    )
    from_prev, from_next = both_ways(up, down, "band", False)
    shared = call(share_kernel, f32(GROUPS * TILES_PER, 128), [], own, from_prev, from_next)
    everyone = exchange(shared)
    gradient = call(
        functools.partial(gradient_kernel, scale),
        f32(LEV, ROWS, COLS),
        [vmem((LEV, 32, COLS), jnp.float32), vmem((COLS, 128), jnp.float32), vmem((COLS, 128), jnp.float32),
         vmem((GROUPS, CHUNK), jnp.float32)],
        everyone, ens, before, after,
    )
    advected = moved[:, :LEV].transpose(1, 2, 0).reshape(LEV, 1, FINE_R * FINE_C)
    return (advected, gradient[None])


def solution(mesh):
    return jax.shard_map(
        shards,
        mesh=mesh,
        in_specs=(
            P("mem", None, "band", None),
            P("mem", None, "band", None),
            P("band"),
            P("band"),
            P(None, ("band", "mem"), None),
            P(("band", "mem"), None),
            P(None, ("band", "mem"), None),
            P(("band", "mem"), None),
        ),
        out_specs=(P(None, ("band", "mem"), None), P("mem", None, "band", None)),
        check_vma=False,
    )
```

time: 192 us -> 102 us (0.53)
  the two profiles are of different devices: /device:TPU:6 before, /device:TPU:1 now
where the time goes in v1:
time: 102 us; the launch traced here: 101 us
  waiting for transfers between devices  45.8 us (45%)
  starting transfers between devices  42 us (41%)
  Pallas kernels  6.98 us (7%)
  local copies, waits for them, and re-layouts  5.54 us (5%)
    all_to_all x2, waiting for transfers between devices, exchange(): lax.all_to_all(flat.reshape(GROUPS, 1, CHUNK), 'mem', 0, 0, tiled=True)  24.9 us
    ppermute x3, starting transfers between devices, both_ways(): lax.ppermute(up_value, axis, up)  19.6 us
    ppermute x3, waiting for transfers between devices, both_ways(): lax.ppermute(down_value, axis, down)  17.8 us
    all_to_all x2, starting transfers between devices, exchange(): lax.all_to_all(flat.reshape(GROUPS, 1, CHUNK), 'mem', 0, 0, tiled=True)  17.4 us
    pallas_call x4, Pallas kernels, call(): pl.pallas_call(kernel, out_shape=out, in_specs=[pl.BlockSpec(memory_space...  6.98 us
    ppermute x3, starting transfers between devices, both_ways(): lax.ppermute(down_value, axis, down)  4.95 us
    unnamed x19, local copies, waits for them, and re-layouts  3.95 us
    ppermute x3, waiting for transfers between devices, both_ways(): lax.ppermute(up_value, axis, up)  3.04 us
  transfers between devices with their start and end apart: 8, of which 6 were waited for; matrix products, arithmetic and copies ran while one was open for 2% of the time, Pallas kernels for 0%

profile of v1, /device:TPU:1, one launch (start us, length us, event | category | flops | bytes accessed | tf_op | source)
XLA Modules:
  0.0 101.4 jit_solution(11371176478298921917)
XLA Ops:
  0.6 1.1 %copy.46 = bf16[1,12,16,512]{3,1,2,0:T(8,128)(2,1)S(1)} copy(bf16[1,12,16,512]{3,2,1,0:T(8,128)(2,1)} %param.8) | data formatting | bytes 393216 | tf_op args[0]
  2.1 11.6 %collective-permute-start = (f32[3,12,512]{2,1,0:T(8,128)S(1)}, f32[3,12,512]{2,1,0:T(8,128)S(1)}, u32[]{:S(2)}, u32[]{:S(2)}) collective-permute-start(f32[3,12,512]{2,1,0:T(8,128)S(1)} %pad_maximum_fusion), channel_id=1, source_target_pairs={{0,1},{1,2},{2,3},{3,4},{4,5},{5,6},{6,7},{8,9},{9,10},{10,11},{11... | collective-permute-start | bytes 221192 | tf_op jit(solution)/shard_map/ppermute | solution.py:170
  13.7 1.3 %collective-permute-start.1 = (f32[3,12,512]{2,1,0:T(8,128)S(1)}, f32[3,12,512]{2,1,0:T(8,128)S(1)}, u32[]{:S(2)}, u32[]{:S(2)}) collective-permute-start(f32[3,12,512]{2,1,0:T(8,128)S(1)} %pad_maximum_fusion.1), channel_id=1, source_target_pairs={{1,0},{2,1},{3,2},{4,3},{5,4},{6,5},{7,6},{9,8},{10,9},{11,10},{12... | collective-permute-start | bytes 221192 | tf_op jit(solution)/shard_map/ppermute | solution.py:170
  15.0 0.3 collective-permute-done.prev_ref
  15.3 10.8 %collective-permute-done.1.next_ref = f32[3,12,512]{2,1,0:T(8,128)S(1)} collective-permute-done((f32[3,12,512]{2,1,0:T(8,128)S(1)}, f32[3,12,512]{2,1,0:T(8,128)S(1)}, u32[]{:S(2)}, u32[]{:S(2)}) %collective-permute-start.1) | collective-permute-done | bytes 73760 | tf_op jit(solution)/shard_map/ppermute | solution.py:170
  26.0 1.8 %shard_map.95 = f32[1088,128]{1,0:T(8,128)} custom-call(f32[12,16,512]{2,1,0:T(8,128)S(1)} %bitcast.49, bf16[12,16,512]{2,1,0:T(8,128)(2,1)S(1)} %bitcast.47, f32[3,12,512]{2,1,0:T(8,128)S(1)} %collective-permute-done.prev_ref, f32[3,12,512]{2,1,0:T(8,128)S(1)} %collective-permute-done.1.next_ref), custom_call_target="tpu_custom_call" | custom-call | tf_op jit(solution)/shard_map/pallas_call | solution.py:152
  27.8 10.6 %all-to-all-start = ((f32[64,1,2176]{2,1,0:T(1,128)}), f32[64,1,2176]{2,1,0:T(1,128)S(1)}, u32[]{:S(2)}, u32[]{:S(2)}) async-start(f32[64,1,2176]{2,1,0:T(1,128)} %bitcast.10), calls=%async_computation | async-start | bytes 1114112 | tf_op jit(solution)/shard_map/all_to_all | solution.py:174
  39.0 2.4 %collective-permute-start.3 = (f32[12,48]{1,0:T(8,128)S(1)}, f32[12,48]{1,0:T(8,128)S(1)}, u32[]{:S(2)}, u32[]{:S(2)}) collective-permute-start(f32[12,48]{1,0:T(8,128)S(1)} %get-tuple-element.21), channel_id=1, source_target_pairs={{8,0},{16,8},{24,16},{32,24},{40,32},{48,40},{56,48},{64,56},{72,6... | collective-permute-start | bytes 6920 | tf_op jit(solution)/shard_map/ppermute | solution.py:170
  41.4 3.2 %collective-permute-start.2 = (f32[12,48]{1,0:T(8,128)S(1)}, f32[12,48]{1,0:T(8,128)S(1)}, u32[]{:S(2)}, u32[]{:S(2)}) collective-permute-start(f32[12,48]{1,0:T(8,128)S(1)} %get-tuple-element.20), channel_id=1, source_target_pairs={{0,8},{8,16},{16,24},{24,32},{32,40},{40,48},{48,56},{56,64},{64,7... | collective-permute-start | bytes 6920 | tf_op jit(solution)/shard_map/ppermute | solution.py:170
  44.6 0.6 copy-done.6
  45.4 0.7 copy-done.7
  46.1 0.6 copy-done.4
  46.7 2.7 %collective-permute-done.2 = f32[12,48]{1,0:T(8,128)S(1)} collective-permute-done((f32[12,48]{1,0:T(8,128)S(1)}, f32[12,48]{1,0:T(8,128)S(1)}, u32[]{:S(2)}, u32[]{:S(2)}) %collective-permute-start.2) | collective-permute-done | bytes 2336 | tf_op jit(solution)/shard_map/ppermute | solution.py:170
  49.5 7.6 %all-to-all-done = f32[64,1,2176]{2,1,0:T(1,128)S(1)} async-done(((f32[64,1,2176]{2,1,0:T(1,128)}), f32[64,1,2176]{2,1,0:T(1,128)S(1)}, u32[]{:S(2)}, u32[]{:S(2)}) %all-to-all-start) | async-done | bytes 557088 | tf_op jit(solution)/shard_map/all_to_all | solution.py:174
  57.1 0.7 copy-done.2
  57.8 2.6 %shard_map.96 = (f32[24,16,48]{2,1,0:T(8,128)S(1)}, f32[17,128]{1,0:T(8,128)S(1)}, f32[17,128]{1,0:T(8,128)S(1)}, f32[17,128]{1,0:T(8,128)S(1)}) custom-call(f32[1088,128]{1,0:T(8,128)S(1)} %bitcast.45, f32[26,16,48]{2,1,0:T(8,128)S(1)} %select_maximum_fusion.bg_ref, s32[48,1]{1,0:T(8,128)S(1)} %copy.33.lower_ref, f32[48,1]{1,0:T(8,128)S(1)} %copy.34.weight_ref, ...), custom_call_target="tpu_custom_call" | custom-call | tf_op jit(solution)/shard_map/pallas_call | solution.py:152
  60.4 4.8 %collective-permute-start.4 = (f32[17,128]{1,0:T(8,128)S(1)}, f32[17,128]{1,0:T(8,128)S(1)}, u32[]{:S(2)}, u32[]{:S(2)}) collective-permute-start(f32[17,128]{1,0:T(8,128)S(1)} %get-tuple-element.8), channel_id=1, source_target_pairs={{0,1},{1,2},{2,3},{3,4},{4,5},{5,6},{6,7},{8,9},{9,10},{10,11},{11... | collective-permute-start | bytes 26120 | tf_op jit(solution)/shard_map/ppermute | solution.py:170
  65.2 1.3 %collective-permute-start.5 = (f32[17,128]{1,0:T(8,128)S(1)}, f32[17,128]{1,0:T(8,128)S(1)}, u32[]{:S(2)}, u32[]{:S(2)}) collective-permute-start(f32[17,128]{1,0:T(8,128)S(1)} %get-tuple-element.9), channel_id=1, source_target_pairs={{1,0},{2,1},{3,2},{4,3},{5,4},{6,5},{7,6},{9,8},{10,9},{11,10},{12... | collective-permute-start | bytes 26120 | tf_op jit(solution)/shard_map/ppermute | solution.py:170
  66.5 7.0 %collective-permute-done.5.next_ref = f32[17,128]{1,0:T(8,128)S(1)} collective-permute-done((f32[17,128]{1,0:T(8,128)S(1)}, f32[17,128]{1,0:T(8,128)S(1)}, u32[]{:S(2)}, u32[]{:S(2)}) %collective-permute-start.5) | collective-permute-done | bytes 8736 | tf_op jit(solution)/shard_map/ppermute | solution.py:170
  73.6 0.9 shard_map.97
  74.5 6.8 %all-to-all-start.1 = ((f32[64,1,2176]{2,1,0:T(1,128)}), f32[64,1,2176]{2,1,0:T(1,128)S(1)}, u32[]{:S(2)}, u32[]{:S(2)}) async-start(f32[64,1,2176]{2,1,0:T(1,128)} %bitcast.20), calls=%async_computation.1 | async-start | bytes 1114112 | tf_op jit(solution)/shard_map/all_to_all | solution.py:174
  81.5 0.9 reshape.54
  82.3 17.4 %all-to-all-done.1 = f32[64,1,2176]{2,1,0:T(1,128)S(1)} async-done(((f32[64,1,2176]{2,1,0:T(1,128)}), f32[64,1,2176]{2,1,0:T(1,128)S(1)}, u32[]{:S(2)}, u32[]{:S(2)}) %all-to-all-start.1) | async-done | bytes 557088 | tf_op jit(solution)/shard_map/all_to_all | solution.py:174
  99.7 1.7 %shard_map.98 = f32[12,16,512]{2,1,0:T(8,128)} custom-call(f32[1088,128]{1,0:T(8,128)S(1)} %bitcast.46, bf16[12,16,512]{2,1,0:T(8,128)(2,1)S(1)} %bitcast.48, f32[3,12,512]{2,1,0:T(8,128)S(1)} %collective-permute-done.prev_ref, f32[3,12,512]{2,1,0:T(8,128)S(1)} %collective-permute-done.1.next_ref), custom_call_target="tpu_custom_call" | custom-call | tf_op jit(solution)/shard_map/pallas_call | solution.py:152
  (31 shorter events, 1.2 us)
Async XLA Ops:
  0.6 1.1 %copy-start.1 = (f32[1,12,16,512]{3,2,1,0:T(8,128)S(1)}, f32[1,12,16,512]{3,2,1,0:T(8,128)}, u32[]{:S(2)}) copy-start(f32[1,12,16,512]{3,2,1,0:T(8,128)} %param.9) | copy-start | bytes 1179652
  2.0 24.0 %copy-start = (bf16[1,12,16,512]{3,2,1,0:T(8,128)(2,1)S(1)}, bf16[1,12,16,512]{3,2,1,0:T(8,128)(2,1)}, u32[]{:S(2)}) copy-start(bf16[1,12,16,512]{3,2,1,0:T(8,128)(2,1)} %param.8) | copy-start | bytes 589828
  2.1 13.2 %collective-permute-start = (f32[3,12,512]{2,1,0:T(8,128)S(1)}, f32[3,12,512]{2,1,0:T(8,128)S(1)}, u32[]{:S(2)}, u32[]{:S(2)}) collective-permute-start(f32[3,12,512]{2,1,0:T(8,128)S(1)} %pad_maximum_fusion), channel_id=1, source_target_pairs={{0,1},{1,2},{2,3},{3,4},{4,5},{5,6},{6,7},{8,9},{9,10},{10,11},{11... | collective-permute-start | bytes 221192 | tf_op jit(solution)/shard_map/ppermute | solution.py:170
  13.7 12.4 %collective-permute-start.1 = (f32[3,12,512]{2,1,0:T(8,128)S(1)}, f32[3,12,512]{2,1,0:T(8,128)S(1)}, u32[]{:S(2)}, u32[]{:S(2)}) collective-permute-start(f32[3,12,512]{2,1,0:T(8,128)S(1)} %pad_maximum_fusion.1), channel_id=1, source_target_pairs={{1,0},{2,1},{3,2},{4,3},{5,4},{6,5},{7,6},{9,8},{10,9},{11,10},{12... | collective-permute-start | bytes 221192 | tf_op jit(solution)/shard_map/ppermute | solution.py:170
  27.8 10.6 %copy-start.3 = (f32[12,1,1152]{2,1,0:T(1,128)S(1)}, f32[12,1,1152]{2,1,0:T(1,128)}, u32[]{:S(2)}) copy-start(f32[12,1,1152]{2,1,0:T(1,128)} %param.12) | copy-start | bytes 165892
  27.8 29.3 %all-to-all-start = ((f32[64,1,2176]{2,1,0:T(1,128)}), f32[64,1,2176]{2,1,0:T(1,128)S(1)}, u32[]{:S(2)}, u32[]{:S(2)}) async-start(f32[64,1,2176]{2,1,0:T(1,128)} %bitcast.10), calls=%async_computation | async-start | bytes 1114112 | tf_op jit(solution)/shard_map/all_to_all | solution.py:174
  39.0 5.6 %copy-start.5 = (s32[1,256]{1,0:T(1,128)S(1)}, s32[1,256]{1,0:T(1,128)}, u32[]{:S(2)}) copy-start(s32[1,256]{1,0:T(1,128)} %param.13) | copy-start | bytes 3076
  39.0 7.7 %collective-permute-start.3 = (f32[12,48]{1,0:T(8,128)S(1)}, f32[12,48]{1,0:T(8,128)S(1)}, u32[]{:S(2)}, u32[]{:S(2)}) collective-permute-start(f32[12,48]{1,0:T(8,128)S(1)} %get-tuple-element.21), channel_id=1, source_target_pairs={{8,0},{16,8},{24,16},{32,24},{40,32},{48,40},{56,48},{64,56},{72,6... | collective-permute-start | bytes 6920 | tf_op jit(solution)/shard_map/ppermute | solution.py:170
  41.4 8.1 %collective-permute-start.2 = (f32[12,48]{1,0:T(8,128)S(1)}, f32[12,48]{1,0:T(8,128)S(1)}, u32[]{:S(2)}, u32[]{:S(2)}) collective-permute-start(f32[12,48]{1,0:T(8,128)S(1)} %get-tuple-element.20), channel_id=1, source_target_pairs={{0,8},{8,16},{16,24},{24,32},{32,40},{40,48},{48,56},{56,64},{64,7... | collective-permute-start | bytes 6920 | tf_op jit(solution)/shard_map/ppermute | solution.py:170
  44.6 0.7 copy-start.6
  45.4 0.7 copy-start.7
  46.0 0.7 copy-start.4
  57.1 0.7 copy-start.2
  60.4 6.1 %collective-permute-start.4 = (f32[17,128]{1,0:T(8,128)S(1)}, f32[17,128]{1,0:T(8,128)S(1)}, u32[]{:S(2)}, u32[]{:S(2)}) collective-permute-start(f32[17,128]{1,0:T(8,128)S(1)} %get-tuple-element.8), channel_id=1, source_target_pairs={{0,1},{1,2},{2,3},{3,4},{4,5},{5,6},{6,7},{8,9},{9,10},{10,11},{11... | collective-permute-start | bytes 26120 | tf_op jit(solution)/shard_map/ppermute | solution.py:170
  65.2 8.3 %collective-permute-start.5 = (f32[17,128]{1,0:T(8,128)S(1)}, f32[17,128]{1,0:T(8,128)S(1)}, u32[]{:S(2)}, u32[]{:S(2)}) collective-permute-start(f32[17,128]{1,0:T(8,128)S(1)} %get-tuple-element.9), channel_id=1, source_target_pairs={{1,0},{2,1},{3,2},{4,3},{5,4},{6,5},{7,6},{9,8},{10,9},{11,10},{12... | collective-permute-start | bytes 26120 | tf_op jit(solution)/shard_map/ppermute | solution.py:170
  74.5 25.2 %all-to-all-start.1 = ((f32[64,1,2176]{2,1,0:T(1,128)}), f32[64,1,2176]{2,1,0:T(1,128)S(1)}, u32[]{:S(2)}, u32[]{:S(2)}) async-start(f32[64,1,2176]{2,1,0:T(1,128)} %bitcast.20), calls=%async_computation.1 | async-start | bytes 1114112 | tf_op jit(solution)/shard_map/all_to_all | solution.py:174

commit v2 on v1

v2 whole, which is shorter than its diff:
```python
import functools
import math

import jax
import jax.numpy as jnp
from jax import lax
from jax.experimental import pallas as pl
from jax.experimental.pallas import tpu as pltpu
from jax.sharding import PartitionSpec as P

LEV = 12
LPAD = 16
ROWS = 16
COLS = 512
CHIPS = 32
BANDS = 8
BLOCK = 8
FRAME = BLOCK + 2
FINE_R = 48
FINE_C = 24
NOBS = 256
MAIN = LEV * ROWS
Q = MAIN + 2 * LEV
TILES = 17
CHUNK = TILES * 128

advect_rate = 0.25
highest = lax.Precision.HIGHEST


def lon_smooth(x):
    axis = x.ndim - 1
    return 0.25 * pltpu.roll(x, 1, axis) + 0.5 * x + 0.25 * pltpu.roll(x, COLS - 1, axis)


def interp(j):
    n = 2 * j + 4
    return n // 6, (n % 6) / 6.0


def halo_kernel(alpha_ref, ens_ref, last_ref, first_ref):
    last_ref[0] = alpha_ref[:, ROWS - 2, :]
    last_ref[1] = alpha_ref[:, ROWS - 1, :]
    last_ref[2] = ens_ref[:, ROWS - 1, :].astype(jnp.float32)
    first_ref[0] = alpha_ref[:, 0, :]
    first_ref[1] = alpha_ref[:, 1, :]
    first_ref[2] = ens_ref[:, 0, :].astype(jnp.float32)


def product_kernel(scale, core_ref, alpha_ref, ens_ref, prev_ref, next_ref, keep_ref, send_ref, pad, x_ref, xt_lo, xt_hi, flat):
    pad[:, 8:24, :] = alpha_ref[...]
    pad[:, 7, :] = prev_ref[1]
    pad[:, 24, :] = next_ref[0]
    body = 0.25 * pad[:, 7:23, :] + 0.5 * alpha_ref[...] + 0.25 * pad[:, 9:25, :]
    body = lon_smooth(body) * (ens_ref[...].astype(jnp.float32) * scale)
    top = 0.25 * prev_ref[0] + 0.5 * prev_ref[1] + 0.25 * alpha_ref[:, 0, :]
    low = 0.25 * alpha_ref[:, ROWS - 1, :] + 0.5 * next_ref[0] + 0.25 * next_ref[1]
    x_ref[:MAIN, :] = body.reshape(MAIN, COLS)
    x_ref[MAIN : MAIN + LEV, :] = lon_smooth(top) * (prev_ref[2] * scale)
    x_ref[MAIN + LEV : Q, :] = lon_smooth(low) * (next_ref[2] * scale)
    x_ref[Q:, :] = jnp.zeros((256 - Q, COLS), jnp.float32)
    for half, xt in enumerate((xt_lo, xt_hi)):
        xt[8 : 8 + COLS, :] = x_ref[128 * half : 128 * (half + 1), :].T
        xt[7:8, :] = xt[7 + COLS : 8 + COLS, :]
        xt[8 + COLS : 9 + COLS, :] = xt[8:9, :]
    flat[:, :, FRAME * Q :] = jnp.zeros((2, CHIPS, CHUNK - FRAME * Q), jnp.float32)
    for core in range(2):
        for c in range(FRAME):
            rows = pl.ds(7 + c + BLOCK * core, CHIPS, stride=2 * BLOCK)
            flat[core, :, c * Q : c * Q + 128] = xt_lo[rows, :]
            flat[core, :, c * Q + 128 : (c + 1) * Q] = xt_hi[rows, :][:, : Q - 128]
    first = core_ref[0] == 0
    for t in range(TILES):
        even = flat[0, :, 128 * t : 128 * (t + 1)]
        odd = flat[1, :, 128 * t : 128 * (t + 1)]
        keep_ref[pl.ds(t, CHIPS, stride=TILES), :] = jnp.where(first, even, odd)
        send_ref[pl.ds(t, CHIPS, stride=TILES), :] = jnp.where(first, odd, even)


def tile_kernel(band_ref, g_ref, bg_ref, lat_ref, obs_ref, adv_ref, own_ref, edge_ref, flat):
    for t in range(TILES):
        part = g_ref[pl.ds(t, CHIPS, stride=TILES), :]
        flat[0:1, 128 * t : 128 * (t + 1)] = jnp.sum(part, axis=0, keepdims=True)
    q = lax.broadcasted_iota(jnp.int32, (1, Q), 1)
    spot = jnp.where(q < MAIN, (q & 15) + 1, jnp.where(q < MAIN + LEV, 0, ROWS + 1))
    level = jnp.where(q < MAIN, q >> 4, jnp.where(q < MAIN + LEV, q - MAIN, q - MAIN - LEV))
    mask = lax.broadcasted_iota(jnp.int32, (LPAD, Q), 0) == level
    low = lat_ref[:, 0:1] + 1.0
    weight = lat_ref[:, 1:2]

    def table(place):
        place = place.astype(jnp.float32)
        return jnp.where(place == low, 1.0 - weight, 0.0) + jnp.where(place == low + 1.0, weight, 0.0)

    lat = table(spot)
    spread = [jnp.where(mask, flat[0:1, c * Q : (c + 1) * Q], 0.0) for c in range(FRAME)]
    lat_rows = lax.dot_general(jnp.concatenate(spread, axis=0), lat, (((1,), (1,)), ((), ())), precision=highest,
                               preferred_element_type=jnp.float32).reshape(FRAME, LPAD, FINE_R)
    state = []
    for j in range(-1, FINE_C + 1):
        lo, f = interp(j)
        state.append((1.0 - f) * lat_rows[lo] + f * lat_rows[lo + 1] + bg_ref[j + 1])
    slope = [0.5 * (state[j + 2] - state[j]) for j in range(FINE_C)]
    model = [state[j + 1] - advect_rate * state[j + 1] * slope[j] for j in range(FINE_C)]
    for j in range(FINE_C):
        adv_ref[j] = model[j]
    value = obs_ref[0:LPAD, :]
    precision = obs_ref[LPAD : LPAD + 1, :]
    row = obs_ref[LPAD + 1 : LPAD + 2, :]
    col = obs_ref[LPAD + 2 : LPAD + 3, :]
    fine_row = lax.broadcasted_iota(jnp.int32, (FINE_R, NOBS), 0).astype(jnp.float32)
    pick_row = jnp.where(fine_row == row, 1.0, 0.0)
    pick_col = [jnp.where(col == float(j), 1.0, 0.0) for j in range(FINE_C)]
    seen = jnp.dot(jnp.concatenate(model, axis=0), pick_row, precision=highest,
                   preferred_element_type=jnp.float32).reshape(FINE_C, LPAD, NOBS)
    observed = sum(pick_col[j] * seen[j] for j in range(FINE_C))
    weighted = precision * (observed - value)
    back = jnp.concatenate([pick_col[j] * weighted for j in range(FINE_C)], axis=0)
    cot = lax.dot_general(back, pick_row, (((1,), (1,)), ((), ())), precision=highest,
                          preferred_element_type=jnp.float32).reshape(FINE_C, LPAD, FINE_R)
    half_rate = 0.5 * advect_rate
    flux = [half_rate * state[j + 1] * cot[j] for j in range(FINE_C)]
    total = [None] * FRAME
    for j in range(-1, FINE_C + 1):
        adj = None
        if 0 <= j < FINE_C:
            adj = cot[j] - advect_rate * cot[j] * slope[j]
        if j + 1 < FINE_C:
            adj = flux[j + 1] if adj is None else adj + flux[j + 1]
        if j - 1 >= 0:
            adj = -flux[j - 1] if adj is None else adj - flux[j - 1]
        lo, f = interp(j)
        for c, w in ((lo, 1.0 - f), (lo + 1, f)):
            if w:
                total[c] = w * adj if total[c] is None else total[c] + w * adj
    coarse = jnp.concatenate(total, axis=0)

    def to_coarse(lat):
        wide = jnp.dot(coarse, lat, precision=highest, preferred_element_type=jnp.float32).reshape(FRAME, LPAD, Q)
        for c in range(FRAME):
            flat[0:1, c * Q : (c + 1) * Q] = jnp.sum(jnp.where(mask, wide[c], 0.0), axis=0, keepdims=True)

    band = band_ref[0]
    edge_ref[...] = jnp.zeros_like(edge_ref)
    for place, off, ok in ((spot + ROWS, 1, band < BANDS - 1), (spot - ROWS, -1, band > 0)):
        to_coarse(table(place))

        @pl.when(ok)
        def _():
            for t in range(TILES):
                edge_ref[pl.ds((band + off) * TILES + t, 1), :] = flat[0:1, 128 * t : 128 * (t + 1)]

    to_coarse(lat)
    for t in range(TILES):
        own_ref[t : t + 1, :] = flat[0:1, 128 * t : 128 * (t + 1)]


def share_kernel(own_ref, edge_ref, out_ref):
    total = own_ref[...]
    for b in range(BANDS):
        total = total + edge_ref[TILES * b : TILES * (b + 1), :]
    for m in range(CHIPS):
        out_ref[TILES * m : TILES * (m + 1), :] = total


def gradient_kernel(scale, g_ref, ens_ref, prev_ref, next_ref, out_ref, pad, xt_lo, xt_hi, flat):
    for core in range(2):
        for t in range(TILES):
            flat[core, :, 128 * t : 128 * (t + 1)] = g_ref[pl.ds(core * CHIPS * TILES + t, CHIPS, stride=TILES), :]
    slots = [[flat[core, :, c * Q : (c + 1) * Q] for c in range(FRAME)] for core in range(2)]
    even, odd = slots
    even_first = even[1] + pltpu.roll(odd[FRAME - 1], 1, 0)
    even_last = even[BLOCK] + odd[0]
    odd_first = odd[1] + even[FRAME - 1]
    odd_last = odd[BLOCK] + pltpu.roll(even[0], CHIPS - 1, 0)
    even[1], even[BLOCK], odd[1], odd[BLOCK] = even_first, even_last, odd_first, odd_last
    for core in range(2):
        for c in range(1, BLOCK + 1):
            rows = pl.ds(c - 1 + BLOCK * core, CHIPS, stride=2 * BLOCK)
            xt_lo[rows, :] = slots[core][c][:, :128]
            xt_hi[rows, : Q - 128] = slots[core][c][:, 128:]
    lo = xt_lo[...].T * scale
    hi = xt_hi[...].T * scale
    field = jnp.concatenate([lo, hi[: MAIN - 128, :]], axis=0).reshape(LEV, ROWS, COLS) * ens_ref[...].astype(jnp.float32)
    pad[:, 8:24, :] = field
    pad[:, 7, :] = hi[MAIN - 128 : MAIN - 128 + LEV, :] * prev_ref[2]
    pad[:, 24, :] = hi[MAIN - 128 + LEV : Q - 128, :] * next_ref[2]
    out_ref[...] = lon_smooth(0.25 * pad[:, 7:23, :] + 0.5 * field + 0.25 * pad[:, 9:25, :])


def call(kernel, out, scratch, *args):
    def spec(x):
        return pl.BlockSpec(memory_space=pltpu.SMEM if x.dtype == jnp.int32 else pltpu.VMEM)

    return pl.pallas_call(
        kernel,
        out_shape=out,
        in_specs=[spec(x) for x in args],
        out_specs=jax.tree.map(spec, out),
        scratch_shapes=[pltpu.VMEM(shape, jnp.float32) for shape in scratch],
        compiler_params=pltpu.CompilerParams(vmem_limit_bytes=40 * 1024 * 1024),
    )(*args)


def f32(*shape):
    return jax.ShapeDtypeStruct(shape, jnp.float32)


def both_ways(up_value, down_value, axis, size, wrap):
    up = [(i, (i + 1) % size) for i in range(size if wrap else size - 1)]
    down = [(j, i) for i, j in up]
    return lax.ppermute(up_value, axis, up), lax.ppermute(down_value, axis, down)


def exchange(flat, axis, size):
    parts = lax.all_to_all(flat.reshape(size, 1, CHUNK), axis, 0, 0, tiled=True)
    return parts.reshape(size * TILES, 128)


def shards(ensemble, alpha, lat_lower, lat_weight, background, obs_cell, obs_value, obs_precision):
    scale = 1.0 / math.sqrt(2 * CHIPS - 1)
    core = lax.axis_index("core").astype(jnp.int32).reshape(1)
    band = lax.axis_index("band").astype(jnp.int32).reshape(1)
    ens = ensemble[0]
    alf = alpha[0]
    last, first = call(halo_kernel, (f32(3, LEV, COLS), f32(3, LEV, COLS)), [], alf, ens)
    before, after = both_ways(last, first, "band", BANDS, False)

    grid = background.reshape(LEV, FINE_R, FINE_C).transpose(2, 0, 1)
    left, right = both_ways(grid[FINE_C - 1], grid[0], ("chip", "core"), 2 * CHIPS, True)
    obs = jnp.concatenate(
        [jnp.pad(obs_value[:, 0, :], ((0, LPAD - LEV), (0, 0))), obs_precision, (obs_cell // FINE_C).astype(jnp.float32),
         (obs_cell % FINE_C).astype(jnp.float32), jnp.zeros((24 - LPAD - 3, NOBS), jnp.float32)], axis=0)
    lat = jnp.stack([lat_lower.astype(jnp.float32), lat_weight], axis=1)
    wide = jnp.concatenate([left[None], grid, right[None]], axis=0)
    wide = jnp.pad(wide, ((0, 0), (0, LPAD - LEV), (0, 0)))
    before, after, wide, obs, lat = lax.optimization_barrier((before, after, wide, obs, lat))

    keep, send = call(
        functools.partial(product_kernel, scale),
        (f32(CHIPS * TILES, 128), f32(CHIPS * TILES, 128)),
        [(LEV, 32, COLS), (256, COLS), (COLS + 16, 128), (COLS + 16, 128), (2, CHIPS, CHUNK)],
        core, alf, ens, before, after,
    )
    pair = keep + lax.ppermute(send, "core", [(0, 1), (1, 0)])
    gathered = exchange(pair, "chip", CHIPS)
    moved, own, edge = call(
        tile_kernel,
        (f32(FINE_C, LPAD, FINE_R), f32(TILES, 128), f32(BANDS * TILES, 128)),
        [(8, CHUNK)],
        band, gathered, wide, lat, obs,
    )
    edge = exchange(edge, "band", BANDS)
    shared = call(share_kernel, f32(CHIPS * TILES, 128), [], own, edge)
    everyone = lax.all_gather(exchange(shared, "chip", CHIPS), "core", axis=0, tiled=True)
    gradient = call(
        functools.partial(gradient_kernel, scale),
        f32(LEV, ROWS, COLS),
        [(LEV, 32, COLS), (COLS, 128), (COLS, 128), (2, CHIPS, CHUNK)],
        everyone, ens, before, after,
    )
    advected = moved[:, :LEV].transpose(1, 2, 0).reshape(LEV, 1, FINE_R * FINE_C)
    return (advected, gradient[None])


def solution(mesh):
    member = ("chip", "core")
    tile = ("band", "chip", "core")
    return jax.shard_map(
        shards,
        mesh=jax.sharding.Mesh(mesh.devices.reshape(CHIPS, 2, BANDS), ("chip", "core", "band")),
        in_specs=(
            P(member, None, "band", None),
            P(member, None, "band", None),
            P("band"),
            P("band"),
            P(None, tile, None),
            P(tile, None),
            P(None, tile, None),
            P(tile, None),
        ),
        out_specs=(P(None, tile, None), P(member, None, "band", None)),
        check_vma=False,
    )
```

time: 102 us -> 102 us (level)
  blocking collectives: 0 us -> 25 us
  waiting for transfers between devices: 45.8 us -> 28.6 us
  starting transfers between devices: 42 us -> 35.5 us
  local copies, waits for them, and re-layouts: 5.54 us -> 4.33 us
    all_to_all x0 -> x1, blocking collectives: none -> 18.7 us  [exchange(): parts = lax.all_to_all(flat.reshape(size, 1, CHUNK), axis, 0, 0, tiled=True)]
    ppermute x3 -> x2, waiting for transfers between devices: 17.8 us -> 0.01 us  [both_ways(): lax.ppermute(down_value, axis, down)]
    all_to_all x2, starting transfers between devices: 17.4 us -> 8.48 us  [exchange(): parts = lax.all_to_all(flat.reshape(size, 1, CHUNK), axis, 0, 0, tiled=True)]
    ppermute x0 -> x1, starting transfers between devices: none -> 8.22 us  [shards(): pair = keep + lax.ppermute(send, 'core', [(0, 1), (1, 0)])]
    all_gather x0 -> x1, blocking collectives: none -> 6.32 us  [shards(): lax.all_gather(exchange(shared, 'chip', CHIPS), 'core', axis=0, tiled=True)]
    ppermute x3 -> x2, starting transfers between devices: 19.6 us -> 14.5 us  [both_ways(): lax.ppermute(up_value, axis, up)]
    all_to_all x2, waiting for transfers between devices: 24.9 us -> 22.7 us  [exchange(): parts = lax.all_to_all(flat.reshape(size, 1, CHUNK), axis, 0, 0, tiled=True)]
    ppermute x3 -> x2, waiting for transfers between devices: 3.04 us -> 4.75 us  [both_ways(): lax.ppermute(up_value, axis, up)]
  transfers between devices with their start and end apart: 8 -> 7, of which waited for: 6 -> 4; matrix products, arithmetic and copies ran while one was open for 2% -> 2% of each run, Pallas kernels for 0% -> 0%
where the time goes in v2:
time: 102 us
  starting transfers between devices  35.5 us (35%)
  waiting for transfers between devices  28.6 us (28%)
  blocking collectives  25 us (25%)
  Pallas kernels  6.63 us (6%)
  local copies, waits for them, and re-layouts  4.33 us (4%)
    all_to_all x2, waiting for transfers between devices, exchange(): parts = lax.all_to_all(flat.reshape(size, 1, CHUNK), axis, 0, 0, tiled=True)  22.7 us
    all_to_all x1, blocking collectives, exchange(): parts = lax.all_to_all(flat.reshape(size, 1, CHUNK), axis, 0, 0, tiled=True)  18.7 us
    ppermute x2, starting transfers between devices, both_ways(): lax.ppermute(up_value, axis, up)  14.5 us
    all_to_all x2, starting transfers between devices, exchange(): parts = lax.all_to_all(flat.reshape(size, 1, CHUNK), axis, 0, 0, tiled=True)  8.48 us
    ppermute x1, starting transfers between devices, shards(): pair = keep + lax.ppermute(send, 'core', [(0, 1), (1, 0)])  8.22 us
    pallas_call x5, Pallas kernels, call(): pl.pallas_call(kernel, out_shape=out, in_specs=[spec(x) for x in args], o...  6.63 us
    all_gather x1, blocking collectives, shards(): lax.all_gather(exchange(shared, 'chip', CHIPS), 'core', axis=0, tiled=True)  6.32 us
    ppermute x2, waiting for transfers between devices, both_ways(): lax.ppermute(up_value, axis, up)  4.75 us
  transfers between devices with their start and end apart: 7, of which 4 were waited for; matrix products, arithmetic and copies ran while one was open for 2% of the time, Pallas kernels for 0%

profile of v2, /device:TPU:1, one launch (start us, length us, event | category | flops | bytes accessed | tf_op | source)
XLA Modules:
  0.0 101.9 jit_solution(10353678006741139408)
XLA Ops:
  0.6 0.9 copy-done
  1.6 1.0 copy-done.2
  2.6 11.5 %collective-permute-start = (f32[3,12,512]{2,1,0:T(8,128)S(1)}, f32[3,12,512]{2,1,0:T(8,128)S(1)}, u32[]{:S(2)}, u32[]{:S(2)}) collective-permute-start(f32[3,12,512]{2,1,0:T(8,128)S(1)} %get-tuple-element.14), channel_id=1, source_target_pairs={{0,1},{1,2},{2,3},{3,4},{4,5},{5,6},{6,7},{8,9},{9,10},{10,11},{11... | collective-permute-start | bytes 221192 | tf_op jit(solution)/shard_map/ppermute | solution.py:212
  14.1 1.3 %collective-permute-start.1 = (f32[3,12,512]{2,1,0:T(8,128)S(1)}, f32[3,12,512]{2,1,0:T(8,128)S(1)}, u32[]{:S(2)}, u32[]{:S(2)}) collective-permute-start(f32[3,12,512]{2,1,0:T(8,128)S(1)} %get-tuple-element.15), channel_id=1, source_target_pairs={{1,0},{2,1},{3,2},{4,3},{5,4},{6,5},{7,6},{9,8},{10,9},{11,10},{12... | collective-permute-start | bytes 221192 | tf_op jit(solution)/shard_map/ppermute | solution.py:212
  15.5 0.2 reshape.36
  15.8 0.2 copy.17
  16.0 3.0 %collective-permute-start.3 = (f32[12,48]{1,0:T(8,128)S(1)}, f32[12,48]{1,0:T(8,128)S(1)}, u32[]{:S(2)}, u32[]{:S(2)}) collective-permute-start(f32[12,48]{1,0:T(8,128)S(1)} %get-tuple-element.31), channel_id=1, source_target_pairs={{8,0},{16,8},{24,16},{32,24},{40,32},{48,40},{56,48},{64,56},{72,6... | collective-permute-start | bytes 6920 | tf_op jit(solution)/shard_map/ppermute | solution.py:212
  19.0 3.0 %collective-permute-start.2 = (f32[12,48]{1,0:T(8,128)S(1)}, f32[12,48]{1,0:T(8,128)S(1)}, u32[]{:S(2)}, u32[]{:S(2)}) collective-permute-start(f32[12,48]{1,0:T(8,128)S(1)} %get-tuple-element.30), channel_id=1, source_target_pairs={{0,8},{8,16},{16,24},{24,32},{32,40},{40,48},{48,56},{56,64},{64,7... | collective-permute-start | bytes 6920 | tf_op jit(solution)/shard_map/ppermute | solution.py:212
  22.2 4.7 %collective-permute-done.2 = f32[12,48]{1,0:T(8,128)S(1)} collective-permute-done((f32[12,48]{1,0:T(8,128)S(1)}, f32[12,48]{1,0:T(8,128)S(1)}, u32[]{:S(2)}, u32[]{:S(2)}) %collective-permute-start.2) | collective-permute-done | bytes 2336 | tf_op jit(solution)/shard_map/ppermute | solution.py:212
  27.0 0.9 copy-done.1
  27.9 0.9 shard_map.96
  28.8 8.2 %collective-permute-start.4 = (f32[544,128]{1,0:T(8,128)S(1)}, f32[544,128]{1,0:T(8,128)S(1)}, u32[]{:S(2)}, u32[]{:S(2)}) collective-permute-start(f32[544,128]{1,0:T(8,128)S(1)} %get-tuple-element.19), channel_id=1, source_target_pairs={{0,8},{8,0},{1,9},{9,1},{2,10},{10,2},{3,11},{11,3},{4,12},{12,4},... | collective-permute-start | bytes 835592 | tf_op jit(solution)/shard_map/ppermute | solution.py:245
  37.0 1.2 %collective-permute-done.4 = f32[544,128]{1,0:T(8,128)S(1)} collective-permute-done((f32[544,128]{1,0:T(8,128)S(1)}, f32[544,128]{1,0:T(8,128)S(1)}, u32[]{:S(2)}, u32[]{:S(2)}) %collective-permute-start.4) | collective-permute-done | bytes 278560 | tf_op jit(solution)/shard_map/ppermute | solution.py:245
  38.2 0.7 add.15
  38.9 4.2 %all-to-all-start = ((f32[32,1,2176]{2,1,0:T(1,128)}), f32[32,1,2176]{2,1,0:T(1,128)S(1)}, u32[]{:S(2)}, u32[]{:S(2)}) async-start(f32[32,1,2176]{2,1,0:T(1,128)} %bitcast.11), calls=%async_computation | async-start | bytes 557056 | tf_op jit(solution)/shard_map/all_to_all | solution.py:216
  43.2 12.5 %all-to-all-done = f32[32,1,2176]{2,1,0:T(1,128)S(1)} async-done(((f32[32,1,2176]{2,1,0:T(1,128)}), f32[32,1,2176]{2,1,0:T(1,128)S(1)}, u32[]{:S(2)}, u32[]{:S(2)}) %all-to-all-start) | async-done | bytes 278560 | tf_op jit(solution)/shard_map/all_to_all | solution.py:216
  55.7 3.3 %shard_map.97 = (f32[24,16,48]{2,1,0:T(8,128)S(1)}, f32[17,128]{1,0:T(8,128)S(1)}, f32[136,128]{1,0:T(8,128)S(1)}) custom-call(s32[1]{0:T(128)} %bitcast.band_ref, f32[544,128]{1,0:T(8,128)S(1)} %bitcast.31, f32[26,16,48]{2,1,0:T(8,128)S(1)} %select_maximum_fusion.bg_ref, f32[48,2]{1,0:T(8,128)S(1)} %copy.19.lat_ref, f32[24,256]{1,0:T(8,128)S(1)} %concatenate.7.obs_ref), custom_call_target="tpu_custom_call" | custom-call | tf_op jit(solution)/shard_map/pallas_call | solution.py:195
  59.0 18.7 %all_to_all.15 = f32[8,1,2176]{2,1,0:T(1,128)S(1)} all-to-all(f32[8,1,2176]{2,1,0:T(1,128)S(1)} %bitcast.33), channel_id=1, replica_groups=mesh['chip'=32,'core'=2,'band'=8] {'band'}, dimensions={0} | all-to-all | bytes 139264 | tf_op jit(solution)/shard_map/all_to_all | solution.py:216
  77.7 0.7 shard_map.98
  78.4 4.3 %all-to-all-start.2 = ((f32[32,1,2176]{2,1,0:T(1,128)}), f32[32,1,2176]{2,1,0:T(1,128)S(1)}, u32[]{:S(2)}, u32[]{:S(2)}) async-start(f32[32,1,2176]{2,1,0:T(1,128)} %bitcast.16), calls=%async_computation.2 | async-start | bytes 557056 | tf_op jit(solution)/shard_map/all_to_all | solution.py:216
  82.9 0.9 reshape.44
  83.7 10.2 %all-to-all-done.2 = f32[32,1,2176]{2,1,0:T(1,128)S(1)} async-done(((f32[32,1,2176]{2,1,0:T(1,128)}), f32[32,1,2176]{2,1,0:T(1,128)S(1)}, u32[]{:S(2)}, u32[]{:S(2)}) %all-to-all-start.2) | async-done | bytes 278560 | tf_op jit(solution)/shard_map/all_to_all | solution.py:216
  93.9 6.3 %all_gather.3.g_ref = f32[1088,128]{1,0:T(8,128)S(1)} all-gather(f32[544,128]{1,0:T(8,128)S(1)} %bitcast.34), channel_id=1, replica_groups=mesh['chip'=32,'core'=2,'band'=8] {'core'}, dimensions={0}, use_global_device_ids=true | all-gather | bytes 835584 | tf_op jit(solution)/shard_map/all_gather | solution.py:255
  100.2 1.6 %shard_map.99 = f32[12,16,512]{2,1,0:T(8,128)} custom-call(f32[1088,128]{1,0:T(8,128)S(1)} %all_gather.3.g_ref, bf16[12,16,512]{2,1,0:T(8,128)(2,1)S(1)} %bitcast.28, f32[3,12,512]{2,1,0:T(8,128)S(1)} %collective-permute-done.prev_ref, f32[3,12,512]{2,1,0:T(8,128)S(1)} %collective-permute-done.1.next_ref), custom_call_target="tpu_custom_call" | custom-call | tf_op jit(solution)/shard_map/pallas_call | solution.py:195
  (34 shorter events, 0.6 us)
Async XLA Ops:
  0.6 0.9 copy-start
  1.6 1.0 copy-start.2
  2.6 12.8 %copy-start.4 = (f32[12,1,1152]{2,1,0:T(1,128)S(1)}, f32[12,1,1152]{2,1,0:T(1,128)}, u32[]{:S(2)}) copy-start(f32[12,1,1152]{2,1,0:T(1,128)} %param.12) | copy-start | bytes 165892
  2.6 24.4 %collective-permute-start = (f32[3,12,512]{2,1,0:T(8,128)S(1)}, f32[3,12,512]{2,1,0:T(8,128)S(1)}, u32[]{:S(2)}, u32[]{:S(2)}) collective-permute-start(f32[3,12,512]{2,1,0:T(8,128)S(1)} %get-tuple-element.14), channel_id=1, source_target_pairs={{0,1},{1,2},{2,3},{3,4},{4,5},{5,6},{6,7},{8,9},{9,10},{10,11},{11... | collective-permute-start | bytes 221192 | tf_op jit(solution)/shard_map/ppermute | solution.py:212
  14.1 12.9 %collective-permute-start.1 = (f32[3,12,512]{2,1,0:T(8,128)S(1)}, f32[3,12,512]{2,1,0:T(8,128)S(1)}, u32[]{:S(2)}, u32[]{:S(2)}) collective-permute-start(f32[3,12,512]{2,1,0:T(8,128)S(1)} %get-tuple-element.15), channel_id=1, source_target_pairs={{1,0},{2,1},{3,2},{4,3},{5,4},{6,5},{7,6},{9,8},{10,9},{11,10},{12... | collective-permute-start | bytes 221192 | tf_op jit(solution)/shard_map/ppermute | solution.py:212
  15.7 6.3 %copy-start.6 = (s32[1,256]{1,0:T(1,128)S(1)}, s32[1,256]{1,0:T(1,128)}, u32[]{:S(2)}) copy-start(s32[1,256]{1,0:T(1,128)} %param.13) | copy-start | bytes 3076
  15.8 6.3 %copy-start.9 = (s32[48]{0:T(128)S(1)}, s32[48]{0:T(128)}, u32[]{:S(2)}) copy-start(s32[48]{0:T(128)} %param.10) | copy-start | bytes 580
  15.8 6.3 %copy-start.8 = (f32[48]{0:T(128)S(1)}, f32[48]{0:T(128)}, u32[]{:S(2)}) copy-start(f32[48]{0:T(128)} %param.11) | copy-start | bytes 580
  15.8 6.3 %copy-start.5 = (f32[12,1,256]{2,1,0:T(1,128)S(1)}, f32[12,1,256]{2,1,0:T(1,128)}, u32[]{:S(2)}) copy-start(f32[12,1,256]{2,1,0:T(1,128)} %param.14) | copy-start | bytes 36868
  15.8 6.4 %copy-start.7 = (f32[1,256]{1,0:T(1,128)S(1)}, f32[1,256]{1,0:T(1,128)}, u32[]{:S(2)}) copy-start(f32[1,256]{1,0:T(1,128)} %param.15) | copy-start | bytes 3076
  16.0 11.0 %copy-start.3 = (f32[1,12,16,512]{3,2,1,0:T(8,128)S(1)}, f32[1,12,16,512]{3,2,1,0:T(8,128)}, u32[]{:S(2)}) copy-start(f32[1,12,16,512]{3,2,1,0:T(8,128)} %param.9) | copy-start | bytes 1179652
  16.0 6.2 %collective-permute-start.3 = (f32[12,48]{1,0:T(8,128)S(1)}, f32[12,48]{1,0:T(8,128)S(1)}, u32[]{:S(2)}, u32[]{:S(2)}) collective-permute-start(f32[12,48]{1,0:T(8,128)S(1)} %get-tuple-element.31), channel_id=1, source_target_pairs={{8,0},{16,8},{24,16},{32,24},{40,32},{48,40},{56,48},{64,56},{72,6... | collective-permute-start | bytes 6920 | tf_op jit(solution)/shard_map/ppermute | solution.py:212
  19.0 7.9 %collective-permute-start.2 = (f32[12,48]{1,0:T(8,128)S(1)}, f32[12,48]{1,0:T(8,128)S(1)}, u32[]{:S(2)}, u32[]{:S(2)}) collective-permute-start(f32[12,48]{1,0:T(8,128)S(1)} %get-tuple-element.30), channel_id=1, source_target_pairs={{0,8},{8,16},{16,24},{24,32},{32,40},{40,48},{48,56},{56,64},{64,7... | collective-permute-start | bytes 6920 | tf_op jit(solution)/shard_map/ppermute | solution.py:212
  26.9 0.9 copy-start.1
  28.8 9.4 %collective-permute-start.4 = (f32[544,128]{1,0:T(8,128)S(1)}, f32[544,128]{1,0:T(8,128)S(1)}, u32[]{:S(2)}, u32[]{:S(2)}) collective-permute-start(f32[544,128]{1,0:T(8,128)S(1)} %get-tuple-element.19), channel_id=1, source_target_pairs={{0,8},{8,0},{1,9},{9,1},{2,10},{10,2},{3,11},{11,3},{4,12},{12,4},... | collective-permute-start | bytes 835592 | tf_op jit(solution)/shard_map/ppermute | solution.py:245
  38.9 16.8 %all-to-all-start = ((f32[32,1,2176]{2,1,0:T(1,128)}), f32[32,1,2176]{2,1,0:T(1,128)S(1)}, u32[]{:S(2)}, u32[]{:S(2)}) async-start(f32[32,1,2176]{2,1,0:T(1,128)} %bitcast.11), calls=%async_computation | async-start | bytes 557056 | tf_op jit(solution)/shard_map/all_to_all | solution.py:216
  78.4 15.5 %all-to-all-start.2 = ((f32[32,1,2176]{2,1,0:T(1,128)}), f32[32,1,2176]{2,1,0:T(1,128)S(1)}, u32[]{:S(2)}, u32[]{:S(2)}) async-start(f32[32,1,2176]{2,1,0:T(1,128)} %bitcast.16), calls=%async_computation.2 | async-start | bytes 557056 | tf_op jit(solution)/shard_map/all_to_all | solution.py:216

commit v3 on v2

--- a/solution.py
+++ b/solution.py
@@ -23,6 +23,9 @@
 Q = MAIN + 2 * LEV
 TILES = 17
 CHUNK = TILES * 128
+SIDE = LEV * FINE_R
+SIDE_T = 5
+WIDE = TILES + SIDE_T
 
 advect_rate = 0.25
 highest = lax.Precision.HIGHEST
@@ -38,7 +41,12 @@
     return n // 6, (n % 6) / 6.0
 
 
-def halo_kernel(alpha_ref, ens_ref, last_ref, first_ref):
+def halo_kernel(alpha_hbm, ens_hbm, last_ref, first_ref, alpha_ref, ens_ref, sems):
+    copies = [pltpu.make_async_copy(alpha_hbm, alpha_ref, sems.at[0]), pltpu.make_async_copy(ens_hbm, ens_ref, sems.at[1])]
+    for copy in copies:
+        copy.start()
+    for copy in copies:
+        copy.wait()
     last_ref[0] = alpha_ref[:, ROWS - 2, :]
     last_ref[1] = alpha_ref[:, ROWS - 1, :]
     last_ref[2] = ens_ref[:, ROWS - 1, :].astype(jnp.float32)
@@ -47,7 +55,7 @@
     first_ref[2] = ens_ref[:, 0, :].astype(jnp.float32)
 
 
-def product_kernel(scale, core_ref, alpha_ref, ens_ref, prev_ref, next_ref, keep_ref, send_ref, pad, x_ref, xt_lo, xt_hi, flat):
+def product_kernel(scale, spot_ref, alpha_ref, ens_ref, prev_ref, next_ref, sides_ref, keep_ref, send_ref, pad, x_ref, xt_lo, xt_hi, flat):
     pad[:, 8:24, :] = alpha_ref[...]
     pad[:, 7, :] = prev_ref[1]
     pad[:, 24, :] = next_ref[0]
@@ -69,18 +77,39 @@
             rows = pl.ds(7 + c + BLOCK * core, CHIPS, stride=2 * BLOCK)
             flat[core, :, c * Q : c * Q + 128] = xt_lo[rows, :]
             flat[core, :, c * Q + 128 : (c + 1) * Q] = xt_hi[rows, :][:, : Q - 128]
-    first = core_ref[0] == 0
+    first = spot_ref[0] == 0
     for t in range(TILES):
         even = flat[0, :, 128 * t : 128 * (t + 1)]
         odd = flat[1, :, 128 * t : 128 * (t + 1)]
-        keep_ref[pl.ds(t, CHIPS, stride=TILES), :] = jnp.where(first, even, odd)
-        send_ref[pl.ds(t, CHIPS, stride=TILES), :] = jnp.where(first, odd, even)
-
-
-def tile_kernel(band_ref, g_ref, bg_ref, lat_ref, obs_ref, adv_ref, own_ref, edge_ref, flat):
+        keep_ref[pl.ds(t, CHIPS, stride=WIDE), :] = jnp.where(first, even, odd)
+        send_ref[pl.ds(t, CHIPS, stride=WIDE), :] = jnp.where(first, odd, even)
+    chip = spot_ref[1]
+    other = lax.rem(chip + jnp.where(first, CHIPS - 1, 1), CHIPS)
+    target = lax.broadcasted_iota(jnp.int32, (CHIPS, 128), 0)
+    for t in range(SIDE_T):
+        lanes = slice(128 * t, 128 * (t + 1))
+        left, right = sides_ref[0:1, lanes], sides_ref[1:2, lanes]
+        near = jnp.where(first, right, left)
+        far = jnp.where(first, left, right)
+        side = jnp.where(target == chip, near, jnp.where(target == other, far, 0.0))
+        keep_ref[pl.ds(TILES + t, CHIPS, stride=WIDE), :] = jnp.zeros((CHIPS, 128), jnp.float32)
+        send_ref[pl.ds(TILES + t, CHIPS, stride=WIDE), :] = side
+
+
+def tile_kernel(spot_ref, g_ref, bg_ref, lat_ref, obs_ref, adv_ref, own_ref, up_ref, down_ref, flat, sides):
     for t in range(TILES):
-        part = g_ref[pl.ds(t, CHIPS, stride=TILES), :]
+        part = g_ref[pl.ds(t, CHIPS, stride=WIDE), :]
         flat[0:1, 128 * t : 128 * (t + 1)] = jnp.sum(part, axis=0, keepdims=True)
+    first = spot_ref[0] == 0
+    chip = spot_ref[1]
+    other = lax.rem(chip + jnp.where(first, CHIPS - 1, 1), CHIPS)
+    for s, source in enumerate((chip, other)):
+        for t in range(SIDE_T):
+            sides[s : s + 1, 128 * t : 128 * (t + 1)] = g_ref[pl.ds(source * WIDE + TILES + t, 1), :]
+    none = jnp.zeros((1, FINE_R), jnp.float32)
+    near, far = (jnp.concatenate([sides[s : s + 1, FINE_R * l : FINE_R * (l + 1)] for l in range(LEV)] + [none] * (LPAD - LEV), axis=0)
+                 for s in range(2))
+    ground = [jnp.where(first, far, near)] + [bg_ref[j] for j in range(FINE_C)] + [jnp.where(first, near, far)]
     q = lax.broadcasted_iota(jnp.int32, (1, Q), 1)
     spot = jnp.where(q < MAIN, (q & 15) + 1, jnp.where(q < MAIN + LEV, 0, ROWS + 1))
     level = jnp.where(q < MAIN, q >> 4, jnp.where(q < MAIN + LEV, q - MAIN, q - MAIN - LEV))
@@ -99,7 +128,7 @@
     state = []
     for j in range(-1, FINE_C + 1):
         lo, f = interp(j)
-        state.append((1.0 - f) * lat_rows[lo] + f * lat_rows[lo + 1] + bg_ref[j + 1])
+        state.append((1.0 - f) * lat_rows[lo] + f * lat_rows[lo + 1] + ground[j + 1])
     slope = [0.5 * (state[j + 2] - state[j]) for j in range(FINE_C)]
     model = [state[j + 1] - advect_rate * state[j + 1] * slope[j] for j in range(FINE_C)]
     for j in range(FINE_C):
@@ -135,30 +164,20 @@
                 total[c] = w * adj if total[c] is None else total[c] + w * adj
     coarse = jnp.concatenate(total, axis=0)
 
-    def to_coarse(lat):
+    def to_coarse(lat, ref):
         wide = jnp.dot(coarse, lat, precision=highest, preferred_element_type=jnp.float32).reshape(FRAME, LPAD, Q)
         for c in range(FRAME):
             flat[0:1, c * Q : (c + 1) * Q] = jnp.sum(jnp.where(mask, wide[c], 0.0), axis=0, keepdims=True)
-
-    band = band_ref[0]
-    edge_ref[...] = jnp.zeros_like(edge_ref)
-    for place, off, ok in ((spot + ROWS, 1, band < BANDS - 1), (spot - ROWS, -1, band > 0)):
-        to_coarse(table(place))
-
-        @pl.when(ok)
-        def _():
-            for t in range(TILES):
-                edge_ref[pl.ds((band + off) * TILES + t, 1), :] = flat[0:1, 128 * t : 128 * (t + 1)]
-
-    to_coarse(lat)
-    for t in range(TILES):
-        own_ref[t : t + 1, :] = flat[0:1, 128 * t : 128 * (t + 1)]
-
-
-def share_kernel(own_ref, edge_ref, out_ref):
-    total = own_ref[...]
-    for b in range(BANDS):
-        total = total + edge_ref[TILES * b : TILES * (b + 1), :]
+        for t in range(TILES):
+            ref[t : t + 1, :] = flat[0:1, 128 * t : 128 * (t + 1)]
+
+    to_coarse(lat, own_ref)
+    to_coarse(table(spot + ROWS), up_ref)
+    to_coarse(table(spot - ROWS), down_ref)
+
+
+def share_kernel(own_ref, prev_ref, next_ref, out_ref):
+    total = own_ref[...] + prev_ref[...] + next_ref[...]
     for m in range(CHIPS):
         out_ref[TILES * m : TILES * (m + 1), :] = total
 
@@ -188,16 +207,16 @@
     out_ref[...] = lon_smooth(0.25 * pad[:, 7:23, :] + 0.5 * field + 0.25 * pad[:, 9:25, :])
 
 
-def call(kernel, out, scratch, *args):
+def call(kernel, out, scratch, *args, hbm=False, sems=()):
     def spec(x):
         return pl.BlockSpec(memory_space=pltpu.SMEM if x.dtype == jnp.int32 else pltpu.VMEM)
 
     return pl.pallas_call(
         kernel,
         out_shape=out,
-        in_specs=[spec(x) for x in args],
+        in_specs=[pl.BlockSpec(memory_space=pltpu.HBM) if hbm else spec(x) for x in args],
         out_specs=jax.tree.map(spec, out),
-        scratch_shapes=[pltpu.VMEM(shape, jnp.float32) for shape in scratch],
+        scratch_shapes=[pltpu.VMEM(shape, jnp.float32) for shape in scratch] + list(sems),
         compiler_params=pltpu.CompilerParams(vmem_limit_bytes=40 * 1024 * 1024),
     )(*args)
 
@@ -212,47 +231,48 @@
     return lax.ppermute(up_value, axis, up), lax.ppermute(down_value, axis, down)
 
 
-def exchange(flat, axis, size):
-    parts = lax.all_to_all(flat.reshape(size, 1, CHUNK), axis, 0, 0, tiled=True)
-    return parts.reshape(size * TILES, 128)
+def exchange(flat, tiles):
+    parts = lax.all_to_all(flat.reshape(CHIPS, 1, tiles * 128), "chip", 0, 0, tiled=True)
+    return parts.reshape(CHIPS * tiles, 128)
 
 
 def shards(ensemble, alpha, lat_lower, lat_weight, background, obs_cell, obs_value, obs_precision):
     scale = 1.0 / math.sqrt(2 * CHIPS - 1)
-    core = lax.axis_index("core").astype(jnp.int32).reshape(1)
-    band = lax.axis_index("band").astype(jnp.int32).reshape(1)
-    ens = ensemble[0]
-    alf = alpha[0]
-    last, first = call(halo_kernel, (f32(3, LEV, COLS), f32(3, LEV, COLS)), [], alf, ens)
+    spot = jnp.stack([lax.axis_index("core"), lax.axis_index("chip")]).astype(jnp.int32)
+    last, first, alf, ens = call(
+        halo_kernel,
+        (f32(3, LEV, COLS), f32(3, LEV, COLS), f32(LEV, ROWS, COLS), jax.ShapeDtypeStruct((LEV, ROWS, COLS), jnp.bfloat16)),
+        [], alpha[0], ensemble[0], hbm=True, sems=[pltpu.SemaphoreType.DMA((2,))],
+    )
     before, after = both_ways(last, first, "band", BANDS, False)
 
     grid = background.reshape(LEV, FINE_R, FINE_C).transpose(2, 0, 1)
-    left, right = both_ways(grid[FINE_C - 1], grid[0], ("chip", "core"), 2 * CHIPS, True)
+    sides = jnp.stack([grid[0].reshape(SIDE), grid[FINE_C - 1].reshape(SIDE)])
+    sides = jnp.pad(sides, ((0, 0), (0, SIDE_T * 128 - SIDE)))
+    ground = jnp.pad(grid, ((0, 0), (0, LPAD - LEV), (0, 0)))
     obs = jnp.concatenate(
         [jnp.pad(obs_value[:, 0, :], ((0, LPAD - LEV), (0, 0))), obs_precision, (obs_cell // FINE_C).astype(jnp.float32),
          (obs_cell % FINE_C).astype(jnp.float32), jnp.zeros((24 - LPAD - 3, NOBS), jnp.float32)], axis=0)
     lat = jnp.stack([lat_lower.astype(jnp.float32), lat_weight], axis=1)
-    wide = jnp.concatenate([left[None], grid, right[None]], axis=0)
-    wide = jnp.pad(wide, ((0, 0), (0, LPAD - LEV), (0, 0)))
-    before, after, wide, obs, lat = lax.optimization_barrier((before, after, wide, obs, lat))
+    before, after, ground, sides, obs, lat = lax.optimization_barrier((before, after, ground, sides, obs, lat))
 
     keep, send = call(
         functools.partial(product_kernel, scale),
-        (f32(CHIPS * TILES, 128), f32(CHIPS * TILES, 128)),
+        (f32(CHIPS * WIDE, 128), f32(CHIPS * WIDE, 128)),
         [(LEV, 32, COLS), (256, COLS), (COLS + 16, 128), (COLS + 16, 128), (2, CHIPS, CHUNK)],
-        core, alf, ens, before, after,
+        spot, alf, ens, before, after, sides,
     )
     pair = keep + lax.ppermute(send, "core", [(0, 1), (1, 0)])
-    gathered = exchange(pair, "chip", CHIPS)
-    moved, own, edge = call(
+    gathered = exchange(pair, WIDE)
+    moved, own, up, down = call(
         tile_kernel,
-        (f32(FINE_C, LPAD, FINE_R), f32(TILES, 128), f32(BANDS * TILES, 128)),
-        [(8, CHUNK)],
-        band, gathered, wide, lat, obs,
-    )
-    edge = exchange(edge, "band", BANDS)
-    shared = call(share_kernel, f32(CHIPS * TILES, 128), [], own, edge)
-    everyone = lax.all_gather(exchange(shared, "chip", CHIPS), "core", axis=0, tiled=True)
+        (f32(FINE_C, LPAD, FINE_R), f32(TILES, 128), f32(TILES, 128), f32(TILES, 128)),
+        [(8, CHUNK), (8, SIDE_T * 128)],
+        spot, gathered, ground, lat, obs,
+    )
+    from_prev, from_next = both_ways(up, down, "band", BANDS, False)
+    shared = call(share_kernel, f32(CHIPS * TILES, 128), [], own, from_prev, from_next)
+    everyone = lax.all_gather(exchange(shared, TILES), "core", axis=0, tiled=True)
     gradient = call(
         functools.partial(gradient_kernel, scale),
         f32(LEV, ROWS, COLS),

time: 102 us -> 97.3 us (0.954)
  blocking collectives: 25 us -> 5.88 us
  waiting for transfers between devices: 28.6 us -> 39.6 us
  local copies, waits for them, and re-layouts: 4.33 us -> 6.16 us
    all_to_all x1 -> x0, blocking collectives: 18.7 us -> none  [exchange(): parts = lax.all_to_all(flat.reshape(size, 1, CHUNK), axis, 0, 0, tiled=True)]
    ppermute x2, waiting for transfers between devices: 0.01 us -> 14.6 us  [both_ways(): lax.ppermute(down_value, axis, down)]
    all_to_all x2, starting transfers between devices: 8.48 us -> 14.3 us  [exchange(): lax.all_to_all(flat.reshape(CHIPS, 1, tiles * 128), 'chip', 0, 0, tiled=T...]
    ppermute x1, starting transfers between devices: 8.22 us -> 2.51 us  [shards(): pair = keep + lax.ppermute(send, 'core', [(0, 1), (1, 0)])]
    ppermute x2, waiting for transfers between devices: 4.75 us -> 0.01 us  [both_ways(): lax.ppermute(up_value, axis, up)]
    ppermute x2, starting transfers between devices: 14.5 us -> 16.3 us  [both_ways(): lax.ppermute(up_value, axis, up)]
    ppermute x2, starting transfers between devices: 4.29 us -> 2.58 us  [both_ways(): lax.ppermute(down_value, axis, down)]
    unnamed x21 -> x17, local copies, waits for them, and re-layouts: 2.83 us -> 4.48 us
  transfers between devices with their start and end apart: 7 -> 7, of which waited for: 4 -> 5; matrix products, arithmetic and copies ran while one was open for 2% -> 2% of each run, Pallas kernels for 0% -> 0%
where the time goes in v3:
time: 97.3 us; the launch traced here: 96.8 us
  waiting for transfers between devices  39.6 us (41%)
  starting transfers between devices  35.7 us (37%)
  Pallas kernels  7.53 us (8%)
  local copies, waits for them, and re-layouts  6.16 us (6%)
  blocking collectives  5.88 us (6%)
  other arithmetic  1.03 us (1%)
    all_to_all x2, waiting for transfers between devices, exchange(): lax.all_to_all(flat.reshape(CHIPS, 1, tiles * 128), 'chip', 0, 0, tiled=T...  23.7 us
    ppermute x2, starting transfers between devices, both_ways(): lax.ppermute(up_value, axis, up)  16.3 us
    ppermute x2, waiting for transfers between devices, both_ways(): lax.ppermute(down_value, axis, down)  14.6 us
    all_to_all x2, starting transfers between devices, exchange(): lax.all_to_all(flat.reshape(CHIPS, 1, tiles * 128), 'chip', 0, 0, tiled=T...  14.3 us
    pallas_call x5, Pallas kernels, call(): pl.pallas_call(kernel, out_shape=out, in_specs=[pl.BlockSpec(memory_space...  7.53 us
    all_gather x1, blocking collectives, shards(): lax.all_gather(exchange(shared, TILES), 'core', axis=0, tiled=True)  5.88 us
    unnamed x17, local copies, waits for them, and re-layouts  4.48 us
    ppermute x2, starting transfers between devices, both_ways(): lax.ppermute(down_value, axis, down)  2.58 us
  transfers between devices with their start and end apart: 7, of which 5 were waited for; matrix products, arithmetic and copies ran while one was open for 2% of the time, Pallas kernels for 0%

profile of v3, /device:TPU:1, one launch (start us, length us, event | category | flops | bytes accessed | tf_op | source)
XLA Modules:
  0.0 96.8 jit_solution(14157453832945141912)
XLA Ops:
  0.6 1.0 %copy-done = f32[1,12,16,512]{3,2,1,0:T(8,128)S(1)} copy-done((f32[1,12,16,512]{3,2,1,0:T(8,128)S(1)}, f32[1,12,16,512]{3,2,1,0:T(8,128)}, u32[]{:S(2)}) %copy-start) | copy-done | bytes 393240
  1.6 0.9 copy-done.1
  3.1 11.5 %collective-permute-start = (f32[3,12,512]{2,1,0:T(8,128)S(1)}, f32[3,12,512]{2,1,0:T(8,128)S(1)}, u32[]{:S(2)}, u32[]{:S(2)}) collective-permute-start(f32[3,12,512]{2,1,0:T(8,128)S(1)} %get-tuple-element.20), channel_id=1, source_target_pairs={{0,1},{1,2},{2,3},{3,4},{4,5},{5,6},{6,7},{8,9},{9,10},{10,11},{11... | collective-permute-start | bytes 221192 | tf_op jit(solution)/shard_map/ppermute | solution.py:231
  14.5 1.3 %collective-permute-start.1 = (f32[3,12,512]{2,1,0:T(8,128)S(1)}, f32[3,12,512]{2,1,0:T(8,128)S(1)}, u32[]{:S(2)}, u32[]{:S(2)}) collective-permute-start(f32[3,12,512]{2,1,0:T(8,128)S(1)} %get-tuple-element.21), channel_id=1, source_target_pairs={{1,0},{2,1},{3,2},{4,3},{5,4},{6,5},{7,6},{9,8},{10,9},{11,10},{12... | collective-permute-start | bytes 221192 | tf_op jit(solution)/shard_map/ppermute | solution.py:231
  17.3 0.6 copy-done.7
  17.9 0.6 copy-done.6
  18.6 0.7 copy-done.5
  19.4 7.6 %collective-permute-done.1.next_ref = f32[3,12,512]{2,1,0:T(8,128)S(1)} collective-permute-done((f32[3,12,512]{2,1,0:T(8,128)S(1)}, f32[3,12,512]{2,1,0:T(8,128)S(1)}, u32[]{:S(2)}, u32[]{:S(2)}) %collective-permute-start.1) | collective-permute-done | bytes 73760 | tf_op jit(solution)/shard_map/ppermute | solution.py:231
  26.9 1.5 %shard_map.96 = (f32[704,128]{1,0:T(8,128)S(1)}, f32[704,128]{1,0:T(8,128)S(1)}) custom-call(s32[2]{0:T(128)S(1)} %pad_add_fusion.spot_ref, f32[12,16,512]{2,1,0:T(8,128)S(1)} %get-tuple-element.18.alpha_ref, bf16[12,16,512]{2,1,0:T(8,128)(2,1)S(1)} %get-tuple-element.19.ens_ref, f32[3,12,512]{2,1,0:T(8,128)S(1)} %collective-permute-done.prev_ref, ...), custom_call_target="tpu_custom_call" | custom-call | tf_op jit(solution)/shard_map/pallas_call | solution.py:214
  28.4 2.5 %collective-permute-start.2 = (f32[704,128]{1,0:T(8,128)S(1)}, f32[704,128]{1,0:T(8,128)S(1)}, u32[]{:S(2)}, u32[]{:S(2)}) collective-permute-start(f32[704,128]{1,0:T(8,128)S(1)} %get-tuple-element.26), channel_id=1, source_target_pairs={{0,8},{8,0},{1,9},{9,1},{2,10},{10,2},{3,11},{11,3},{4,12},{12,4},... | collective-permute-start | bytes 1081352 | tf_op jit(solution)/shard_map/ppermute | solution.py:265
  30.9 1.3 %collective-permute-done.2 = f32[704,128]{1,0:T(8,128)S(1)} collective-permute-done((f32[704,128]{1,0:T(8,128)S(1)}, f32[704,128]{1,0:T(8,128)S(1)}, u32[]{:S(2)}, u32[]{:S(2)}) %collective-permute-start.2) | collective-permute-done | bytes 360480 | tf_op jit(solution)/shard_map/ppermute | solution.py:265
  32.2 0.8 add.17
  33.0 9.4 %all-to-all-start = ((f32[32,1,2816]{2,1,0:T(1,128)}), f32[32,1,2816]{2,1,0:T(1,128)S(1)}, u32[]{:S(2)}, u32[]{:S(2)}) async-start(f32[32,1,2816]{2,1,0:T(1,128)} %bitcast.7), calls=%async_computation | async-start | bytes 720896 | tf_op jit(solution)/shard_map/all_to_all | solution.py:235
  42.5 13.6 %all-to-all-done = f32[32,1,2816]{2,1,0:T(1,128)S(1)} async-done(((f32[32,1,2816]{2,1,0:T(1,128)}), f32[32,1,2816]{2,1,0:T(1,128)S(1)}, u32[]{:S(2)}, u32[]{:S(2)}) %all-to-all-start) | async-done | bytes 360480 | tf_op jit(solution)/shard_map/all_to_all | solution.py:235
  56.1 3.2 %shard_map.97 = (f32[24,16,48]{2,1,0:T(8,128)S(1)}, f32[17,128]{1,0:T(8,128)S(1)}, f32[17,128]{1,0:T(8,128)S(1)}, f32[17,128]{1,0:T(8,128)S(1)}) custom-call(s32[2]{0:T(128)S(1)} %pad_add_fusion.spot_ref, f32[704,128]{1,0:T(8,128)S(1)} %bitcast.18, f32[24,16,48]{2,1,0:T(8,128)S(1)} %pad.12.bg_ref, f32[48,2]{1,0:T(8,128)S(1)} %copy.19.lat_ref, ...), custom_call_target="tpu_custom_call" | custom-call | tf_op jit(solution)/shard_map/pallas_call | solution.py:214
  59.3 4.8 %collective-permute-start.3 = (f32[17,128]{1,0:T(8,128)S(1)}, f32[17,128]{1,0:T(8,128)S(1)}, u32[]{:S(2)}, u32[]{:S(2)}) collective-permute-start(f32[17,128]{1,0:T(8,128)S(1)} %get-tuple-element.32), channel_id=1, source_target_pairs={{0,1},{1,2},{2,3},{3,4},{4,5},{5,6},{6,7},{8,9},{9,10},{10,11},{11... | collective-permute-start | bytes 26120 | tf_op jit(solution)/shard_map/ppermute | solution.py:231
  64.2 1.3 %collective-permute-start.4 = (f32[17,128]{1,0:T(8,128)S(1)}, f32[17,128]{1,0:T(8,128)S(1)}, u32[]{:S(2)}, u32[]{:S(2)}) collective-permute-start(f32[17,128]{1,0:T(8,128)S(1)} %get-tuple-element.33), channel_id=1, source_target_pairs={{1,0},{2,1},{3,2},{4,3},{5,4},{6,5},{7,6},{9,8},{10,9},{11,10},{12... | collective-permute-start | bytes 26120 | tf_op jit(solution)/shard_map/ppermute | solution.py:231
  65.5 7.0 %collective-permute-done.4.next_ref = f32[17,128]{1,0:T(8,128)S(1)} collective-permute-done((f32[17,128]{1,0:T(8,128)S(1)}, f32[17,128]{1,0:T(8,128)S(1)}, u32[]{:S(2)}, u32[]{:S(2)}) %collective-permute-start.4) | collective-permute-done | bytes 8736 | tf_op jit(solution)/shard_map/ppermute | solution.py:231
  72.5 0.7 shard_map.98
  73.2 4.9 %all-to-all-start.1 = ((f32[32,1,2176]{2,1,0:T(1,128)}), f32[32,1,2176]{2,1,0:T(1,128)S(1)}, u32[]{:S(2)}, u32[]{:S(2)}) async-start(f32[32,1,2176]{2,1,0:T(1,128)} %bitcast.10), calls=%async_computation.1 | async-start | bytes 557056 | tf_op jit(solution)/shard_map/all_to_all | solution.py:235
  78.3 0.9 reshape.28
  79.2 10.1 %all-to-all-done.1 = f32[32,1,2176]{2,1,0:T(1,128)S(1)} async-done(((f32[32,1,2176]{2,1,0:T(1,128)}), f32[32,1,2176]{2,1,0:T(1,128)S(1)}, u32[]{:S(2)}, u32[]{:S(2)}) %all-to-all-start.1) | async-done | bytes 278560 | tf_op jit(solution)/shard_map/all_to_all | solution.py:235
  89.3 5.9 %all_gather.3.g_ref = f32[1088,128]{1,0:T(8,128)S(1)} all-gather(f32[544,128]{1,0:T(8,128)S(1)} %bitcast.21), channel_id=1, replica_groups=mesh['chip'=32,'core'=2,'band'=8] {'core'}, dimensions={0}, use_global_device_ids=true | all-gather | bytes 835584 | tf_op jit(solution)/shard_map/all_gather | solution.py:275
  95.2 1.6 %shard_map.99 = f32[12,16,512]{2,1,0:T(8,128)} custom-call(f32[1088,128]{1,0:T(8,128)S(1)} %all_gather.3.g_ref, bf16[12,16,512]{2,1,0:T(8,128)(2,1)S(1)} %get-tuple-element.19.ens_ref, f32[3,12,512]{2,1,0:T(8,128)S(1)} %collective-permute-done.prev_ref, f32[3,12,512]{2,1,0:T(8,128)S(1)} %collective-permute-done.1.next_ref), custom_call_target="tpu_custom_call" | custom-call | tf_op jit(solution)/shard_map/pallas_call | solution.py:214
  (33 shorter events, 2.2 us)
Async XLA Ops:
  0.6 1.0 %copy-start = (f32[1,12,16,512]{3,2,1,0:T(8,128)S(1)}, f32[1,12,16,512]{3,2,1,0:T(8,128)}, u32[]{:S(2)}) copy-start(f32[1,12,16,512]{3,2,1,0:T(8,128)} %param.9) | copy-start | bytes 1179652
  1.6 0.9 copy-start.1
  2.6 13.3 %copy-start.2 = (f32[12,1,1152]{2,1,0:T(1,128)S(1)}, f32[12,1,1152]{2,1,0:T(1,128)}, u32[]{:S(2)}) copy-start(f32[12,1,1152]{2,1,0:T(1,128)} %param.12) | copy-start | bytes 165892
  3.1 16.3 %collective-permute-start = (f32[3,12,512]{2,1,0:T(8,128)S(1)}, f32[3,12,512]{2,1,0:T(8,128)S(1)}, u32[]{:S(2)}, u32[]{:S(2)}) collective-permute-start(f32[3,12,512]{2,1,0:T(8,128)S(1)} %get-tuple-element.20), channel_id=1, source_target_pairs={{0,1},{1,2},{2,3},{3,4},{4,5},{5,6},{6,7},{8,9},{9,10},{10,11},{11... | collective-permute-start | bytes 221192 | tf_op jit(solution)/shard_map/ppermute | solution.py:231
  14.5 12.4 %collective-permute-start.1 = (f32[3,12,512]{2,1,0:T(8,128)S(1)}, f32[3,12,512]{2,1,0:T(8,128)S(1)}, u32[]{:S(2)}, u32[]{:S(2)}) collective-permute-start(f32[3,12,512]{2,1,0:T(8,128)S(1)} %get-tuple-element.21), channel_id=1, source_target_pairs={{1,0},{2,1},{3,2},{4,3},{5,4},{6,5},{7,6},{9,8},{10,9},{11,10},{12... | collective-permute-start | bytes 221192 | tf_op jit(solution)/shard_map/ppermute | solution.py:231
  16.4 0.8 copy-start.3
  16.5 0.7 copy-start.4
  17.2 0.7 copy-start.7
  17.9 0.7 copy-start.6
  18.6 0.7 copy-start.5
  28.4 3.8 %collective-permute-start.2 = (f32[704,128]{1,0:T(8,128)S(1)}, f32[704,128]{1,0:T(8,128)S(1)}, u32[]{:S(2)}, u32[]{:S(2)}) collective-permute-start(f32[704,128]{1,0:T(8,128)S(1)} %get-tuple-element.26), channel_id=1, source_target_pairs={{0,8},{8,0},{1,9},{9,1},{2,10},{10,2},{3,11},{11,3},{4,12},{12,4},... | collective-permute-start | bytes 1081352 | tf_op jit(solution)/shard_map/ppermute | solution.py:265
  33.0 23.1 %all-to-all-start = ((f32[32,1,2816]{2,1,0:T(1,128)}), f32[32,1,2816]{2,1,0:T(1,128)S(1)}, u32[]{:S(2)}, u32[]{:S(2)}) async-start(f32[32,1,2816]{2,1,0:T(1,128)} %bitcast.7), calls=%async_computation | async-start | bytes 720896 | tf_op jit(solution)/shard_map/all_to_all | solution.py:235
  59.3 6.2 %collective-permute-start.3 = (f32[17,128]{1,0:T(8,128)S(1)}, f32[17,128]{1,0:T(8,128)S(1)}, u32[]{:S(2)}, u32[]{:S(2)}) collective-permute-start(f32[17,128]{1,0:T(8,128)S(1)} %get-tuple-element.32), channel_id=1, source_target_pairs={{0,1},{1,2},{2,3},{3,4},{4,5},{5,6},{6,7},{8,9},{9,10},{10,11},{11... | collective-permute-start | bytes 26120 | tf_op jit(solution)/shard_map/ppermute | solution.py:231
  64.2 8.3 %collective-permute-start.4 = (f32[17,128]{1,0:T(8,128)S(1)}, f32[17,128]{1,0:T(8,128)S(1)}, u32[]{:S(2)}, u32[]{:S(2)}) collective-permute-start(f32[17,128]{1,0:T(8,128)S(1)} %get-tuple-element.33), channel_id=1, source_target_pairs={{1,0},{2,1},{3,2},{4,3},{5,4},{6,5},{7,6},{9,8},{10,9},{11,10},{12... | collective-permute-start | bytes 26120 | tf_op jit(solution)/shard_map/ppermute | solution.py:231
  73.2 16.0 %all-to-all-start.1 = ((f32[32,1,2176]{2,1,0:T(1,128)}), f32[32,1,2176]{2,1,0:T(1,128)S(1)}, u32[]{:S(2)}, u32[]{:S(2)}) async-start(f32[32,1,2176]{2,1,0:T(1,128)} %bitcast.10), calls=%async_computation.1 | async-start | bytes 557056 | tf_op jit(solution)/shard_map/all_to_all | solution.py:235

commit v4 on v3

--- a/solution.py
+++ b/solution.py
@@ -23,9 +23,7 @@
 Q = MAIN + 2 * LEV
 TILES = 17
 CHUNK = TILES * 128
-SIDE = LEV * FINE_R
-SIDE_T = 5
-WIDE = TILES + SIDE_T
+PAIR = CHIPS * TILES
 
 advect_rate = 0.25
 highest = lax.Precision.HIGHEST
@@ -81,34 +79,31 @@
     for t in range(TILES):
         even = flat[0, :, 128 * t : 128 * (t + 1)]
         odd = flat[1, :, 128 * t : 128 * (t + 1)]
-        keep_ref[pl.ds(t, CHIPS, stride=WIDE), :] = jnp.where(first, even, odd)
-        send_ref[pl.ds(t, CHIPS, stride=WIDE), :] = jnp.where(first, odd, even)
-    chip = spot_ref[1]
-    other = lax.rem(chip + jnp.where(first, CHIPS - 1, 1), CHIPS)
-    target = lax.broadcasted_iota(jnp.int32, (CHIPS, 128), 0)
-    for t in range(SIDE_T):
-        lanes = slice(128 * t, 128 * (t + 1))
-        left, right = sides_ref[0:1, lanes], sides_ref[1:2, lanes]
-        near = jnp.where(first, right, left)
-        far = jnp.where(first, left, right)
-        side = jnp.where(target == chip, near, jnp.where(target == other, far, 0.0))
-        keep_ref[pl.ds(TILES + t, CHIPS, stride=WIDE), :] = jnp.zeros((CHIPS, 128), jnp.float32)
-        send_ref[pl.ds(TILES + t, CHIPS, stride=WIDE), :] = side
-
-
-def tile_kernel(spot_ref, g_ref, bg_ref, lat_ref, obs_ref, adv_ref, own_ref, up_ref, down_ref, flat, sides):
+        keep_ref[pl.ds(t, CHIPS, stride=TILES), :] = jnp.where(first, even, odd)
+        send_ref[pl.ds(t, CHIPS, stride=TILES), :] = jnp.where(first, odd, even)
+    send_ref[PAIR:, :] = sides_ref[...]
+
+
+def pair_kernel(keep_ref, got_ref, out_ref):
+    out_ref[...] = keep_ref[...] + got_ref[:PAIR, :]
+
+
+def split_dot(x, pick, dim):
+    total = None
+    for _ in range(3):
+        part = x.astype(jnp.bfloat16)
+        x = x - part.astype(jnp.float32)
+        got = lax.dot_general(part, pick, (((1,), (dim,)), ((), ())), preferred_element_type=jnp.float32)
+        total = got if total is None else total + got
+    return total
+
+
+def tile_kernel(spot_ref, g_ref, near_ref, far_ref, bg_ref, lat_ref, obs_ref, adv_ref, own_ref, edge_ref, flat):
     for t in range(TILES):
-        part = g_ref[pl.ds(t, CHIPS, stride=WIDE), :]
+        part = g_ref[pl.ds(t, CHIPS, stride=TILES), :]
         flat[0:1, 128 * t : 128 * (t + 1)] = jnp.sum(part, axis=0, keepdims=True)
     first = spot_ref[0] == 0
-    chip = spot_ref[1]
-    other = lax.rem(chip + jnp.where(first, CHIPS - 1, 1), CHIPS)
-    for s, source in enumerate((chip, other)):
-        for t in range(SIDE_T):
-            sides[s : s + 1, 128 * t : 128 * (t + 1)] = g_ref[pl.ds(source * WIDE + TILES + t, 1), :]
-    none = jnp.zeros((1, FINE_R), jnp.float32)
-    near, far = (jnp.concatenate([sides[s : s + 1, FINE_R * l : FINE_R * (l + 1)] for l in range(LEV)] + [none] * (LPAD - LEV), axis=0)
-                 for s in range(2))
+    near, far = near_ref[...], far_ref[...]
     ground = [jnp.where(first, far, near)] + [bg_ref[j] for j in range(FINE_C)] + [jnp.where(first, near, far)]
     q = lax.broadcasted_iota(jnp.int32, (1, Q), 1)
     spot = jnp.where(q < MAIN, (q & 15) + 1, jnp.where(q < MAIN + LEV, 0, ROWS + 1))
@@ -138,15 +133,13 @@
     row = obs_ref[LPAD + 1 : LPAD + 2, :]
     col = obs_ref[LPAD + 2 : LPAD + 3, :]
     fine_row = lax.broadcasted_iota(jnp.int32, (FINE_R, NOBS), 0).astype(jnp.float32)
-    pick_row = jnp.where(fine_row == row, 1.0, 0.0)
+    pick_row = jnp.where(fine_row == row, 1.0, 0.0).astype(jnp.bfloat16)
     pick_col = [jnp.where(col == float(j), 1.0, 0.0) for j in range(FINE_C)]
-    seen = jnp.dot(jnp.concatenate(model, axis=0), pick_row, precision=highest,
-                   preferred_element_type=jnp.float32).reshape(FINE_C, LPAD, NOBS)
+    seen = split_dot(jnp.concatenate(model, axis=0), pick_row, 0).reshape(FINE_C, LPAD, NOBS)
     observed = sum(pick_col[j] * seen[j] for j in range(FINE_C))
     weighted = precision * (observed - value)
     back = jnp.concatenate([pick_col[j] * weighted for j in range(FINE_C)], axis=0)
-    cot = lax.dot_general(back, pick_row, (((1,), (1,)), ((), ())), precision=highest,
-                          preferred_element_type=jnp.float32).reshape(FINE_C, LPAD, FINE_R)
+    cot = split_dot(back, pick_row, 1).reshape(FINE_C, LPAD, FINE_R)
     half_rate = 0.5 * advect_rate
     flux = [half_rate * state[j + 1] * cot[j] for j in range(FINE_C)]
     total = [None] * FRAME
@@ -172,12 +165,17 @@
             ref[t : t + 1, :] = flat[0:1, 128 * t : 128 * (t + 1)]
 
     to_coarse(lat, own_ref)
-    to_coarse(table(spot + ROWS), up_ref)
-    to_coarse(table(spot - ROWS), down_ref)
+    to_coarse(table(jnp.where(spot < 2, spot + ROWS, spot - ROWS)), edge_ref)
 
 
 def share_kernel(own_ref, prev_ref, next_ref, out_ref):
-    total = own_ref[...] + prev_ref[...] + next_ref[...]
+    shape = (TILES, 128)
+    q = lax.rem(lax.broadcasted_iota(jnp.int32, shape, 0) * 128 + lax.broadcasted_iota(jnp.int32, shape, 1), Q)
+    row = q & 15
+    inner = q < MAIN
+    from_prev = (inner & (row == 0)) | ((q >= MAIN) & (q < MAIN + LEV))
+    from_next = (inner & (row == ROWS - 1)) | (q >= MAIN + LEV)
+    total = own_ref[...] + jnp.where(from_prev, prev_ref[...], 0.0) + jnp.where(from_next, next_ref[...], 0.0)
     for m in range(CHIPS):
         out_ref[TILES * m : TILES * (m + 1), :] = total
 
@@ -242,13 +240,18 @@
     last, first, alf, ens = call(
         halo_kernel,
         (f32(3, LEV, COLS), f32(3, LEV, COLS), f32(LEV, ROWS, COLS), jax.ShapeDtypeStruct((LEV, ROWS, COLS), jnp.bfloat16)),
-        [], alpha[0], ensemble[0], hbm=True, sems=[pltpu.SemaphoreType.DMA((2,))],
+        [], pltpu.with_memory_space_constraint(alpha[0], pltpu.HBM), pltpu.with_memory_space_constraint(ensemble[0], pltpu.HBM), hbm=True, sems=[pltpu.SemaphoreType.DMA((2,))],
     )
     before, after = both_ways(last, first, "band", BANDS, False)
 
     grid = background.reshape(LEV, FINE_R, FINE_C).transpose(2, 0, 1)
-    sides = jnp.stack([grid[0].reshape(SIDE), grid[FINE_C - 1].reshape(SIDE)])
-    sides = jnp.pad(sides, ((0, 0), (0, SIDE_T * 128 - SIDE)))
+    first_core = lax.axis_index("core") == 0
+    sides = jnp.where(first_core, grid[FINE_C - 1], grid[0])
+    sides = jnp.pad(sides, ((0, LPAD - LEV), (0, 128 - FINE_R)))
+    far = jnp.where(first_core, grid[0], grid[FINE_C - 1])
+    size = 2 * CHIPS
+    far = lax.ppermute(far, ("chip", "core"), [(i, (i + (1 if i % 2 else size - 1)) % size) for i in range(size)])
+    far = jnp.pad(far, ((0, LPAD - LEV), (0, 0)))
     ground = jnp.pad(grid, ((0, 0), (0, LPAD - LEV), (0, 0)))
     obs = jnp.concatenate(
         [jnp.pad(obs_value[:, 0, :], ((0, LPAD - LEV), (0, 0))), obs_precision, (obs_cell // FINE_C).astype(jnp.float32),
@@ -258,19 +261,19 @@
 
     keep, send = call(
         functools.partial(product_kernel, scale),
-        (f32(CHIPS * WIDE, 128), f32(CHIPS * WIDE, 128)),
+        (f32(PAIR, 128), f32(PAIR + LPAD, 128)),
         [(LEV, 32, COLS), (256, COLS), (COLS + 16, 128), (COLS + 16, 128), (2, CHIPS, CHUNK)],
         spot, alf, ens, before, after, sides,
     )
-    pair = keep + lax.ppermute(send, "core", [(0, 1), (1, 0)])
-    gathered = exchange(pair, WIDE)
-    moved, own, up, down = call(
+    got = lax.ppermute(send, "core", [(0, 1), (1, 0)])
+    gathered = exchange(call(pair_kernel, f32(PAIR, 128), [], keep, got), TILES)
+    moved, own, edge = call(
         tile_kernel,
-        (f32(FINE_C, LPAD, FINE_R), f32(TILES, 128), f32(TILES, 128), f32(TILES, 128)),
-        [(8, CHUNK), (8, SIDE_T * 128)],
-        spot, gathered, ground, lat, obs,
-    )
-    from_prev, from_next = both_ways(up, down, "band", BANDS, False)
+        (f32(FINE_C, LPAD, FINE_R), f32(TILES, 128), f32(TILES, 128)),
+        [(8, CHUNK)],
+        spot, gathered, got[PAIR:, :FINE_R], far, ground, lat, obs,
+    )
+    from_prev, from_next = both_ways(edge, edge, "band", BANDS, False)
     shared = call(share_kernel, f32(CHIPS * TILES, 128), [], own, from_prev, from_next)
     everyone = lax.all_gather(exchange(shared, TILES), "core", axis=0, tiled=True)
     gradient = call(

time: 97.3 us -> 94.3 us (0.969)
  waiting for transfers between devices: 39.6 us -> 34.5 us
  starting transfers between devices: 35.7 us -> 39.5 us
  local copies, waits for them, and re-layouts: 6.16 us -> 4.17 us
    all_to_all x2, waiting for transfers between devices: 23.7 us -> 16.7 us  [exchange(): lax.all_to_all(flat.reshape(CHIPS, 1, tiles * 128), 'chip', 0, 0, tiled=T...]
    ppermute x1 -> x2, starting transfers between devices: 2.51 us -> 6.46 us  [the longest x1 3.96 us: shards(): lax.ppermute(far, ('chip', 'core'), [(i, (i + (1 if i % 2 else size - 1))...]
    ppermute x1 -> x2, waiting for transfers between devices: 1.28 us -> 3.15 us  [the longest x1 1.98 us: shards(): lax.ppermute(far, ('chip', 'core'), [(i, (i + (1 if i % 2 else size - 1))...]
    unnamed x17 -> x13, local copies, waits for them, and re-layouts: 4.48 us -> 2.63 us
    pallas_call x5 -> x6, Pallas kernels: 7.53 us -> 8.2 us  [call(): pl.pallas_call(kernel, out_shape=out, in_specs=[pl.BlockSpec(memory_space...]
  transfers between devices with their start and end apart: 7 -> 8, of which waited for: 5 -> 6; matrix products, arithmetic and copies ran while one was open for 2% -> 2% of each run, Pallas kernels for 0% -> 0%
where the time goes in v4:
time: 94.3 us; the launch traced here: 93.7 us
  starting transfers between devices  39.5 us (42%)
  waiting for transfers between devices  34.5 us (37%)
  Pallas kernels  8.2 us (9%)
  blocking collectives  6.29 us (7%)
  local copies, waits for them, and re-layouts  4.17 us (4%)
    all_to_all x2, waiting for transfers between devices, exchange(): lax.all_to_all(flat.reshape(CHIPS, 1, tiles * 128), 'chip', 0, 0, tiled=T...  16.7 us
    ppermute x2, starting transfers between devices, both_ways(): lax.ppermute(up_value, axis, up)  16.3 us
    ppermute x2, waiting for transfers between devices, both_ways(): lax.ppermute(down_value, axis, down)  14.7 us
    all_to_all x2, starting transfers between devices, exchange(): lax.all_to_all(flat.reshape(CHIPS, 1, tiles * 128), 'chip', 0, 0, tiled=T...  14.1 us
    pallas_call x6, Pallas kernels, call(): pl.pallas_call(kernel, out_shape=out, in_specs=[pl.BlockSpec(memory_space...  8.2 us
    all_gather x1, blocking collectives, shards(): lax.all_gather(exchange(shared, TILES), 'core', axis=0, tiled=True)  6.29 us
    ppermute x1, starting transfers between devices, shards(): lax.ppermute(far, ('chip', 'core'), [(i, (i + (1 if i % 2 else size - 1))...  3.96 us
    unnamed x13, local copies, waits for them, and re-layouts  2.63 us
  transfers between devices with their start and end apart: 8, of which 6 were waited for; matrix products, arithmetic and copies ran while one was open for 2% of the time, Pallas kernels for 0%

profile of v4, /device:TPU:1, one launch (start us, length us, event | category | flops | bytes accessed | tf_op | source)
XLA Modules:
  0.0 93.7 jit_solution(8782343866450229283)
XLA Ops:
  0.6 1.1 %shard_map.95 = (f32[3,12,512]{2,1,0:T(8,128)S(1)}, f32[3,12,512]{2,1,0:T(8,128)S(1)}, f32[12,16,512]{2,1,0:T(8,128)S(1)}, bf16[12,16,512]{2,1,0:T(8,128)(2,1)S(1)}) custom-call(f32[12,16,512]{2,1,0:T(8,128)} %bitcast.26, bf16[12,16,512]{2,1,0:T(8,128)(2,1)} %bitcast.28), custom_call_target="tpu_custom_call" | custom-call | tf_op jit(solution)/shard_map/pallas_call | solution.py:212
  1.8 11.5 %collective-permute-start = (f32[3,12,512]{2,1,0:T(8,128)S(1)}, f32[3,12,512]{2,1,0:T(8,128)S(1)}, u32[]{:S(2)}, u32[]{:S(2)}) collective-permute-start(f32[3,12,512]{2,1,0:T(8,128)S(1)} %get-tuple-element.19), channel_id=1, source_target_pairs={{0,1},{1,2},{2,3},{3,4},{4,5},{5,6},{6,7},{8,9},{9,10},{10,11},{11... | collective-permute-start | bytes 221192 | tf_op jit(solution)/shard_map/ppermute | solution.py:229
  13.3 1.3 %collective-permute-start.1 = (f32[3,12,512]{2,1,0:T(8,128)S(1)}, f32[3,12,512]{2,1,0:T(8,128)S(1)}, u32[]{:S(2)}, u32[]{:S(2)}) collective-permute-start(f32[3,12,512]{2,1,0:T(8,128)S(1)} %get-tuple-element.20), channel_id=1, source_target_pairs={{1,0},{2,1},{3,2},{4,3},{5,4},{6,5},{7,6},{9,8},{10,9},{11,10},{12... | collective-permute-start | bytes 221192 | tf_op jit(solution)/shard_map/ppermute | solution.py:229
  15.2 0.7 copy-done.2
  17.2 0.7 copy-done.3
  18.0 7.7 %collective-permute-done.1.next_ref = f32[3,12,512]{2,1,0:T(8,128)S(1)} collective-permute-done((f32[3,12,512]{2,1,0:T(8,128)S(1)}, f32[3,12,512]{2,1,0:T(8,128)S(1)}, u32[]{:S(2)}, u32[]{:S(2)}) %collective-permute-start.1) | collective-permute-done | bytes 73760 | tf_op jit(solution)/shard_map/ppermute | solution.py:229
  25.6 1.5 %shard_map.96 = (f32[544,128]{1,0:T(8,128)S(1)}, f32[560,128]{1,0:T(8,128)S(1)}) custom-call(s32[2]{0:T(128)S(1)} %pad_add_fusion.spot_ref, f32[12,16,512]{2,1,0:T(8,128)S(1)} %get-tuple-element.17.alpha_ref, bf16[12,16,512]{2,1,0:T(8,128)(2,1)S(1)} %get-tuple-element.18.ens_ref, f32[3,12,512]{2,1,0:T(8,128)S(1)} %collective-permute-done.prev_ref, ...), custom_call_target="tpu_custom_call" | custom-call | tf_op jit(solution)/shard_map/pallas_call | solution.py:212
  27.1 2.5 %collective-permute-start.2 = (f32[560,128]{1,0:T(8,128)S(1)}, f32[560,128]{1,0:T(8,128)S(1)}, u32[]{:S(2)}, u32[]{:S(2)}) collective-permute-start(f32[560,128]{1,0:T(8,128)S(1)} %get-tuple-element.25), channel_id=1, source_target_pairs={{0,8},{8,0},{1,9},{9,1},{2,10},{10,2},{3,11},{11,3},{4,12},{12,4},... | collective-permute-start | bytes 860168 | tf_op jit(solution)/shard_map/ppermute | solution.py:268
  29.6 1.2 %collective-permute-done.2.got_ref = f32[560,128]{1,0:T(8,128)S(1)} collective-permute-done((f32[560,128]{1,0:T(8,128)S(1)}, f32[560,128]{1,0:T(8,128)S(1)}, u32[]{:S(2)}, u32[]{:S(2)}) %collective-permute-start.2) | collective-permute-done | bytes 286752 | tf_op jit(solution)/shard_map/ppermute | solution.py:268
  30.8 0.7 shard_map.97
  31.5 9.4 %all-to-all-start = ((f32[32,1,2176]{2,1,0:T(1,128)}), f32[32,1,2176]{2,1,0:T(1,128)S(1)}, u32[]{:S(2)}, u32[]{:S(2)}) async-start(f32[32,1,2176]{2,1,0:T(1,128)} %bitcast.8), calls=%async_computation | async-start | bytes 557056 | tf_op jit(solution)/shard_map/all_to_all | solution.py:233
  41.0 4.0 %collective-permute-start.3 = (f32[12,48]{1,0:T(8,128)S(1)}, f32[12,48]{1,0:T(8,128)S(1)}, u32[]{:S(2)}, u32[]{:S(2)}) collective-permute-start(f32[12,48]{1,0:T(8,128)S(1)} %get-tuple-element.36), channel_id=1, source_target_pairs={{0,504},{8,16},{16,8},{24,32},{32,24},{40,48},{48,40},{56,64},{64,... | collective-permute-start | bytes 6920 | tf_op jit(solution)/shard_map/ppermute | solution.py:253
  44.9 2.0 %collective-permute-done.3 = f32[12,48]{1,0:T(8,128)S(1)} collective-permute-done((f32[12,48]{1,0:T(8,128)S(1)}, f32[12,48]{1,0:T(8,128)S(1)}, u32[]{:S(2)}, u32[]{:S(2)}) %collective-permute-start.3) | collective-permute-done | bytes 2336 | tf_op jit(solution)/shard_map/ppermute | solution.py:253
  47.0 6.6 %all-to-all-done = f32[32,1,2176]{2,1,0:T(1,128)S(1)} async-done(((f32[32,1,2176]{2,1,0:T(1,128)}), f32[32,1,2176]{2,1,0:T(1,128)S(1)}, u32[]{:S(2)}, u32[]{:S(2)}) %all-to-all-start) | async-done | bytes 278560 | tf_op jit(solution)/shard_map/all_to_all | solution.py:233
  53.6 2.5 %shard_map.98 = (f32[24,16,48]{2,1,0:T(8,128)S(1)}, f32[17,128]{1,0:T(8,128)S(1)}, f32[17,128]{1,0:T(8,128)S(1)}) custom-call(s32[2]{0:T(128)S(1)} %pad_add_fusion.spot_ref, f32[544,128]{1,0:T(8,128)S(1)} %bitcast.22, f32[16,48]{1,0:T(8,128)S(1)} %slice.20.near_ref, f32[16,48]{1,0:T(8,128)S(1)} %pad.19.far_ref, f32[24,16,48]{2,1,0:T(8,128)S(1)} %pad.16.bg_ref, ...), custom_call_target="tpu_custom_call" | custom-call | tf_op jit(solution)/shard_map/pallas_call | solution.py:212
  56.1 4.8 %collective-permute-start.4 = (f32[17,128]{1,0:T(8,128)S(1)}, f32[17,128]{1,0:T(8,128)S(1)}, u32[]{:S(2)}, u32[]{:S(2)}) collective-permute-start(f32[17,128]{1,0:T(8,128)S(1)} %get-tuple-element.31), channel_id=1, source_target_pairs={{0,1},{1,2},{2,3},{3,4},{4,5},{5,6},{6,7},{8,9},{9,10},{10,11},{11... | collective-permute-start | bytes 26120 | tf_op jit(solution)/shard_map/ppermute | solution.py:229
  60.9 1.3 %collective-permute-start.5 = (f32[17,128]{1,0:T(8,128)S(1)}, f32[17,128]{1,0:T(8,128)S(1)}, u32[]{:S(2)}, u32[]{:S(2)}) collective-permute-start(f32[17,128]{1,0:T(8,128)S(1)} %get-tuple-element.31), channel_id=1, source_target_pairs={{1,0},{2,1},{3,2},{4,3},{5,4},{6,5},{7,6},{9,8},{10,9},{11,10},{12... | collective-permute-start | bytes 26120 | tf_op jit(solution)/shard_map/ppermute | solution.py:229
  62.2 7.0 %collective-permute-done.5.next_ref = f32[17,128]{1,0:T(8,128)S(1)} collective-permute-done((f32[17,128]{1,0:T(8,128)S(1)}, f32[17,128]{1,0:T(8,128)S(1)}, u32[]{:S(2)}, u32[]{:S(2)}) %collective-permute-start.5) | collective-permute-done | bytes 8736 | tf_op jit(solution)/shard_map/ppermute | solution.py:229
  69.2 0.8 shard_map.99
  70.0 4.7 %all-to-all-start.1 = ((f32[32,1,2176]{2,1,0:T(1,128)}), f32[32,1,2176]{2,1,0:T(1,128)S(1)}, u32[]{:S(2)}, u32[]{:S(2)}) async-start(f32[32,1,2176]{2,1,0:T(1,128)} %bitcast.12), calls=%async_computation.1 | async-start | bytes 557056 | tf_op jit(solution)/shard_map/all_to_all | solution.py:233
  74.9 0.9 reshape.32
  75.7 10.1 %all-to-all-done.1 = f32[32,1,2176]{2,1,0:T(1,128)S(1)} async-done(((f32[32,1,2176]{2,1,0:T(1,128)}), f32[32,1,2176]{2,1,0:T(1,128)S(1)}, u32[]{:S(2)}, u32[]{:S(2)}) %all-to-all-start.1) | async-done | bytes 278560 | tf_op jit(solution)/shard_map/all_to_all | solution.py:233
  85.8 6.3 %all_gather.3.g_ref = f32[1088,128]{1,0:T(8,128)S(1)} all-gather(f32[544,128]{1,0:T(8,128)S(1)} %bitcast.23), channel_id=1, replica_groups=mesh['chip'=32,'core'=2,'band'=8] {'core'}, dimensions={0}, use_global_device_ids=true | all-gather | bytes 835584 | tf_op jit(solution)/shard_map/all_gather | solution.py:278
  92.1 1.6 %shard_map.100 = f32[12,16,512]{2,1,0:T(8,128)} custom-call(f32[1088,128]{1,0:T(8,128)S(1)} %all_gather.3.g_ref, bf16[12,16,512]{2,1,0:T(8,128)(2,1)S(1)} %get-tuple-element.18.ens_ref, f32[3,12,512]{2,1,0:T(8,128)S(1)} %collective-permute-done.prev_ref, f32[3,12,512]{2,1,0:T(8,128)S(1)} %collective-permute-done.1.next_ref), custom_call_target="tpu_custom_call" | custom-call | tf_op jit(solution)/shard_map/pallas_call | solution.py:212
  (31 shorter events, 2.2 us)
Async XLA Ops:
  0.6 13.9 %copy-start = (f32[12,1,1152]{2,1,0:T(1,128)S(1)}, f32[12,1,1152]{2,1,0:T(1,128)}, u32[]{:S(2)}) copy-start(f32[12,1,1152]{2,1,0:T(1,128)} %param.12) | copy-start | bytes 165892
  1.8 16.2 %collective-permute-start = (f32[3,12,512]{2,1,0:T(8,128)S(1)}, f32[3,12,512]{2,1,0:T(8,128)S(1)}, u32[]{:S(2)}, u32[]{:S(2)}) collective-permute-start(f32[3,12,512]{2,1,0:T(8,128)S(1)} %get-tuple-element.19), channel_id=1, source_target_pairs={{0,1},{1,2},{2,3},{3,4},{4,5},{5,6},{6,7},{8,9},{9,10},{10,11},{11... | collective-permute-start | bytes 221192 | tf_op jit(solution)/shard_map/ppermute | solution.py:229
  13.3 12.4 %collective-permute-start.1 = (f32[3,12,512]{2,1,0:T(8,128)S(1)}, f32[3,12,512]{2,1,0:T(8,128)S(1)}, u32[]{:S(2)}, u32[]{:S(2)}) collective-permute-start(f32[3,12,512]{2,1,0:T(8,128)S(1)} %get-tuple-element.20), channel_id=1, source_target_pairs={{1,0},{2,1},{3,2},{4,3},{5,4},{6,5},{7,6},{9,8},{10,9},{11,10},{12... | collective-permute-start | bytes 221192 | tf_op jit(solution)/shard_map/ppermute | solution.py:229
  15.1 0.7 copy-start.1
  15.1 0.7 copy-start.2
  15.9 0.7 copy-start.5
  16.5 0.7 copy-start.4
  17.2 0.7 copy-start.3
  27.1 3.7 %collective-permute-start.2 = (f32[560,128]{1,0:T(8,128)S(1)}, f32[560,128]{1,0:T(8,128)S(1)}, u32[]{:S(2)}, u32[]{:S(2)}) collective-permute-start(f32[560,128]{1,0:T(8,128)S(1)} %get-tuple-element.25), channel_id=1, source_target_pairs={{0,8},{8,0},{1,9},{9,1},{2,10},{10,2},{3,11},{11,3},{4,12},{12,4},... | collective-permute-start | bytes 860168 | tf_op jit(solution)/shard_map/ppermute | solution.py:268
  31.5 22.1 %all-to-all-start = ((f32[32,1,2176]{2,1,0:T(1,128)}), f32[32,1,2176]{2,1,0:T(1,128)S(1)}, u32[]{:S(2)}, u32[]{:S(2)}) async-start(f32[32,1,2176]{2,1,0:T(1,128)} %bitcast.8), calls=%async_computation | async-start | bytes 557056 | tf_op jit(solution)/shard_map/all_to_all | solution.py:233
  41.0 5.9 %collective-permute-start.3 = (f32[12,48]{1,0:T(8,128)S(1)}, f32[12,48]{1,0:T(8,128)S(1)}, u32[]{:S(2)}, u32[]{:S(2)}) collective-permute-start(f32[12,48]{1,0:T(8,128)S(1)} %get-tuple-element.36), channel_id=1, source_target_pairs={{0,504},{8,16},{16,8},{24,32},{32,24},{40,48},{48,40},{56,64},{64,... | collective-permute-start | bytes 6920 | tf_op jit(solution)/shard_map/ppermute | solution.py:253
  56.1 6.2 %collective-permute-start.4 = (f32[17,128]{1,0:T(8,128)S(1)}, f32[17,128]{1,0:T(8,128)S(1)}, u32[]{:S(2)}, u32[]{:S(2)}) collective-permute-start(f32[17,128]{1,0:T(8,128)S(1)} %get-tuple-element.31), channel_id=1, source_target_pairs={{0,1},{1,2},{2,3},{3,4},{4,5},{5,6},{6,7},{8,9},{9,10},{10,11},{11... | collective-permute-start | bytes 26120 | tf_op jit(solution)/shard_map/ppermute | solution.py:229
  60.9 8.3 %collective-permute-start.5 = (f32[17,128]{1,0:T(8,128)S(1)}, f32[17,128]{1,0:T(8,128)S(1)}, u32[]{:S(2)}, u32[]{:S(2)}) collective-permute-start(f32[17,128]{1,0:T(8,128)S(1)} %get-tuple-element.31), channel_id=1, source_target_pairs={{1,0},{2,1},{3,2},{4,3},{5,4},{6,5},{7,6},{9,8},{10,9},{11,10},{12... | collective-permute-start | bytes 26120 | tf_op jit(solution)/shard_map/ppermute | solution.py:229
  70.0 15.8 %all-to-all-start.1 = ((f32[32,1,2176]{2,1,0:T(1,128)}), f32[32,1,2176]{2,1,0:T(1,128)S(1)}, u32[]{:S(2)}, u32[]{:S(2)}) async-start(f32[32,1,2176]{2,1,0:T(1,128)} %bitcast.12), calls=%async_computation.1 | async-start | bytes 557056 | tf_op jit(solution)/shard_map/all_to_all | solution.py:233

commit v5 on v4

--- a/solution.py
+++ b/solution.py
@@ -75,7 +75,7 @@
             rows = pl.ds(7 + c + BLOCK * core, CHIPS, stride=2 * BLOCK)
             flat[core, :, c * Q : c * Q + 128] = xt_lo[rows, :]
             flat[core, :, c * Q + 128 : (c + 1) * Q] = xt_hi[rows, :][:, : Q - 128]
-    first = spot_ref[0] == 0
+    first = spot_ref[0:1, :128] == 0.0
     for t in range(TILES):
         even = flat[0, :, 128 * t : 128 * (t + 1)]
         odd = flat[1, :, 128 * t : 128 * (t + 1)]
@@ -102,7 +102,7 @@
     for t in range(TILES):
         part = g_ref[pl.ds(t, CHIPS, stride=TILES), :]
         flat[0:1, 128 * t : 128 * (t + 1)] = jnp.sum(part, axis=0, keepdims=True)
-    first = spot_ref[0] == 0
+    first = spot_ref[0:1, :FINE_R] == 0.0
     near, far = near_ref[...], far_ref[...]
     ground = [jnp.where(first, far, near)] + [bg_ref[j] for j in range(FINE_C)] + [jnp.where(first, near, far)]
     q = lax.broadcasted_iota(jnp.int32, (1, Q), 1)
@@ -236,7 +236,7 @@
 
 def shards(ensemble, alpha, lat_lower, lat_weight, background, obs_cell, obs_value, obs_precision):
     scale = 1.0 / math.sqrt(2 * CHIPS - 1)
-    spot = jnp.stack([lax.axis_index("core"), lax.axis_index("chip")]).astype(jnp.int32)
+    spot = jnp.broadcast_to(lax.axis_index("core").astype(jnp.float32), (1, COLS))
     last, first, alf, ens = call(
         halo_kernel,
         (f32(3, LEV, COLS), f32(3, LEV, COLS), f32(LEV, ROWS, COLS), jax.ShapeDtypeStruct((LEV, ROWS, COLS), jnp.bfloat16)),

time: 94.3 us -> 93.2 us (0.988)
  Pallas kernels: 8.2 us -> 7.11 us
    pallas_call x6, Pallas kernels: 8.2 us -> 7.11 us  [call(): pl.pallas_call(kernel, out_shape=out, in_specs=[pl.BlockSpec(memory_space...]
where the time goes in v5:
time: 93.2 us; the launch traced here: 92.7 us
  starting transfers between devices  39.5 us (42%)
  waiting for transfers between devices  34.6 us (37%)
  Pallas kernels  7.11 us (8%)
  blocking collectives  6.3 us (7%)
  local copies, waits for them, and re-layouts  4.18 us (4%)
    all_to_all x2, waiting for transfers between devices, exchange(): lax.all_to_all(flat.reshape(CHIPS, 1, tiles * 128), 'chip', 0, 0, tiled=T...  16.7 us
    ppermute x2, starting transfers between devices, both_ways(): lax.ppermute(up_value, axis, up)  16.3 us
    ppermute x2, waiting for transfers between devices, both_ways(): lax.ppermute(down_value, axis, down)  14.8 us
    all_to_all x2, starting transfers between devices, exchange(): lax.all_to_all(flat.reshape(CHIPS, 1, tiles * 128), 'chip', 0, 0, tiled=T...  14.1 us
    pallas_call x6, Pallas kernels, call(): pl.pallas_call(kernel, out_shape=out, in_specs=[pl.BlockSpec(memory_space...  7.11 us
    all_gather x1, blocking collectives, shards(): lax.all_gather(exchange(shared, TILES), 'core', axis=0, tiled=True)  6.3 us
    ppermute x1, starting transfers between devices, shards(): lax.ppermute(far, ('chip', 'core'), [(i, (i + (1 if i % 2 else size - 1))...  3.96 us
    unnamed x13, local copies, waits for them, and re-layouts  2.64 us
  transfers between devices with their start and end apart: 8, of which 6 were waited for; matrix products, arithmetic and copies ran while one was open for 2% of the time, Pallas kernels for 0%

profile of v5, /device:TPU:1, one launch (start us, length us, event | category | flops | bytes accessed | tf_op | source)
XLA Modules:
  0.0 92.7 jit_solution(12934328631027230777)
XLA Ops:
  0.6 1.1 %shard_map.95 = (f32[3,12,512]{2,1,0:T(8,128)S(1)}, f32[3,12,512]{2,1,0:T(8,128)S(1)}, f32[12,16,512]{2,1,0:T(8,128)S(1)}, bf16[12,16,512]{2,1,0:T(8,128)(2,1)S(1)}) custom-call(f32[12,16,512]{2,1,0:T(8,128)} %bitcast.24, bf16[12,16,512]{2,1,0:T(8,128)(2,1)} %bitcast.26), custom_call_target="tpu_custom_call" | custom-call | tf_op jit(solution)/shard_map/pallas_call | solution.py:212
  1.8 11.5 %collective-permute-start = (f32[3,12,512]{2,1,0:T(8,128)S(1)}, f32[3,12,512]{2,1,0:T(8,128)S(1)}, u32[]{:S(2)}, u32[]{:S(2)}) collective-permute-start(f32[3,12,512]{2,1,0:T(8,128)S(1)} %get-tuple-element.19), channel_id=1, source_target_pairs={{0,1},{1,2},{2,3},{3,4},{4,5},{5,6},{6,7},{8,9},{9,10},{10,11},{11... | collective-permute-start | bytes 221192 | tf_op jit(solution)/shard_map/ppermute | solution.py:229
  13.3 1.3 %collective-permute-start.1 = (f32[3,12,512]{2,1,0:T(8,128)S(1)}, f32[3,12,512]{2,1,0:T(8,128)S(1)}, u32[]{:S(2)}, u32[]{:S(2)}) collective-permute-start(f32[3,12,512]{2,1,0:T(8,128)S(1)} %get-tuple-element.20), channel_id=1, source_target_pairs={{1,0},{2,1},{3,2},{4,3},{5,4},{6,5},{7,6},{9,8},{10,9},{11,10},{12... | collective-permute-start | bytes 221192 | tf_op jit(solution)/shard_map/ppermute | solution.py:229
  15.2 0.7 copy-done.2
  16.5 0.7 copy-done.3
  17.9 7.7 %collective-permute-done.1.next_ref = f32[3,12,512]{2,1,0:T(8,128)S(1)} collective-permute-done((f32[3,12,512]{2,1,0:T(8,128)S(1)}, f32[3,12,512]{2,1,0:T(8,128)S(1)}, u32[]{:S(2)}, u32[]{:S(2)}) %collective-permute-start.1) | collective-permute-done | bytes 73760 | tf_op jit(solution)/shard_map/ppermute | solution.py:229
  25.6 0.9 shard_map.96
  26.6 2.5 %collective-permute-start.2 = (f32[560,128]{1,0:T(8,128)S(1)}, f32[560,128]{1,0:T(8,128)S(1)}, u32[]{:S(2)}, u32[]{:S(2)}) collective-permute-start(f32[560,128]{1,0:T(8,128)S(1)} %get-tuple-element.25), channel_id=1, source_target_pairs={{0,8},{8,0},{1,9},{9,1},{2,10},{10,2},{3,11},{11,3},{4,12},{12,4},... | collective-permute-start | bytes 860168 | tf_op jit(solution)/shard_map/ppermute | solution.py:268
  29.1 1.2 %collective-permute-done.2.got_ref = f32[560,128]{1,0:T(8,128)S(1)} collective-permute-done((f32[560,128]{1,0:T(8,128)S(1)}, f32[560,128]{1,0:T(8,128)S(1)}, u32[]{:S(2)}, u32[]{:S(2)}) %collective-permute-start.2) | collective-permute-done | bytes 286752 | tf_op jit(solution)/shard_map/ppermute | solution.py:268
  30.2 0.7 shard_map.97
  31.0 9.4 %all-to-all-start = ((f32[32,1,2176]{2,1,0:T(1,128)}), f32[32,1,2176]{2,1,0:T(1,128)S(1)}, u32[]{:S(2)}, u32[]{:S(2)}) async-start(f32[32,1,2176]{2,1,0:T(1,128)} %bitcast.6), calls=%async_computation | async-start | bytes 557056 | tf_op jit(solution)/shard_map/all_to_all | solution.py:233
  40.4 4.0 %collective-permute-start.3 = (f32[12,48]{1,0:T(8,128)S(1)}, f32[12,48]{1,0:T(8,128)S(1)}, u32[]{:S(2)}, u32[]{:S(2)}) collective-permute-start(f32[12,48]{1,0:T(8,128)S(1)} %get-tuple-element.36), channel_id=1, source_target_pairs={{0,504},{8,16},{16,8},{24,32},{32,24},{40,48},{48,40},{56,64},{64,... | collective-permute-start | bytes 6920 | tf_op jit(solution)/shard_map/ppermute | solution.py:253
  44.4 2.0 %collective-permute-done.3 = f32[12,48]{1,0:T(8,128)S(1)} collective-permute-done((f32[12,48]{1,0:T(8,128)S(1)}, f32[12,48]{1,0:T(8,128)S(1)}, u32[]{:S(2)}, u32[]{:S(2)}) %collective-permute-start.3) | collective-permute-done | bytes 2336 | tf_op jit(solution)/shard_map/ppermute | solution.py:253
  46.5 6.6 %all-to-all-done = f32[32,1,2176]{2,1,0:T(1,128)S(1)} async-done(((f32[32,1,2176]{2,1,0:T(1,128)}), f32[32,1,2176]{2,1,0:T(1,128)S(1)}, u32[]{:S(2)}, u32[]{:S(2)}) %all-to-all-start) | async-done | bytes 278560 | tf_op jit(solution)/shard_map/all_to_all | solution.py:233
  53.0 1.9 %shard_map.98 = (f32[24,16,48]{2,1,0:T(8,128)S(1)}, f32[17,128]{1,0:T(8,128)S(1)}, f32[17,128]{1,0:T(8,128)S(1)}) custom-call(f32[1,512]{1,0:T(1,128)S(1)} %broadcast_in_dim.9.spot_ref, f32[544,128]{1,0:T(8,128)S(1)} %bitcast.20, f32[16,48]{1,0:T(8,128)S(1)} %slice.20.near_ref, f32[16,48]{1,0:T(8,128)S(1)} %pad.19.far_ref, f32[24,16,48]{2,1,0:T(8,128)S(1)} %pad.16.bg_ref, ...), custom_call_target="tpu_custom_call" | custom-call | tf_op jit(solution)/shard_map/pallas_call | solution.py:212
  55.0 4.8 %collective-permute-start.4 = (f32[17,128]{1,0:T(8,128)S(1)}, f32[17,128]{1,0:T(8,128)S(1)}, u32[]{:S(2)}, u32[]{:S(2)}) collective-permute-start(f32[17,128]{1,0:T(8,128)S(1)} %get-tuple-element.31), channel_id=1, source_target_pairs={{0,1},{1,2},{2,3},{3,4},{4,5},{5,6},{6,7},{8,9},{9,10},{10,11},{11... | collective-permute-start | bytes 26120 | tf_op jit(solution)/shard_map/ppermute | solution.py:229
  59.8 1.3 %collective-permute-start.5 = (f32[17,128]{1,0:T(8,128)S(1)}, f32[17,128]{1,0:T(8,128)S(1)}, u32[]{:S(2)}, u32[]{:S(2)}) collective-permute-start(f32[17,128]{1,0:T(8,128)S(1)} %get-tuple-element.31), channel_id=1, source_target_pairs={{1,0},{2,1},{3,2},{4,3},{5,4},{6,5},{7,6},{9,8},{10,9},{11,10},{12... | collective-permute-start | bytes 26120 | tf_op jit(solution)/shard_map/ppermute | solution.py:229
  61.1 7.0 %collective-permute-done.5.next_ref = f32[17,128]{1,0:T(8,128)S(1)} collective-permute-done((f32[17,128]{1,0:T(8,128)S(1)}, f32[17,128]{1,0:T(8,128)S(1)}, u32[]{:S(2)}, u32[]{:S(2)}) %collective-permute-start.5) | collective-permute-done | bytes 8736 | tf_op jit(solution)/shard_map/ppermute | solution.py:229
  68.2 0.8 shard_map.99
  68.9 4.7 %all-to-all-start.1 = ((f32[32,1,2176]{2,1,0:T(1,128)}), f32[32,1,2176]{2,1,0:T(1,128)S(1)}, u32[]{:S(2)}, u32[]{:S(2)}) async-start(f32[32,1,2176]{2,1,0:T(1,128)} %bitcast.10), calls=%async_computation.1 | async-start | bytes 557056 | tf_op jit(solution)/shard_map/all_to_all | solution.py:233
  73.8 0.9 reshape.32
  74.6 10.1 %all-to-all-done.1 = f32[32,1,2176]{2,1,0:T(1,128)S(1)} async-done(((f32[32,1,2176]{2,1,0:T(1,128)}), f32[32,1,2176]{2,1,0:T(1,128)S(1)}, u32[]{:S(2)}, u32[]{:S(2)}) %all-to-all-start.1) | async-done | bytes 278560 | tf_op jit(solution)/shard_map/all_to_all | solution.py:233
  84.7 6.3 %all_gather.3.g_ref = f32[1088,128]{1,0:T(8,128)S(1)} all-gather(f32[544,128]{1,0:T(8,128)S(1)} %bitcast.21), channel_id=1, replica_groups=mesh['chip'=32,'core'=2,'band'=8] {'core'}, dimensions={0}, use_global_device_ids=true | all-gather | bytes 835584 | tf_op jit(solution)/shard_map/all_gather | solution.py:278
  91.0 1.6 %shard_map.100 = f32[12,16,512]{2,1,0:T(8,128)} custom-call(f32[1088,128]{1,0:T(8,128)S(1)} %all_gather.3.g_ref, bf16[12,16,512]{2,1,0:T(8,128)(2,1)S(1)} %get-tuple-element.18.ens_ref, f32[3,12,512]{2,1,0:T(8,128)S(1)} %collective-permute-done.prev_ref, f32[3,12,512]{2,1,0:T(8,128)S(1)} %collective-permute-done.1.next_ref), custom_call_target="tpu_custom_call" | custom-call | tf_op jit(solution)/shard_map/pallas_call | solution.py:212
  (31 shorter events, 2.2 us)
Async XLA Ops:
  0.6 13.9 %copy-start = (f32[12,1,1152]{2,1,0:T(1,128)S(1)}, f32[12,1,1152]{2,1,0:T(1,128)}, u32[]{:S(2)}) copy-start(f32[12,1,1152]{2,1,0:T(1,128)} %param.12) | copy-start | bytes 165892
  1.8 16.1 %collective-permute-start = (f32[3,12,512]{2,1,0:T(8,128)S(1)}, f32[3,12,512]{2,1,0:T(8,128)S(1)}, u32[]{:S(2)}, u32[]{:S(2)}) collective-permute-start(f32[3,12,512]{2,1,0:T(8,128)S(1)} %get-tuple-element.19), channel_id=1, source_target_pairs={{0,1},{1,2},{2,3},{3,4},{4,5},{5,6},{6,7},{8,9},{9,10},{10,11},{11... | collective-permute-start | bytes 221192 | tf_op jit(solution)/shard_map/ppermute | solution.py:229
  13.3 12.4 %collective-permute-start.1 = (f32[3,12,512]{2,1,0:T(8,128)S(1)}, f32[3,12,512]{2,1,0:T(8,128)S(1)}, u32[]{:S(2)}, u32[]{:S(2)}) collective-permute-start(f32[3,12,512]{2,1,0:T(8,128)S(1)} %get-tuple-element.20), channel_id=1, source_target_pairs={{1,0},{2,1},{3,2},{4,3},{5,4},{6,5},{7,6},{9,8},{10,9},{11,10},{12... | collective-permute-start | bytes 221192 | tf_op jit(solution)/shard_map/ppermute | solution.py:229
  15.1 0.7 copy-start.1
  15.1 0.7 copy-start.2
  15.9 0.7 copy-start.5
  16.5 0.7 copy-start.3
  17.2 0.7 copy-start.4
  26.6 3.7 %collective-permute-start.2 = (f32[560,128]{1,0:T(8,128)S(1)}, f32[560,128]{1,0:T(8,128)S(1)}, u32[]{:S(2)}, u32[]{:S(2)}) collective-permute-start(f32[560,128]{1,0:T(8,128)S(1)} %get-tuple-element.25), channel_id=1, source_target_pairs={{0,8},{8,0},{1,9},{9,1},{2,10},{10,2},{3,11},{11,3},{4,12},{12,4},... | collective-permute-start | bytes 860168 | tf_op jit(solution)/shard_map/ppermute | solution.py:268
  31.0 22.1 %all-to-all-start = ((f32[32,1,2176]{2,1,0:T(1,128)}), f32[32,1,2176]{2,1,0:T(1,128)S(1)}, u32[]{:S(2)}, u32[]{:S(2)}) async-start(f32[32,1,2176]{2,1,0:T(1,128)} %bitcast.6), calls=%async_computation | async-start | bytes 557056 | tf_op jit(solution)/shard_map/all_to_all | solution.py:233
  40.4 5.9 %collective-permute-start.3 = (f32[12,48]{1,0:T(8,128)S(1)}, f32[12,48]{1,0:T(8,128)S(1)}, u32[]{:S(2)}, u32[]{:S(2)}) collective-permute-start(f32[12,48]{1,0:T(8,128)S(1)} %get-tuple-element.36), channel_id=1, source_target_pairs={{0,504},{8,16},{16,8},{24,32},{32,24},{40,48},{48,40},{56,64},{64,... | collective-permute-start | bytes 6920 | tf_op jit(solution)/shard_map/ppermute | solution.py:253
  55.0 6.2 %collective-permute-start.4 = (f32[17,128]{1,0:T(8,128)S(1)}, f32[17,128]{1,0:T(8,128)S(1)}, u32[]{:S(2)}, u32[]{:S(2)}) collective-permute-start(f32[17,128]{1,0:T(8,128)S(1)} %get-tuple-element.31), channel_id=1, source_target_pairs={{0,1},{1,2},{2,3},{3,4},{4,5},{5,6},{6,7},{8,9},{9,10},{10,11},{11... | collective-permute-start | bytes 26120 | tf_op jit(solution)/shard_map/ppermute | solution.py:229
  59.8 8.3 %collective-permute-start.5 = (f32[17,128]{1,0:T(8,128)S(1)}, f32[17,128]{1,0:T(8,128)S(1)}, u32[]{:S(2)}, u32[]{:S(2)}) collective-permute-start(f32[17,128]{1,0:T(8,128)S(1)} %get-tuple-element.31), channel_id=1, source_target_pairs={{1,0},{2,1},{3,2},{4,3},{5,4},{6,5},{7,6},{9,8},{10,9},{11,10},{12... | collective-permute-start | bytes 26120 | tf_op jit(solution)/shard_map/ppermute | solution.py:229
  68.9 15.8 %all-to-all-start.1 = ((f32[32,1,2176]{2,1,0:T(1,128)}), f32[32,1,2176]{2,1,0:T(1,128)S(1)}, u32[]{:S(2)}, u32[]{:S(2)}) async-start(f32[32,1,2176]{2,1,0:T(1,128)} %bitcast.10), calls=%async_computation.1 | async-start | bytes 557056 | tf_op jit(solution)/shard_map/all_to_all | solution.py:233

commit v6 on v5

--- a/solution.py
+++ b/solution.py
@@ -84,8 +84,10 @@
     send_ref[PAIR:, :] = sides_ref[...]
 
 
-def pair_kernel(keep_ref, got_ref, out_ref):
-    out_ref[...] = keep_ref[...] + got_ref[:PAIR, :]
+def pair_kernel(spot_ref, keep_ref, both_ref, out_ref, near_ref):
+    first = spot_ref[0:1, :128] == 0.0
+    out_ref[...] = keep_ref[...] + jnp.where(first, both_ref[PAIR + LPAD : 2 * PAIR + LPAD, :], both_ref[:PAIR, :])
+    near_ref[...] = jnp.where(first, both_ref[2 * PAIR + LPAD :, :], both_ref[PAIR : PAIR + LPAD, :])
 
 
 def split_dot(x, pick, dim):
@@ -103,7 +105,7 @@
         part = g_ref[pl.ds(t, CHIPS, stride=TILES), :]
         flat[0:1, 128 * t : 128 * (t + 1)] = jnp.sum(part, axis=0, keepdims=True)
     first = spot_ref[0:1, :FINE_R] == 0.0
-    near, far = near_ref[...], far_ref[...]
+    near, far = near_ref[:, :FINE_R], far_ref[...]
     ground = [jnp.where(first, far, near)] + [bg_ref[j] for j in range(FINE_C)] + [jnp.where(first, near, far)]
     q = lax.broadcasted_iota(jnp.int32, (1, Q), 1)
     spot = jnp.where(q < MAIN, (q & 15) + 1, jnp.where(q < MAIN + LEV, 0, ROWS + 1))
@@ -265,13 +267,14 @@
         [(LEV, 32, COLS), (256, COLS), (COLS + 16, 128), (COLS + 16, 128), (2, CHIPS, CHUNK)],
         spot, alf, ens, before, after, sides,
     )
-    got = lax.ppermute(send, "core", [(0, 1), (1, 0)])
-    gathered = exchange(call(pair_kernel, f32(PAIR, 128), [], keep, got), TILES)
+    both = lax.all_gather(send, "core", axis=0, tiled=True)
+    paired, near = call(pair_kernel, (f32(PAIR, 128), f32(LPAD, 128)), [], spot, keep, both)
+    gathered = exchange(paired, TILES)
     moved, own, edge = call(
         tile_kernel,
         (f32(FINE_C, LPAD, FINE_R), f32(TILES, 128), f32(TILES, 128)),
         [(8, CHUNK)],
-        spot, gathered, got[PAIR:, :FINE_R], far, ground, lat, obs,
+        spot, gathered, near, far, ground, lat, obs,
     )
     from_prev, from_next = both_ways(edge, edge, "band", BANDS, False)
     shared = call(share_kernel, f32(CHIPS * TILES, 128), [], own, from_prev, from_next)

time: 93.2 us -> 92 us (0.987)
  starting transfers between devices: 39.5 us -> 37 us
  blocking collectives: 6.3 us -> 8.74 us
  waiting for transfers between devices: 34.6 us -> 33.4 us
    ppermute x1 -> x0, starting transfers between devices: 2.51 us -> none  [shards(): got = lax.ppermute(send, 'core', [(0, 1), (1, 0)])]
    all_gather x0 -> x1, blocking collectives: none -> 2.44 us  [shards(): both = lax.all_gather(send, 'core', axis=0, tiled=True)]
    ppermute x1 -> x0, waiting for transfers between devices: 1.18 us -> none  [shards(): got = lax.ppermute(send, 'core', [(0, 1), (1, 0)])]
  transfers between devices with their start and end apart: 8 -> 7, of which waited for: 6 -> 5; matrix products, arithmetic and copies ran while one was open for 2% -> 2% of each run, Pallas kernels for 0% -> 0%
where the time goes in v6:
time: 92 us; the launch traced here: 91.4 us
  starting transfers between devices  37 us (40%)
  waiting for transfers between devices  33.4 us (36%)
  blocking collectives  8.74 us (10%)
  Pallas kernels  7.12 us (8%)
  local copies, waits for them, and re-layouts  4.18 us (5%)
    all_to_all x2, waiting for transfers between devices, exchange(): lax.all_to_all(flat.reshape(CHIPS, 1, tiles * 128), 'chip', 0, 0, tiled=T...  16.7 us
    ppermute x2, starting transfers between devices, both_ways(): lax.ppermute(up_value, axis, up)  16.3 us
    ppermute x2, waiting for transfers between devices, both_ways(): lax.ppermute(down_value, axis, down)  14.8 us
    all_to_all x2, starting transfers between devices, exchange(): lax.all_to_all(flat.reshape(CHIPS, 1, tiles * 128), 'chip', 0, 0, tiled=T...  14.1 us
    pallas_call x6, Pallas kernels, call(): pl.pallas_call(kernel, out_shape=out, in_specs=[pl.BlockSpec(memory_space...  7.12 us
    all_gather x1, blocking collectives, shards(): lax.all_gather(exchange(shared, TILES), 'core', axis=0, tiled=True)  6.3 us
    ppermute x1, starting transfers between devices, shards(): lax.ppermute(far, ('chip', 'core'), [(i, (i + (1 if i % 2 else size - 1))...  3.96 us
    unnamed x13, local copies, waits for them, and re-layouts  2.64 us
  transfers between devices with their start and end apart: 7, of which 5 were waited for; matrix products, arithmetic and copies ran while one was open for 2% of the time, Pallas kernels for 0%

profile of v6, /device:TPU:1, one launch (start us, length us, event | category | flops | bytes accessed | tf_op | source)
XLA Modules:
  0.0 91.4 jit_solution(7712690431881534650)
XLA Ops:
  0.6 1.1 %shard_map.95 = (f32[3,12,512]{2,1,0:T(8,128)S(1)}, f32[3,12,512]{2,1,0:T(8,128)S(1)}, f32[12,16,512]{2,1,0:T(8,128)S(1)}, bf16[12,16,512]{2,1,0:T(8,128)(2,1)S(1)}) custom-call(f32[12,16,512]{2,1,0:T(8,128)} %bitcast.24, bf16[12,16,512]{2,1,0:T(8,128)(2,1)} %bitcast.26), custom_call_target="tpu_custom_call" | custom-call | tf_op jit(solution)/shard_map/pallas_call | solution.py:214
  1.8 11.5 %collective-permute-start = (f32[3,12,512]{2,1,0:T(8,128)S(1)}, f32[3,12,512]{2,1,0:T(8,128)S(1)}, u32[]{:S(2)}, u32[]{:S(2)}) collective-permute-start(f32[3,12,512]{2,1,0:T(8,128)S(1)} %get-tuple-element.21), channel_id=1, source_target_pairs={{0,1},{1,2},{2,3},{3,4},{4,5},{5,6},{6,7},{8,9},{9,10},{10,11},{11... | collective-permute-start | bytes 221192 | tf_op jit(solution)/shard_map/ppermute | solution.py:231
  13.3 1.3 %collective-permute-start.1 = (f32[3,12,512]{2,1,0:T(8,128)S(1)}, f32[3,12,512]{2,1,0:T(8,128)S(1)}, u32[]{:S(2)}, u32[]{:S(2)}) collective-permute-start(f32[3,12,512]{2,1,0:T(8,128)S(1)} %get-tuple-element.22), channel_id=1, source_target_pairs={{1,0},{2,1},{3,2},{4,3},{5,4},{6,5},{7,6},{9,8},{10,9},{11,10},{12... | collective-permute-start | bytes 221192 | tf_op jit(solution)/shard_map/ppermute | solution.py:231
  15.2 0.7 copy-done.2
  16.5 0.7 copy-done.3
  17.2 0.7 copy-done.4
  17.9 7.7 %collective-permute-done.1.next_ref = f32[3,12,512]{2,1,0:T(8,128)S(1)} collective-permute-done((f32[3,12,512]{2,1,0:T(8,128)S(1)}, f32[3,12,512]{2,1,0:T(8,128)S(1)}, u32[]{:S(2)}, u32[]{:S(2)}) %collective-permute-start.1) | collective-permute-done | bytes 73760 | tf_op jit(solution)/shard_map/ppermute | solution.py:231
  25.6 0.9 shard_map.96
  26.6 2.4 %all_gather.6.both_ref = f32[1120,128]{1,0:T(8,128)S(1)} all-gather(f32[560,128]{1,0:T(8,128)S(1)} %get-tuple-element.27), channel_id=1, replica_groups=mesh['chip'=32,'core'=2,'band'=8] {'core'}, dimensions={0}, use_global_device_ids=true | all-gather | bytes 860160 | tf_op jit(solution)/shard_map/all_gather | solution.py:270
  29.0 0.7 shard_map.97
  29.7 9.4 %all-to-all-start = ((f32[32,1,2176]{2,1,0:T(1,128)}), f32[32,1,2176]{2,1,0:T(1,128)S(1)}, u32[]{:S(2)}, u32[]{:S(2)}) async-start(f32[32,1,2176]{2,1,0:T(1,128)} %bitcast.6), calls=%async_computation | async-start | bytes 557056 | tf_op jit(solution)/shard_map/all_to_all | solution.py:235
  39.2 4.0 %collective-permute-start.2 = (f32[12,48]{1,0:T(8,128)S(1)}, f32[12,48]{1,0:T(8,128)S(1)}, u32[]{:S(2)}, u32[]{:S(2)}) collective-permute-start(f32[12,48]{1,0:T(8,128)S(1)} %get-tuple-element.40), channel_id=1, source_target_pairs={{0,504},{8,16},{16,8},{24,32},{32,24},{40,48},{48,40},{56,64},{64,... | collective-permute-start | bytes 6920 | tf_op jit(solution)/shard_map/ppermute | solution.py:255
  43.1 2.0 %collective-permute-done.2 = f32[12,48]{1,0:T(8,128)S(1)} collective-permute-done((f32[12,48]{1,0:T(8,128)S(1)}, f32[12,48]{1,0:T(8,128)S(1)}, u32[]{:S(2)}, u32[]{:S(2)}) %collective-permute-start.2) | collective-permute-done | bytes 2336 | tf_op jit(solution)/shard_map/ppermute | solution.py:255
  45.2 6.6 %all-to-all-done = f32[32,1,2176]{2,1,0:T(1,128)S(1)} async-done(((f32[32,1,2176]{2,1,0:T(1,128)}), f32[32,1,2176]{2,1,0:T(1,128)S(1)}, u32[]{:S(2)}, u32[]{:S(2)}) %all-to-all-start) | async-done | bytes 278560 | tf_op jit(solution)/shard_map/all_to_all | solution.py:235
  51.8 1.9 %shard_map.98 = (f32[24,16,48]{2,1,0:T(8,128)S(1)}, f32[17,128]{1,0:T(8,128)S(1)}, f32[17,128]{1,0:T(8,128)S(1)}) custom-call(f32[1,512]{1,0:T(1,128)S(1)} %broadcast_in_dim.9.spot_ref, f32[544,128]{1,0:T(8,128)S(1)} %bitcast.20, f32[16,128]{1,0:T(8,128)S(1)} %get-tuple-element.29.near_ref, f32[16,48]{1,0:T(8,128)S(1)} %pad.19.far_ref, ...), custom_call_target="tpu_custom_call" | custom-call | tf_op jit(solution)/shard_map/pallas_call | solution.py:214
  53.7 4.8 %collective-permute-start.3 = (f32[17,128]{1,0:T(8,128)S(1)}, f32[17,128]{1,0:T(8,128)S(1)}, u32[]{:S(2)}, u32[]{:S(2)}) collective-permute-start(f32[17,128]{1,0:T(8,128)S(1)} %get-tuple-element.35), channel_id=1, source_target_pairs={{0,1},{1,2},{2,3},{3,4},{4,5},{5,6},{6,7},{8,9},{9,10},{10,11},{11... | collective-permute-start | bytes 26120 | tf_op jit(solution)/shard_map/ppermute | solution.py:231
  58.6 1.3 %collective-permute-start.4 = (f32[17,128]{1,0:T(8,128)S(1)}, f32[17,128]{1,0:T(8,128)S(1)}, u32[]{:S(2)}, u32[]{:S(2)}) collective-permute-start(f32[17,128]{1,0:T(8,128)S(1)} %get-tuple-element.35), channel_id=1, source_target_pairs={{1,0},{2,1},{3,2},{4,3},{5,4},{6,5},{7,6},{9,8},{10,9},{11,10},{12... | collective-permute-start | bytes 26120 | tf_op jit(solution)/shard_map/ppermute | solution.py:231
  59.9 7.0 %collective-permute-done.4.next_ref = f32[17,128]{1,0:T(8,128)S(1)} collective-permute-done((f32[17,128]{1,0:T(8,128)S(1)}, f32[17,128]{1,0:T(8,128)S(1)}, u32[]{:S(2)}, u32[]{:S(2)}) %collective-permute-start.4) | collective-permute-done | bytes 8736 | tf_op jit(solution)/shard_map/ppermute | solution.py:231
  66.9 0.8 shard_map.99
  67.7 4.7 %all-to-all-start.1 = ((f32[32,1,2176]{2,1,0:T(1,128)}), f32[32,1,2176]{2,1,0:T(1,128)S(1)}, u32[]{:S(2)}, u32[]{:S(2)}) async-start(f32[32,1,2176]{2,1,0:T(1,128)} %bitcast.10), calls=%async_computation.1 | async-start | bytes 557056 | tf_op jit(solution)/shard_map/all_to_all | solution.py:235
  72.5 0.9 reshape.32
  73.4 10.1 %all-to-all-done.1 = f32[32,1,2176]{2,1,0:T(1,128)S(1)} async-done(((f32[32,1,2176]{2,1,0:T(1,128)}), f32[32,1,2176]{2,1,0:T(1,128)S(1)}, u32[]{:S(2)}, u32[]{:S(2)}) %all-to-all-start.1) | async-done | bytes 278560 | tf_op jit(solution)/shard_map/all_to_all | solution.py:235
  83.5 6.3 %all_gather.7.g_ref = f32[1088,128]{1,0:T(8,128)S(1)} all-gather(f32[544,128]{1,0:T(8,128)S(1)} %bitcast.21), channel_id=1, replica_groups=mesh['chip'=32,'core'=2,'band'=8] {'core'}, dimensions={0}, use_global_device_ids=true | all-gather | bytes 835584 | tf_op jit(solution)/shard_map/all_gather | solution.py:281
  89.8 1.6 %shard_map.100 = f32[12,16,512]{2,1,0:T(8,128)} custom-call(f32[1088,128]{1,0:T(8,128)S(1)} %all_gather.7.g_ref, bf16[12,16,512]{2,1,0:T(8,128)(2,1)S(1)} %get-tuple-element.20.ens_ref, f32[3,12,512]{2,1,0:T(8,128)S(1)} %collective-permute-done.prev_ref, f32[3,12,512]{2,1,0:T(8,128)S(1)} %collective-permute-done.1.next_ref), custom_call_target="tpu_custom_call" | custom-call | tf_op jit(solution)/shard_map/pallas_call | solution.py:214
  (29 shorter events, 1.5 us)
Async XLA Ops:
  0.6 13.9 %copy-start = (f32[12,1,1152]{2,1,0:T(1,128)S(1)}, f32[12,1,1152]{2,1,0:T(1,128)}, u32[]{:S(2)}) copy-start(f32[12,1,1152]{2,1,0:T(1,128)} %param.12) | copy-start | bytes 165892
  1.8 16.1 %collective-permute-start = (f32[3,12,512]{2,1,0:T(8,128)S(1)}, f32[3,12,512]{2,1,0:T(8,128)S(1)}, u32[]{:S(2)}, u32[]{:S(2)}) collective-permute-start(f32[3,12,512]{2,1,0:T(8,128)S(1)} %get-tuple-element.21), channel_id=1, source_target_pairs={{0,1},{1,2},{2,3},{3,4},{4,5},{5,6},{6,7},{8,9},{9,10},{10,11},{11... | collective-permute-start | bytes 221192 | tf_op jit(solution)/shard_map/ppermute | solution.py:231
  13.3 12.4 %collective-permute-start.1 = (f32[3,12,512]{2,1,0:T(8,128)S(1)}, f32[3,12,512]{2,1,0:T(8,128)S(1)}, u32[]{:S(2)}, u32[]{:S(2)}) collective-permute-start(f32[3,12,512]{2,1,0:T(8,128)S(1)} %get-tuple-element.22), channel_id=1, source_target_pairs={{1,0},{2,1},{3,2},{4,3},{5,4},{6,5},{7,6},{9,8},{10,9},{11,10},{12... | collective-permute-start | bytes 221192 | tf_op jit(solution)/shard_map/ppermute | solution.py:231
  15.1 0.7 copy-start.1
  15.1 0.7 copy-start.2
  15.9 0.7 copy-start.5
  16.5 0.7 copy-start.3
  17.2 0.7 copy-start.4
  29.7 22.1 %all-to-all-start = ((f32[32,1,2176]{2,1,0:T(1,128)}), f32[32,1,2176]{2,1,0:T(1,128)S(1)}, u32[]{:S(2)}, u32[]{:S(2)}) async-start(f32[32,1,2176]{2,1,0:T(1,128)} %bitcast.6), calls=%async_computation | async-start | bytes 557056 | tf_op jit(solution)/shard_map/all_to_all | solution.py:235
  39.2 5.9 %collective-permute-start.2 = (f32[12,48]{1,0:T(8,128)S(1)}, f32[12,48]{1,0:T(8,128)S(1)}, u32[]{:S(2)}, u32[]{:S(2)}) collective-permute-start(f32[12,48]{1,0:T(8,128)S(1)} %get-tuple-element.40), channel_id=1, source_target_pairs={{0,504},{8,16},{16,8},{24,32},{32,24},{40,48},{48,40},{56,64},{64,... | collective-permute-start | bytes 6920 | tf_op jit(solution)/shard_map/ppermute | solution.py:255
  53.7 6.2 %collective-permute-start.3 = (f32[17,128]{1,0:T(8,128)S(1)}, f32[17,128]{1,0:T(8,128)S(1)}, u32[]{:S(2)}, u32[]{:S(2)}) collective-permute-start(f32[17,128]{1,0:T(8,128)S(1)} %get-tuple-element.35), channel_id=1, source_target_pairs={{0,1},{1,2},{2,3},{3,4},{4,5},{5,6},{6,7},{8,9},{9,10},{10,11},{11... | collective-permute-start | bytes 26120 | tf_op jit(solution)/shard_map/ppermute | solution.py:231
  58.6 8.3 %collective-permute-start.4 = (f32[17,128]{1,0:T(8,128)S(1)}, f32[17,128]{1,0:T(8,128)S(1)}, u32[]{:S(2)}, u32[]{:S(2)}) collective-permute-start(f32[17,128]{1,0:T(8,128)S(1)} %get-tuple-element.35), channel_id=1, source_target_pairs={{1,0},{2,1},{3,2},{4,3},{5,4},{6,5},{7,6},{9,8},{10,9},{11,10},{12... | collective-permute-start | bytes 26120 | tf_op jit(solution)/shard_map/ppermute | solution.py:231
  67.7 15.8 %all-to-all-start.1 = ((f32[32,1,2176]{2,1,0:T(1,128)}), f32[32,1,2176]{2,1,0:T(1,128)S(1)}, u32[]{:S(2)}, u32[]{:S(2)}) async-start(f32[32,1,2176]{2,1,0:T(1,128)} %bitcast.10), calls=%async_computation.1 | async-start | bytes 557056 | tf_op jit(solution)/shard_map/all_to_all | solution.py:235

commit v7 on v6

--- a/solution.py
+++ b/solution.py
@@ -100,24 +100,43 @@
     return total
 
 
-def tile_kernel(spot_ref, g_ref, near_ref, far_ref, bg_ref, lat_ref, obs_ref, adv_ref, own_ref, edge_ref, flat):
+def places(lat_ref):
+    q = lax.broadcasted_iota(jnp.int32, (1, Q), 1)
+    spot = jnp.where(q < MAIN, (q & 15) + 1, jnp.where(q < MAIN + LEV, 0, ROWS + 1))
+    level = jnp.where(q < MAIN, q >> 4, jnp.where(q < MAIN + LEV, q - MAIN, q - MAIN - LEV))
+    mask = lax.broadcasted_iota(jnp.int32, (LPAD, Q), 0) == level
+    low = lat_ref[:, 0:1] + 1.0
+    weight = lat_ref[:, 1:2]
+
+    def table(place):
+        place = place.astype(jnp.float32)
+        return jnp.where(place == low, 1.0 - weight, 0.0) + jnp.where(place == low + 1.0, weight, 0.0)
+
+    return spot, mask, table
+
+
+def to_coarse(coarse, lat, mask, flat, ref):
+    wide = jnp.dot(coarse, lat, precision=highest, preferred_element_type=jnp.float32).reshape(FRAME, LPAD, Q)
+    for c in range(FRAME):
+        flat[0:1, c * Q : (c + 1) * Q] = jnp.sum(jnp.where(mask, wide[c], 0.0), axis=0, keepdims=True)
+    for t in range(TILES):
+        ref[t : t + 1, :] = flat[0:1, 128 * t : 128 * (t + 1)]
+
+
+def own_kernel(coarse_ref, lat_ref, own_ref, flat):
+    flat[...] = jnp.zeros_like(flat)
+    spot, mask, table = places(lat_ref)
+    to_coarse(coarse_ref[...], table(spot), mask, flat, own_ref)
+
+
+def tile_kernel(spot_ref, g_ref, near_ref, far_ref, bg_ref, lat_ref, obs_ref, adv_ref, coarse_ref, edge_ref, flat):
     for t in range(TILES):
         part = g_ref[pl.ds(t, CHIPS, stride=TILES), :]
         flat[0:1, 128 * t : 128 * (t + 1)] = jnp.sum(part, axis=0, keepdims=True)
     first = spot_ref[0:1, :FINE_R] == 0.0
     near, far = near_ref[:, :FINE_R], far_ref[...]
     ground = [jnp.where(first, far, near)] + [bg_ref[j] for j in range(FINE_C)] + [jnp.where(first, near, far)]
-    q = lax.broadcasted_iota(jnp.int32, (1, Q), 1)
-    spot = jnp.where(q < MAIN, (q & 15) + 1, jnp.where(q < MAIN + LEV, 0, ROWS + 1))
-    level = jnp.where(q < MAIN, q >> 4, jnp.where(q < MAIN + LEV, q - MAIN, q - MAIN - LEV))
-    mask = lax.broadcasted_iota(jnp.int32, (LPAD, Q), 0) == level
-    low = lat_ref[:, 0:1] + 1.0
-    weight = lat_ref[:, 1:2]
-
-    def table(place):
-        place = place.astype(jnp.float32)
-        return jnp.where(place == low, 1.0 - weight, 0.0) + jnp.where(place == low + 1.0, weight, 0.0)
-
+    spot, mask, table = places(lat_ref)
     lat = table(spot)
     spread = [jnp.where(mask, flat[0:1, c * Q : (c + 1) * Q], 0.0) for c in range(FRAME)]
     lat_rows = lax.dot_general(jnp.concatenate(spread, axis=0), lat, (((1,), (1,)), ((), ())), precision=highest,
@@ -159,15 +178,8 @@
                 total[c] = w * adj if total[c] is None else total[c] + w * adj
     coarse = jnp.concatenate(total, axis=0)
 
-    def to_coarse(lat, ref):
-        wide = jnp.dot(coarse, lat, precision=highest, preferred_element_type=jnp.float32).reshape(FRAME, LPAD, Q)
-        for c in range(FRAME):
-            flat[0:1, c * Q : (c + 1) * Q] = jnp.sum(jnp.where(mask, wide[c], 0.0), axis=0, keepdims=True)
-        for t in range(TILES):
-            ref[t : t + 1, :] = flat[0:1, 128 * t : 128 * (t + 1)]
-
-    to_coarse(lat, own_ref)
-    to_coarse(table(jnp.where(spot < 2, spot + ROWS, spot - ROWS)), edge_ref)
+    coarse_ref[...] = coarse
+    to_coarse(coarse, table(jnp.where(spot < 2, spot + ROWS, spot - ROWS)), mask, flat, edge_ref)
 
 
 def share_kernel(own_ref, prev_ref, next_ref, out_ref):
@@ -182,7 +194,7 @@
         out_ref[TILES * m : TILES * (m + 1), :] = total
 
 
-def gradient_kernel(scale, g_ref, ens_ref, prev_ref, next_ref, out_ref, pad, xt_lo, xt_hi, flat):
+def gradient_kernel(scale, g_ref, ens_ref, prev_ref, next_ref, out_hbm, pad, xt_lo, xt_hi, flat, out_ref, sems):
     for core in range(2):
         for t in range(TILES):
             flat[core, :, 128 * t : 128 * (t + 1)] = g_ref[pl.ds(core * CHIPS * TILES + t, CHIPS, stride=TILES), :]
@@ -204,10 +216,17 @@
     pad[:, 8:24, :] = field
     pad[:, 7, :] = hi[MAIN - 128 : MAIN - 128 + LEV, :] * prev_ref[2]
     pad[:, 24, :] = hi[MAIN - 128 + LEV : Q - 128, :] * next_ref[2]
-    out_ref[...] = lon_smooth(0.25 * pad[:, 7:23, :] + 0.5 * field + 0.25 * pad[:, 9:25, :])
-
-
-def call(kernel, out, scratch, *args, hbm=False, sems=()):
+    copies = []
+    for k in range(3):
+        lev = slice(4 * k, 4 * (k + 1))
+        out_ref[lev] = lon_smooth(0.25 * pad[lev, 7:23, :] + 0.5 * pad[lev, 8:24, :] + 0.25 * pad[lev, 9:25, :])
+        copies.append(pltpu.make_async_copy(out_ref.at[lev], out_hbm.at[lev], sems.at[k]))
+        copies[k].start()
+    for copy in copies:
+        copy.wait()
+
+
+def call(kernel, out, scratch, *args, hbm=False, sems=(), away=False):
     def spec(x):
         return pl.BlockSpec(memory_space=pltpu.SMEM if x.dtype == jnp.int32 else pltpu.VMEM)
 
@@ -215,7 +234,7 @@
         kernel,
         out_shape=out,
         in_specs=[pl.BlockSpec(memory_space=pltpu.HBM) if hbm else spec(x) for x in args],
-        out_specs=jax.tree.map(spec, out),
+        out_specs=pl.BlockSpec(memory_space=pl.ANY) if away else jax.tree.map(spec, out),
         scratch_shapes=[pltpu.VMEM(shape, jnp.float32) for shape in scratch] + list(sems),
         compiler_params=pltpu.CompilerParams(vmem_limit_bytes=40 * 1024 * 1024),
     )(*args)
@@ -252,14 +271,12 @@
     sides = jnp.pad(sides, ((0, LPAD - LEV), (0, 128 - FINE_R)))
     far = jnp.where(first_core, grid[0], grid[FINE_C - 1])
     size = 2 * CHIPS
-    far = lax.ppermute(far, ("chip", "core"), [(i, (i + (1 if i % 2 else size - 1)) % size) for i in range(size)])
-    far = jnp.pad(far, ((0, LPAD - LEV), (0, 0)))
     ground = jnp.pad(grid, ((0, 0), (0, LPAD - LEV), (0, 0)))
     obs = jnp.concatenate(
         [jnp.pad(obs_value[:, 0, :], ((0, LPAD - LEV), (0, 0))), obs_precision, (obs_cell // FINE_C).astype(jnp.float32),
          (obs_cell % FINE_C).astype(jnp.float32), jnp.zeros((24 - LPAD - 3, NOBS), jnp.float32)], axis=0)
     lat = jnp.stack([lat_lower.astype(jnp.float32), lat_weight], axis=1)
-    before, after, ground, sides, obs, lat = lax.optimization_barrier((before, after, ground, sides, obs, lat))
+    before, after, ground, sides, far = lax.optimization_barrier((before, after, ground, sides, far))
 
     keep, send = call(
         functools.partial(product_kernel, scale),
@@ -269,21 +286,26 @@
     )
     both = lax.all_gather(send, "core", axis=0, tiled=True)
     paired, near = call(pair_kernel, (f32(PAIR, 128), f32(LPAD, 128)), [], spot, keep, both)
+    paired, far = lax.optimization_barrier((paired, far))
     gathered = exchange(paired, TILES)
-    moved, own, edge = call(
+    far = lax.ppermute(far, ("chip", "core"), [(i, (i + (1 if i % 2 else size - 1)) % size) for i in range(size)])
+    far = jnp.pad(far, ((0, LPAD - LEV), (0, 0)))
+    moved, coarse, edge = call(
         tile_kernel,
-        (f32(FINE_C, LPAD, FINE_R), f32(TILES, 128), f32(TILES, 128)),
+        (f32(FINE_C, LPAD, FINE_R), f32(FRAME * LPAD, FINE_R), f32(TILES, 128)),
         [(8, CHUNK)],
         spot, gathered, near, far, ground, lat, obs,
     )
     from_prev, from_next = both_ways(edge, edge, "band", BANDS, False)
+    own = call(own_kernel, f32(TILES, 128), [(8, CHUNK)], coarse, lat)
     shared = call(share_kernel, f32(CHIPS * TILES, 128), [], own, from_prev, from_next)
     everyone = lax.all_gather(exchange(shared, TILES), "core", axis=0, tiled=True)
     gradient = call(
         functools.partial(gradient_kernel, scale),
         f32(LEV, ROWS, COLS),
-        [(LEV, 32, COLS), (COLS, 128), (COLS, 128), (2, CHIPS, CHUNK)],
+        [(LEV, 32, COLS), (COLS, 128), (COLS, 128), (2, CHIPS, CHUNK), (LEV, ROWS, COLS)],
         everyone, ens, before, after,
+        sems=[pltpu.SemaphoreType.DMA((3,))], away=True,
     )
     advected = moved[:, :LEV].transpose(1, 2, 0).reshape(LEV, 1, FINE_R * FINE_C)
     return (advected, gradient[None])

time: 92 us -> 91.8 us (level)
  local copies, waits for them, and re-layouts: 4.18 us -> 2.9 us
    ppermute x2, waiting for transfers between devices: 14.8 us -> 17.1 us  [both_ways(): lax.ppermute(down_value, axis, down)]
    unnamed x13, local copies, waits for them, and re-layouts: 2.64 us -> 1.36 us
    ppermute x1, waiting for transfers between devices: 1.98 us -> 0.77 us  [shards(): lax.ppermute(far, ('chip', 'core'), [(i, (i + (1 if i % 2 else size - 1))...]
    pallas_call x6 -> x7, Pallas kernels: 7.12 us -> 7.34 us  [call(): pl.pallas_call(kernel, out_shape=out, in_specs=[pl.BlockSpec(memory_space...]
  transfers between devices with their start and end apart: 7 -> 7, of which waited for: 5 -> 5; matrix products, arithmetic and copies ran while one was open for 2% -> 2% of each run, Pallas kernels for 0% -> 1%
where the time goes in v7:
time: 91.8 us; the launch traced here: 91.3 us
  starting transfers between devices  37.7 us (41%)
  waiting for transfers between devices  34.3 us (37%)
  blocking collectives  8.04 us (9%)
  Pallas kernels  7.34 us (8%)
  local copies, waits for them, and re-layouts  2.9 us (3%)
    ppermute x2, waiting for transfers between devices, both_ways(): lax.ppermute(down_value, axis, down)  17.1 us
    all_to_all x2, waiting for transfers between devices, exchange(): lax.all_to_all(flat.reshape(CHIPS, 1, tiles * 128), 'chip', 0, 0, tiled=T...  16.4 us
    ppermute x2, starting transfers between devices, both_ways(): lax.ppermute(up_value, axis, up)  16.3 us
    all_to_all x2, starting transfers between devices, exchange(): lax.all_to_all(flat.reshape(CHIPS, 1, tiles * 128), 'chip', 0, 0, tiled=T...  14.9 us
    pallas_call x7, Pallas kernels, call(): pl.pallas_call(kernel, out_shape=out, in_specs=[pl.BlockSpec(memory_space...  7.34 us
    all_gather x1, blocking collectives, shards(): lax.all_gather(exchange(shared, TILES), 'core', axis=0, tiled=True)  5.59 us
    ppermute x1, starting transfers between devices, shards(): lax.ppermute(far, ('chip', 'core'), [(i, (i + (1 if i % 2 else size - 1))...  3.96 us
    ppermute x2, starting transfers between devices, both_ways(): lax.ppermute(down_value, axis, down)  2.58 us
  transfers between devices with their start and end apart: 7, of which 5 were waited for; matrix products, arithmetic and copies ran while one was open for 2% of the time, Pallas kernels for 1%

profile of v7, /device:TPU:1, one launch (start us, length us, event | category | flops | bytes accessed | tf_op | source)
XLA Modules:
  0.0 91.3 jit_solution(6761020518543970499)
XLA Ops:
  0.6 1.1 %shard_map.95 = (f32[3,12,512]{2,1,0:T(8,128)S(1)}, f32[3,12,512]{2,1,0:T(8,128)S(1)}, f32[12,16,512]{2,1,0:T(8,128)S(1)}, bf16[12,16,512]{2,1,0:T(8,128)(2,1)S(1)}) custom-call(f32[12,16,512]{2,1,0:T(8,128)} %bitcast.24, bf16[12,16,512]{2,1,0:T(8,128)(2,1)} %bitcast.26), custom_call_target="tpu_custom_call" | custom-call | tf_op jit(solution)/shard_map/pallas_call | solution.py:233
  1.8 11.5 %collective-permute-start = (f32[3,12,512]{2,1,0:T(8,128)S(1)}, f32[3,12,512]{2,1,0:T(8,128)S(1)}, u32[]{:S(2)}, u32[]{:S(2)}) collective-permute-start(f32[3,12,512]{2,1,0:T(8,128)S(1)} %get-tuple-element.22), channel_id=1, source_target_pairs={{0,1},{1,2},{2,3},{3,4},{4,5},{5,6},{6,7},{8,9},{9,10},{10,11},{11... | collective-permute-start | bytes 221192 | tf_op jit(solution)/shard_map/ppermute | solution.py:250
  13.3 1.3 %collective-permute-start.1 = (f32[3,12,512]{2,1,0:T(8,128)S(1)}, f32[3,12,512]{2,1,0:T(8,128)S(1)}, u32[]{:S(2)}, u32[]{:S(2)}) collective-permute-start(f32[3,12,512]{2,1,0:T(8,128)S(1)} %get-tuple-element.23), channel_id=1, source_target_pairs={{1,0},{2,1},{3,2},{4,3},{5,4},{6,5},{7,6},{9,8},{10,9},{11,10},{12... | collective-permute-start | bytes 221192 | tf_op jit(solution)/shard_map/ppermute | solution.py:250
  15.2 10.5 %collective-permute-done.1.next_ref = f32[3,12,512]{2,1,0:T(8,128)S(1)} collective-permute-done((f32[3,12,512]{2,1,0:T(8,128)S(1)}, f32[3,12,512]{2,1,0:T(8,128)S(1)}, u32[]{:S(2)}, u32[]{:S(2)}) %collective-permute-start.1) | collective-permute-done | bytes 73760 | tf_op jit(solution)/shard_map/ppermute | solution.py:250
  25.6 0.9 shard_map.96
  26.6 2.4 %all_gather.6.both_ref = f32[1120,128]{1,0:T(8,128)S(1)} all-gather(f32[560,128]{1,0:T(8,128)S(1)} %get-tuple-element.28), channel_id=1, replica_groups=mesh['chip'=32,'core'=2,'band'=8] {'core'}, dimensions={0}, use_global_device_ids=true | all-gather | bytes 860160 | tf_op jit(solution)/shard_map/all_gather | solution.py:287
  29.0 0.7 shard_map.97
  29.7 9.6 %all-to-all-start = ((f32[32,1,2176]{2,1,0:T(1,128)}), f32[32,1,2176]{2,1,0:T(1,128)S(1)}, u32[]{:S(2)}, u32[]{:S(2)}) async-start(f32[32,1,2176]{2,1,0:T(1,128)} %bitcast.5), calls=%async_computation | async-start | bytes 557056 | tf_op jit(solution)/shard_map/all_to_all | solution.py:254
  39.4 0.7 copy-done.2
  40.0 4.0 %collective-permute-start.2 = (f32[12,48]{1,0:T(8,128)S(1)}, f32[12,48]{1,0:T(8,128)S(1)}, u32[]{:S(2)}, u32[]{:S(2)}) collective-permute-start(f32[12,48]{1,0:T(8,128)S(1)} %get-tuple-element.33), channel_id=1, source_target_pairs={{0,504},{8,16},{16,8},{24,32},{32,24},{40,48},{48,40},{56,64},{64,... | collective-permute-start | bytes 6920 | tf_op jit(solution)/shard_map/ppermute | solution.py:291
  44.2 0.7 copy-done.3
  44.9 0.8 collective-permute-done.2
  45.6 6.3 %all-to-all-done = f32[32,1,2176]{2,1,0:T(1,128)S(1)} async-done(((f32[32,1,2176]{2,1,0:T(1,128)}), f32[32,1,2176]{2,1,0:T(1,128)S(1)}, u32[]{:S(2)}, u32[]{:S(2)}) %all-to-all-start) | async-done | bytes 278560 | tf_op jit(solution)/shard_map/all_to_all | solution.py:254
  51.9 1.8 %shard_map.98 = (f32[24,16,48]{2,1,0:T(8,128)S(1)}, f32[160,48]{1,0:T(8,128)S(1)}, f32[17,128]{1,0:T(8,128)S(1)}) custom-call(f32[1,512]{1,0:T(1,128)S(1)} %broadcast_in_dim.9.spot_ref, f32[544,128]{1,0:T(8,128)S(1)} %bitcast.20, f32[16,128]{1,0:T(8,128)S(1)} %get-tuple-element.32.near_ref, f32[16,48]{1,0:T(8,128)S(1)} %pad.18.far_ref, ...), custom_call_target="tpu_custom_call" | custom-call | tf_op jit(solution)/shard_map/pallas_call | solution.py:233
  53.7 4.8 %collective-permute-start.3 = (f32[17,128]{1,0:T(8,128)S(1)}, f32[17,128]{1,0:T(8,128)S(1)}, u32[]{:S(2)}, u32[]{:S(2)}) collective-permute-start(f32[17,128]{1,0:T(8,128)S(1)} %get-tuple-element.37), channel_id=1, source_target_pairs={{0,1},{1,2},{2,3},{3,4},{4,5},{5,6},{6,7},{8,9},{9,10},{10,11},{11... | collective-permute-start | bytes 26120 | tf_op jit(solution)/shard_map/ppermute | solution.py:250
  58.5 1.3 %collective-permute-start.4 = (f32[17,128]{1,0:T(8,128)S(1)}, f32[17,128]{1,0:T(8,128)S(1)}, u32[]{:S(2)}, u32[]{:S(2)}) collective-permute-start(f32[17,128]{1,0:T(8,128)S(1)} %get-tuple-element.37), channel_id=1, source_target_pairs={{1,0},{2,1},{3,2},{4,3},{5,4},{6,5},{7,6},{9,8},{10,9},{11,10},{12... | collective-permute-start | bytes 26120 | tf_op jit(solution)/shard_map/ppermute | solution.py:250
  59.8 0.5 shard_map.99.own_ref
  60.3 6.6 %collective-permute-done.4.next_ref = f32[17,128]{1,0:T(8,128)S(1)} collective-permute-done((f32[17,128]{1,0:T(8,128)S(1)}, f32[17,128]{1,0:T(8,128)S(1)}, u32[]{:S(2)}, u32[]{:S(2)}) %collective-permute-start.4) | collective-permute-done | bytes 8736 | tf_op jit(solution)/shard_map/ppermute | solution.py:250
  66.9 0.8 shard_map.100
  67.6 5.3 %all-to-all-start.1 = ((f32[32,1,2176]{2,1,0:T(1,128)}), f32[32,1,2176]{2,1,0:T(1,128)S(1)}, u32[]{:S(2)}, u32[]{:S(2)}) async-start(f32[32,1,2176]{2,1,0:T(1,128)} %bitcast.10), calls=%async_computation.1 | async-start | bytes 557056 | tf_op jit(solution)/shard_map/all_to_all | solution.py:254
  73.1 0.9 reshape.32
  74.0 10.2 %all-to-all-done.1 = f32[32,1,2176]{2,1,0:T(1,128)S(1)} async-done(((f32[32,1,2176]{2,1,0:T(1,128)}), f32[32,1,2176]{2,1,0:T(1,128)S(1)}, u32[]{:S(2)}, u32[]{:S(2)}) %all-to-all-start.1) | async-done | bytes 278560 | tf_op jit(solution)/shard_map/all_to_all | solution.py:254
  84.1 5.6 %all_gather.7.g_ref = f32[1088,128]{1,0:T(8,128)S(1)} all-gather(f32[544,128]{1,0:T(8,128)S(1)} %bitcast.21), channel_id=1, replica_groups=mesh['chip'=32,'core'=2,'band'=8] {'core'}, dimensions={0}, use_global_device_ids=true | all-gather | bytes 835584 | tf_op jit(solution)/shard_map/all_gather | solution.py:302
  89.7 1.6 %shard_map.101 = f32[12,16,512]{2,1,0:T(8,128)} custom-call(f32[1088,128]{1,0:T(8,128)S(1)} %all_gather.7.g_ref, bf16[12,16,512]{2,1,0:T(8,128)(2,1)S(1)} %get-tuple-element.21.ens_ref, f32[3,12,512]{2,1,0:T(8,128)S(1)} %collective-permute-done.prev_ref, f32[3,12,512]{2,1,0:T(8,128)S(1)} %collective-permute-done.1.next_ref), custom_call_target="tpu_custom_call" | custom-call | tf_op jit(solution)/shard_map/pallas_call | solution.py:233
  (30 shorter events, 0.9 us)
Async XLA Ops:
  0.6 13.9 %copy-start = (f32[12,1,1152]{2,1,0:T(1,128)S(1)}, f32[12,1,1152]{2,1,0:T(1,128)}, u32[]{:S(2)}) copy-start(f32[12,1,1152]{2,1,0:T(1,128)} %param.12) | copy-start | bytes 165892
  1.8 13.4 %collective-permute-start = (f32[3,12,512]{2,1,0:T(8,128)S(1)}, f32[3,12,512]{2,1,0:T(8,128)S(1)}, u32[]{:S(2)}, u32[]{:S(2)}) collective-permute-start(f32[3,12,512]{2,1,0:T(8,128)S(1)} %get-tuple-element.22), channel_id=1, source_target_pairs={{0,1},{1,2},{2,3},{3,4},{4,5},{5,6},{6,7},{8,9},{9,10},{10,11},{11... | collective-permute-start | bytes 221192 | tf_op jit(solution)/shard_map/ppermute | solution.py:250
  13.3 12.4 %collective-permute-start.1 = (f32[3,12,512]{2,1,0:T(8,128)S(1)}, f32[3,12,512]{2,1,0:T(8,128)S(1)}, u32[]{:S(2)}, u32[]{:S(2)}) collective-permute-start(f32[3,12,512]{2,1,0:T(8,128)S(1)} %get-tuple-element.23), channel_id=1, source_target_pairs={{1,0},{2,1},{3,2},{4,3},{5,4},{6,5},{7,6},{9,8},{10,9},{11,10},{12... | collective-permute-start | bytes 221192 | tf_op jit(solution)/shard_map/ppermute | solution.py:250
  29.7 9.6 %copy-start.5 = (s32[48]{0:T(128)S(1)}, s32[48]{0:T(128)}, u32[]{:S(2)}) copy-start(s32[48]{0:T(128)} %param.10) | copy-start | bytes 580
  29.7 14.3 %copy-start.1 = (f32[12,1,256]{2,1,0:T(1,128)S(1)}, f32[12,1,256]{2,1,0:T(1,128)}, u32[]{:S(2)}) copy-start(f32[12,1,256]{2,1,0:T(1,128)} %param.14) | copy-start | bytes 36868
  29.7 22.2 %all-to-all-start = ((f32[32,1,2176]{2,1,0:T(1,128)}), f32[32,1,2176]{2,1,0:T(1,128)S(1)}, u32[]{:S(2)}, u32[]{:S(2)}) async-start(f32[32,1,2176]{2,1,0:T(1,128)} %bitcast.5), calls=%async_computation | async-start | bytes 557056 | tf_op jit(solution)/shard_map/all_to_all | solution.py:254
  39.3 0.7 copy-start.2
  40.0 4.0 %copy-start.4 = (f32[48]{0:T(128)S(1)}, f32[48]{0:T(128)}, u32[]{:S(2)}) copy-start(f32[48]{0:T(128)} %param.11) | copy-start | bytes 580
  40.0 5.6 %collective-permute-start.2 = (f32[12,48]{1,0:T(8,128)S(1)}, f32[12,48]{1,0:T(8,128)S(1)}, u32[]{:S(2)}, u32[]{:S(2)}) collective-permute-start(f32[12,48]{1,0:T(8,128)S(1)} %get-tuple-element.33), channel_id=1, source_target_pairs={{0,504},{8,16},{16,8},{24,32},{32,24},{40,48},{48,40},{56,64},{64,... | collective-permute-start | bytes 6920 | tf_op jit(solution)/shard_map/ppermute | solution.py:291
  44.2 0.7 copy-start.3
  53.7 6.6 %collective-permute-start.3 = (f32[17,128]{1,0:T(8,128)S(1)}, f32[17,128]{1,0:T(8,128)S(1)}, u32[]{:S(2)}, u32[]{:S(2)}) collective-permute-start(f32[17,128]{1,0:T(8,128)S(1)} %get-tuple-element.37), channel_id=1, source_target_pairs={{0,1},{1,2},{2,3},{3,4},{4,5},{5,6},{6,7},{8,9},{9,10},{10,11},{11... | collective-permute-start | bytes 26120 | tf_op jit(solution)/shard_map/ppermute | solution.py:250
  58.5 8.3 %collective-permute-start.4 = (f32[17,128]{1,0:T(8,128)S(1)}, f32[17,128]{1,0:T(8,128)S(1)}, u32[]{:S(2)}, u32[]{:S(2)}) collective-permute-start(f32[17,128]{1,0:T(8,128)S(1)} %get-tuple-element.37), channel_id=1, source_target_pairs={{1,0},{2,1},{3,2},{4,3},{5,4},{6,5},{7,6},{9,8},{10,9},{11,10},{12... | collective-permute-start | bytes 26120 | tf_op jit(solution)/shard_map/ppermute | solution.py:250
  67.6 16.5 %all-to-all-start.1 = ((f32[32,1,2176]{2,1,0:T(1,128)}), f32[32,1,2176]{2,1,0:T(1,128)S(1)}, u32[]{:S(2)}, u32[]{:S(2)}) async-start(f32[32,1,2176]{2,1,0:T(1,128)} %bitcast.10), calls=%async_computation.1 | async-start | bytes 557056 | tf_op jit(solution)/shard_map/all_to_all | solution.py:254

commit v8 on v7

--- a/solution.py
+++ b/solution.py
@@ -182,14 +182,17 @@
     to_coarse(coarse, table(jnp.where(spot < 2, spot + ROWS, spot - ROWS)), mask, flat, edge_ref)
 
 
-def share_kernel(own_ref, prev_ref, next_ref, out_ref):
+def share_kernel(spot_ref, own_ref, one_ref, two_ref, out_ref):
+    even = spot_ref[1:2, :128] == 0.0
+    before = jnp.where(even, two_ref[...], one_ref[...])
+    after = jnp.where(even, one_ref[...], two_ref[...])
     shape = (TILES, 128)
     q = lax.rem(lax.broadcasted_iota(jnp.int32, shape, 0) * 128 + lax.broadcasted_iota(jnp.int32, shape, 1), Q)
     row = q & 15
     inner = q < MAIN
     from_prev = (inner & (row == 0)) | ((q >= MAIN) & (q < MAIN + LEV))
     from_next = (inner & (row == ROWS - 1)) | (q >= MAIN + LEV)
-    total = own_ref[...] + jnp.where(from_prev, prev_ref[...], 0.0) + jnp.where(from_next, next_ref[...], 0.0)
+    total = own_ref[...] + jnp.where(from_prev, before, 0.0) + jnp.where(from_next, after, 0.0)
     for m in range(CHIPS):
         out_ref[TILES * m : TILES * (m + 1), :] = total
 
@@ -257,7 +260,8 @@
 
 def shards(ensemble, alpha, lat_lower, lat_weight, background, obs_cell, obs_value, obs_precision):
     scale = 1.0 / math.sqrt(2 * CHIPS - 1)
-    spot = jnp.broadcast_to(lax.axis_index("core").astype(jnp.float32), (1, COLS))
+    spot = jnp.stack([lax.axis_index("core"), lax.axis_index("band") % 2]).astype(jnp.float32)
+    spot = jnp.broadcast_to(spot[:, None], (2, COLS))
     last, first, alf, ens = call(
         halo_kernel,
         (f32(3, LEV, COLS), f32(3, LEV, COLS), f32(LEV, ROWS, COLS), jax.ShapeDtypeStruct((LEV, ROWS, COLS), jnp.bfloat16)),
@@ -296,9 +300,10 @@
         [(8, CHUNK)],
         spot, gathered, near, far, ground, lat, obs,
     )
-    from_prev, from_next = both_ways(edge, edge, "band", BANDS, False)
+    one = lax.ppermute(edge, "band", [(b, b ^ 1) for b in range(BANDS)])
+    two = lax.ppermute(edge, "band", [(b, ((b + 1) ^ 1) - 1) for b in range(1, BANDS - 1)])
     own = call(own_kernel, f32(TILES, 128), [(8, CHUNK)], coarse, lat)
-    shared = call(share_kernel, f32(CHIPS * TILES, 128), [], own, from_prev, from_next)
+    shared = call(share_kernel, f32(CHIPS * TILES, 128), [], spot, own, one, two)
     everyone = lax.all_gather(exchange(shared, TILES), "core", axis=0, tiled=True)
     gradient = call(
         functools.partial(gradient_kernel, scale),

time: 91.8 us -> 91.9 us (level)
  the two profiles are of different devices: /device:TPU:1 before, /device:TPU:3 now
where the time goes in v8:
time: 91.9 us; the launch traced here: 91.5 us
  starting transfers between devices  40.5 us (44%)
  waiting for transfers between devices  31.5 us (34%)
  blocking collectives  8.03 us (9%)
  Pallas kernels  7.34 us (8%)
  local copies, waits for them, and re-layouts  2.96 us (3%)
    all_to_all x2, waiting for transfers between devices, exchange(): lax.all_to_all(flat.reshape(CHIPS, 1, tiles * 128), 'chip', 0, 0, tiled=T...  16.4 us
    all_to_all x2, starting transfers between devices, exchange(): lax.all_to_all(flat.reshape(CHIPS, 1, tiles * 128), 'chip', 0, 0, tiled=T...  14.8 us
    ppermute x1, starting transfers between devices, both_ways(): lax.ppermute(up_value, axis, up)  10.6 us
    ppermute x1, waiting for transfers between devices, both_ways(): lax.ppermute(down_value, axis, down)  9.84 us
    pallas_call x7, Pallas kernels, call(): pl.pallas_call(kernel, out_shape=out, in_specs=[pl.BlockSpec(memory_space...  7.34 us
    all_gather x1, blocking collectives, shards(): lax.all_gather(exchange(shared, TILES), 'core', axis=0, tiled=True)  5.59 us
    ppermute x1, starting transfers between devices, shards(): one = lax.ppermute(edge, 'band', [(b, b ^ 1) for b in range(BANDS)])  4.85 us
    ppermute x1, waiting for transfers between devices, shards(): lax.ppermute(edge, 'band', [(b, (b + 1 ^ 1) - 1) for b in range(1, BANDS...  4.46 us
  transfers between devices with their start and end apart: 7, of which 5 were waited for; matrix products, arithmetic and copies ran while one was open for 2% of the time, Pallas kernels for 1%

profile of v8, /device:TPU:3, one launch (start us, length us, event | category | flops | bytes accessed | tf_op | source)
XLA Modules:
  0.0 91.5 jit_solution(3306348402603134239)
XLA Ops:
  0.6 1.1 %shard_map.95 = (f32[3,12,512]{2,1,0:T(8,128)S(1)}, f32[3,12,512]{2,1,0:T(8,128)S(1)}, f32[12,16,512]{2,1,0:T(8,128)S(1)}, bf16[12,16,512]{2,1,0:T(8,128)(2,1)S(1)}) custom-call(f32[12,16,512]{2,1,0:T(8,128)} %bitcast.26, bf16[12,16,512]{2,1,0:T(8,128)(2,1)} %bitcast.28), custom_call_target="tpu_custom_call" | custom-call | tf_op jit(solution)/shard_map/pallas_call | solution.py:236
  1.8 10.6 %collective-permute-start = (f32[3,12,512]{2,1,0:T(8,128)S(1)}, f32[3,12,512]{2,1,0:T(8,128)S(1)}, u32[]{:S(2)}, u32[]{:S(2)}) collective-permute-start(f32[3,12,512]{2,1,0:T(8,128)S(1)} %get-tuple-element.22), channel_id=1, source_target_pairs={{0,1},{1,2},{2,3},{3,4},{4,5},{5,6},{6,7},{8,9},{9,10},{10,11},{11... | collective-permute-start | bytes 221192 | tf_op jit(solution)/shard_map/ppermute | solution.py:253
  12.4 1.9 %collective-permute-start.1 = (f32[3,12,512]{2,1,0:T(8,128)S(1)}, f32[3,12,512]{2,1,0:T(8,128)S(1)}, u32[]{:S(2)}, u32[]{:S(2)}) collective-permute-start(f32[3,12,512]{2,1,0:T(8,128)S(1)} %get-tuple-element.23), channel_id=1, source_target_pairs={{1,0},{2,1},{3,2},{4,3},{5,4},{6,5},{7,6},{9,8},{10,9},{11,10},{12... | collective-permute-start | bytes 221192 | tf_op jit(solution)/shard_map/ppermute | solution.py:253
  15.0 9.8 %collective-permute-done.1.next_ref = f32[3,12,512]{2,1,0:T(8,128)S(1)} collective-permute-done((f32[3,12,512]{2,1,0:T(8,128)S(1)}, f32[3,12,512]{2,1,0:T(8,128)S(1)}, u32[]{:S(2)}, u32[]{:S(2)}) %collective-permute-start.1) | collective-permute-done | bytes 73760 | tf_op jit(solution)/shard_map/ppermute | solution.py:253
  25.0 0.9 shard_map.96
  25.9 2.4 %all_gather.6.both_ref = f32[1120,128]{1,0:T(8,128)S(1)} all-gather(f32[560,128]{1,0:T(8,128)S(1)} %get-tuple-element.28), channel_id=1, replica_groups=mesh['chip'=32,'core'=2,'band'=8] {'core'}, dimensions={0}, use_global_device_ids=true | all-gather | bytes 860160 | tf_op jit(solution)/shard_map/all_gather | solution.py:291
  28.3 0.7 shard_map.97
  29.1 9.5 %all-to-all-start = ((f32[32,1,2176]{2,1,0:T(1,128)}), f32[32,1,2176]{2,1,0:T(1,128)S(1)}, u32[]{:S(2)}, u32[]{:S(2)}) async-start(f32[32,1,2176]{2,1,0:T(1,128)} %bitcast.7), calls=%async_computation | async-start | bytes 557056 | tf_op jit(solution)/shard_map/all_to_all | solution.py:257
  38.6 0.7 copy-done.2
  39.3 4.0 %collective-permute-start.2 = (f32[12,48]{1,0:T(8,128)S(1)}, f32[12,48]{1,0:T(8,128)S(1)}, u32[]{:S(2)}, u32[]{:S(2)}) collective-permute-start(f32[12,48]{1,0:T(8,128)S(1)} %get-tuple-element.33), channel_id=1, source_target_pairs={{0,504},{8,16},{16,8},{24,32},{32,24},{40,48},{48,40},{56,64},{64,... | collective-permute-start | bytes 6920 | tf_op jit(solution)/shard_map/ppermute | solution.py:295
  43.4 0.7 copy-done.3
  44.1 0.8 collective-permute-done.2
  44.9 6.3 %all-to-all-done = f32[32,1,2176]{2,1,0:T(1,128)S(1)} async-done(((f32[32,1,2176]{2,1,0:T(1,128)}), f32[32,1,2176]{2,1,0:T(1,128)S(1)}, u32[]{:S(2)}, u32[]{:S(2)}) %all-to-all-start) | async-done | bytes 278560 | tf_op jit(solution)/shard_map/all_to_all | solution.py:257
  51.2 1.8 %shard_map.98 = (f32[24,16,48]{2,1,0:T(8,128)S(1)}, f32[160,48]{1,0:T(8,128)S(1)}, f32[17,128]{1,0:T(8,128)S(1)}) custom-call(f32[2,512]{1,0:T(2,128)S(1)} %broadcast_in_dim.12.spot_ref, f32[544,128]{1,0:T(8,128)S(1)} %bitcast.22, f32[16,128]{1,0:T(8,128)S(1)} %get-tuple-element.32.near_ref, f32[16,48]{1,0:T(8,128)S(1)} %pad.18.far_ref, ...), custom_call_target="tpu_custom_call" | custom-call | tf_op jit(solution)/shard_map/pallas_call | solution.py:236
  52.9 4.8 %collective-permute-start.3 = (f32[17,128]{1,0:T(8,128)S(1)}, f32[17,128]{1,0:T(8,128)S(1)}, u32[]{:S(2)}, u32[]{:S(2)}) collective-permute-start(f32[17,128]{1,0:T(8,128)S(1)} %get-tuple-element.37), channel_id=1, source_target_pairs={{0,1},{1,0},{2,3},{3,2},{4,5},{5,4},{6,7},{7,6},{8,9},{9,8},{10,11... | collective-permute-start | bytes 26120 | tf_op jit(solution)/shard_map/ppermute | solution.py:303
  57.8 4.3 %collective-permute-start.4 = (f32[17,128]{1,0:T(8,128)S(1)}, f32[17,128]{1,0:T(8,128)S(1)}, u32[]{:S(2)}, u32[]{:S(2)}) collective-permute-start(f32[17,128]{1,0:T(8,128)S(1)} %get-tuple-element.37), channel_id=1, source_target_pairs={{1,2},{2,1},{3,4},{4,3},{5,6},{6,5},{9,10},{10,9},{11,12},{12,11},... | collective-permute-start | bytes 26120 | tf_op jit(solution)/shard_map/ppermute | solution.py:304
  62.1 0.5 shard_map.99.own_ref
  62.6 4.5 %collective-permute-done.4.two_ref = f32[17,128]{1,0:T(8,128)S(1)} collective-permute-done((f32[17,128]{1,0:T(8,128)S(1)}, f32[17,128]{1,0:T(8,128)S(1)}, u32[]{:S(2)}, u32[]{:S(2)}) %collective-permute-start.4) | collective-permute-done | bytes 8736 | tf_op jit(solution)/shard_map/ppermute | solution.py:304
  67.0 0.8 shard_map.100
  67.8 5.3 %all-to-all-start.1 = ((f32[32,1,2176]{2,1,0:T(1,128)}), f32[32,1,2176]{2,1,0:T(1,128)S(1)}, u32[]{:S(2)}, u32[]{:S(2)}) async-start(f32[32,1,2176]{2,1,0:T(1,128)} %bitcast.12), calls=%async_computation.1 | async-start | bytes 557056 | tf_op jit(solution)/shard_map/all_to_all | solution.py:257
  73.3 0.9 reshape.49
  74.1 10.2 %all-to-all-done.1 = f32[32,1,2176]{2,1,0:T(1,128)S(1)} async-done(((f32[32,1,2176]{2,1,0:T(1,128)}), f32[32,1,2176]{2,1,0:T(1,128)S(1)}, u32[]{:S(2)}, u32[]{:S(2)}) %all-to-all-start.1) | async-done | bytes 278560 | tf_op jit(solution)/shard_map/all_to_all | solution.py:257
  84.3 5.6 %all_gather.7.g_ref = f32[1088,128]{1,0:T(8,128)S(1)} all-gather(f32[544,128]{1,0:T(8,128)S(1)} %bitcast.23), channel_id=1, replica_groups=mesh['chip'=32,'core'=2,'band'=8] {'core'}, dimensions={0}, use_global_device_ids=true | all-gather | bytes 835584 | tf_op jit(solution)/shard_map/all_gather | solution.py:307
  89.9 1.6 %shard_map.101 = f32[12,16,512]{2,1,0:T(8,128)} custom-call(f32[1088,128]{1,0:T(8,128)S(1)} %all_gather.7.g_ref, bf16[12,16,512]{2,1,0:T(8,128)(2,1)S(1)} %get-tuple-element.21.ens_ref, f32[3,12,512]{2,1,0:T(8,128)S(1)} %collective-permute-done.prev_ref, f32[3,12,512]{2,1,0:T(8,128)S(1)} %collective-permute-done.1.next_ref), custom_call_target="tpu_custom_call" | custom-call | tf_op jit(solution)/shard_map/pallas_call | solution.py:236
  (31 shorter events, 1.0 us)
Async XLA Ops:
  0.6 13.7 %copy-start = (f32[12,1,1152]{2,1,0:T(1,128)S(1)}, f32[12,1,1152]{2,1,0:T(1,128)}, u32[]{:S(2)}) copy-start(f32[12,1,1152]{2,1,0:T(1,128)} %param.12) | copy-start | bytes 165892
  1.8 13.3 %collective-permute-start = (f32[3,12,512]{2,1,0:T(8,128)S(1)}, f32[3,12,512]{2,1,0:T(8,128)S(1)}, u32[]{:S(2)}, u32[]{:S(2)}) collective-permute-start(f32[3,12,512]{2,1,0:T(8,128)S(1)} %get-tuple-element.22), channel_id=1, source_target_pairs={{0,1},{1,2},{2,3},{3,4},{4,5},{5,6},{6,7},{8,9},{9,10},{10,11},{11... | collective-permute-start | bytes 221192 | tf_op jit(solution)/shard_map/ppermute | solution.py:253
  12.4 12.5 %collective-permute-start.1 = (f32[3,12,512]{2,1,0:T(8,128)S(1)}, f32[3,12,512]{2,1,0:T(8,128)S(1)}, u32[]{:S(2)}, u32[]{:S(2)}) collective-permute-start(f32[3,12,512]{2,1,0:T(8,128)S(1)} %get-tuple-element.23), channel_id=1, source_target_pairs={{1,0},{2,1},{3,2},{4,3},{5,4},{6,5},{7,6},{9,8},{10,9},{11,10},{12... | collective-permute-start | bytes 221192 | tf_op jit(solution)/shard_map/ppermute | solution.py:253
  29.1 9.5 %copy-start.5 = (s32[48]{0:T(128)S(1)}, s32[48]{0:T(128)}, u32[]{:S(2)}) copy-start(s32[48]{0:T(128)} %param.10) | copy-start | bytes 580
  29.1 14.2 %copy-start.1 = (f32[12,1,256]{2,1,0:T(1,128)S(1)}, f32[12,1,256]{2,1,0:T(1,128)}, u32[]{:S(2)}) copy-start(f32[12,1,256]{2,1,0:T(1,128)} %param.14) | copy-start | bytes 36868
  29.1 22.1 %all-to-all-start = ((f32[32,1,2176]{2,1,0:T(1,128)}), f32[32,1,2176]{2,1,0:T(1,128)S(1)}, u32[]{:S(2)}, u32[]{:S(2)}) async-start(f32[32,1,2176]{2,1,0:T(1,128)} %bitcast.7), calls=%async_computation | async-start | bytes 557056 | tf_op jit(solution)/shard_map/all_to_all | solution.py:257
  38.6 0.7 copy-start.2
  39.3 4.0 %copy-start.4 = (f32[48]{0:T(128)S(1)}, f32[48]{0:T(128)}, u32[]{:S(2)}) copy-start(f32[48]{0:T(128)} %param.11) | copy-start | bytes 580
  39.3 5.6 %collective-permute-start.2 = (f32[12,48]{1,0:T(8,128)S(1)}, f32[12,48]{1,0:T(8,128)S(1)}, u32[]{:S(2)}, u32[]{:S(2)}) collective-permute-start(f32[12,48]{1,0:T(8,128)S(1)} %get-tuple-element.33), channel_id=1, source_target_pairs={{0,504},{8,16},{16,8},{24,32},{32,24},{40,48},{48,40},{56,64},{64,... | collective-permute-start | bytes 6920 | tf_op jit(solution)/shard_map/ppermute | solution.py:295
  43.4 0.7 copy-start.3
  52.9 9.6 %collective-permute-start.3 = (f32[17,128]{1,0:T(8,128)S(1)}, f32[17,128]{1,0:T(8,128)S(1)}, u32[]{:S(2)}, u32[]{:S(2)}) collective-permute-start(f32[17,128]{1,0:T(8,128)S(1)} %get-tuple-element.37), channel_id=1, source_target_pairs={{0,1},{1,0},{2,3},{3,2},{4,5},{5,4},{6,7},{7,6},{8,9},{9,8},{10,11... | collective-permute-start | bytes 26120 | tf_op jit(solution)/shard_map/ppermute | solution.py:303
  57.8 9.2 %collective-permute-start.4 = (f32[17,128]{1,0:T(8,128)S(1)}, f32[17,128]{1,0:T(8,128)S(1)}, u32[]{:S(2)}, u32[]{:S(2)}) collective-permute-start(f32[17,128]{1,0:T(8,128)S(1)} %get-tuple-element.37), channel_id=1, source_target_pairs={{1,2},{2,1},{3,4},{4,3},{5,6},{6,5},{9,10},{10,9},{11,12},{12,11},... | collective-permute-start | bytes 26120 | tf_op jit(solution)/shard_map/ppermute | solution.py:304
  67.8 16.5 %all-to-all-start.1 = ((f32[32,1,2176]{2,1,0:T(1,128)}), f32[32,1,2176]{2,1,0:T(1,128)S(1)}, u32[]{:S(2)}, u32[]{:S(2)}) async-start(f32[32,1,2176]{2,1,0:T(1,128)} %bitcast.12), calls=%async_computation.1 | async-start | bytes 557056 | tf_op jit(solution)/shard_map/all_to_all | solution.py:257
